TPU v7x, 256 devices: a whole 4x4x8 slice. The times are simulated.
256 devices in a mesh: echo: 8 (over x, y_lo), coil: 16 (over z, core), read: 2 (over y_hi).
Axes of the slice: x: 4, y: 4 (y_hi: 2, y_lo: 2; y = y_hi * 2 + y_lo), z: 8, core: 2. Of those that a mesh axis runs over, the one named last changes fastest.
Arguments:
- kspace: bfloat16 [384, 8, 16, 4, 2, 192], P(None, 'echo', 'coil', 'read'), may hold values from -3 to 3
- sampling: int32 [384, 8, 192], P(None, 'echo'), may hold values 0 or 1
- coil_maps: bfloat16 [384, 16, 4, 2, 192], P(None, 'coil', 'read'), may hold values from -1.5 to 1.5
- image: float32 [384, 8, 4, 2, 192], P('coil', 'echo', 'read'), may hold values from -6 to 6
- filters: bfloat16 [48, 3, 3, 3, 2], replicated, may hold values from -0.875 to 0.875
- thresholds: float32 [48], replicated, may hold values from 0.5 to 8
- dc_weight: float32 [8], P('echo'), may hold values from 0.5 to 2
Outputs:
- updated: float32 [384, 8, 4, 2, 192], P('coil', 'echo', 'read')
All inputs are finite; a program needn't handle non-finite values. No bound on the sum of `sampling` on one device may be relied on, other than what follows from the above.
Results may differ from a plain program's by a relative error of at most 0.0033.
Values may be sent and summed in bfloat16 or wider, within the bound.
No kernel may reach another device: no remote copies, remote signals or barrier semaphores. Data moves between devices by JAX's collectives and lax.ppermute only.
A program may use at most 128 MiB of HBM per device.

v0:
```python
import jax
import jax.numpy as jnp
from jax import lax
from jax.sharding import PartitionSpec as P

NY = 384
NZ = 192


def in_order(parts, dim):
    shape = list(parts.shape[1:])
    shape[dim] *= parts.shape[0]
    return jnp.moveaxis(parts, 0, dim).reshape(shape)


def from_everyone(array, axis):
    copies = jnp.broadcast_to(array, (lax.axis_size(axis), *array.shape))
    return lax.all_to_all(copies, axis, split_axis=0, concat_axis=0, tiled=True)


def gathered_copies(array, axis, dim):
    return in_order(from_everyone(array, axis), dim)


def cut_along(array, dim, length):
    shape = array.shape
    parts = array.reshape(*shape[:dim], length, shape[dim] // length, *shape[dim + 1 :])
    return jnp.moveaxis(parts, dim, 0)


def summed_on_arrival(array, axis, dim):
    length = lax.axis_size(axis)
    parts = lax.all_to_all(cut_along(array, dim, length), axis, 0, 0, tiled=True)
    return jnp.sum(parts.astype(jnp.float32), axis=0)


def extended(block, sides, width):
    for axis, dim in sides:
        count = lax.axis_size(axis)
        forward = [(i, i + 1) for i in range(count - 1)]
        backward = [(target, source) for source, target in forward]
        low = lax.ppermute(
            lax.slice_in_dim(block, block.shape[dim] - width, None, axis=dim), axis, forward
        )
        high = lax.ppermute(lax.slice_in_dim(block, 0, width, axis=dim), axis, backward)
        block = jnp.concatenate([low, block, high], axis=dim)
    return block


def tables(length):
    positions = jnp.arange(length, dtype=jnp.int32)
    product = positions[:, None] * positions[None, :] % length
    phases = product.astype(jnp.float32) * (2.0 * jnp.pi / length)
    normalize = length ** (-0.5)
    return (jnp.cos(phases) * normalize, jnp.sin(phases) * normalize)


def complex_times(left, right, conjugate):
    left_real = left[..., 0, :]
    left_imag = left[..., 1, :]
    right_real = right[..., 0, :]
    right_imag = right[..., 1, :]
    if conjugate:
        return jnp.stack(
            [
                left_real * right_real + left_imag * right_imag,
                left_real * right_imag - left_imag * right_real,
            ],
            -2,
        )
    return jnp.stack(
        [
            left_real * right_real - left_imag * right_imag,
            left_real * right_imag + left_imag * right_real,
        ],
        -2,
    )


def column_section(values, block):
    shape = values.shape
    merged = values.reshape(shape[:-2] + (shape[-2] * shape[-1],))
    result = jnp.dot(merged, block, preferred_element_type=jnp.float32)
    return result.reshape(shape)


def row_section(values, row_table, adjoint):
    lines = values.shape[0]
    result = jnp.einsum("ay,y...->a...", row_table, values, preferred_element_type=jnp.float32)
    cosine_part = result[:lines]
    sine_part = result[lines:]
    if adjoint:
        return jnp.stack(
            [
                cosine_part[..., 0, :] - sine_part[..., 1, :],
                cosine_part[..., 1, :] + sine_part[..., 0, :],
            ],
            -2,
        )
    return jnp.stack(
        [
            cosine_part[..., 0, :] + sine_part[..., 1, :],
            cosine_part[..., 1, :] - sine_part[..., 0, :],
        ],
        -2,
    )


def coil_side(halfway, kspace, sampling, row_table):
    sampled = sampling.astype(jnp.float32)[:, :, None, None, None, :]
    spectrum = row_section(halfway, row_table, False)
    residual = (sampled * (spectrum - kspace.astype(jnp.float32))).astype(jnp.bfloat16)
    return row_section(residual, row_table, True).astype(jnp.bfloat16)


def respond(padded, weights, row_count, slices):
    columns = padded.shape[-1]
    z_padded = jnp.pad(padded, ((0, 0), (0, 0), (0, 0), (0, 0), (1, 1)))
    patches = jnp.stack(
        [
            z_padded[
                shift_y : shift_y + row_count,
                :,
                shift_r : shift_r + slices,
                :,
                shift_z : shift_z + columns,
            ]
            for shift_y in range(3)
            for shift_r in range(3)
            for shift_z in range(3)
        ],
        0,
    )
    return jnp.einsum("koc,oyercz->kyerz", weights, patches, preferred_element_type=jnp.float32)


def shrink(response, energy, thresholds):
    magnitude = jnp.sqrt(energy)
    factor = magnitude / (magnitude + thresholds[:, None, None, None])
    return (response * factor[:, :, None]).astype(jnp.bfloat16)


def transposed(shrunk_pad, weights, row_count, slices):
    columns = shrunk_pad.shape[-1]
    z_padded = jnp.pad(shrunk_pad, ((0, 0), (0, 0), (0, 0), (0, 0), (1, 1)))
    summed = jnp.zeros((row_count, z_padded.shape[2], slices, 2, columns), jnp.float32)
    for shift_y in range(3):
        for shift_r in range(3):
            for shift_z in range(3):
                offset = shift_y * 9 + shift_r * 3 + shift_z
                window = z_padded[
                    :,
                    2 - shift_y : 2 - shift_y + row_count,
                    :,
                    2 - shift_r : 2 - shift_r + slices,
                    2 - shift_z : 2 - shift_z + columns,
                ]
                summed = summed + jnp.einsum(
                    "kc,kyerz->yercz",
                    weights[:, offset],
                    window,
                    preferred_element_type=jnp.float32,
                )
    return summed


def body(kspace, sampling, coil_maps, image, filters, thresholds, dc_weight):
    row_cos, row_sin = tables(NY)
    row_table = jnp.concatenate([row_cos, row_sin], 0).astype(jnp.bfloat16)
    col_cos, col_sin = tables(NZ)
    forward_block = jnp.block([[col_cos, -col_sin], [col_sin, col_cos]]).astype(jnp.bfloat16)
    adjoint_block = jnp.block([[col_cos, col_sin], [-col_sin, col_cos]]).astype(jnp.bfloat16)
    rounded = image.astype(jnp.bfloat16)
    row_count = image.shape[0]
    slices = image.shape[2]
    gathered = gathered_copies(rounded, "coil", 0)
    sensitivity = coil_maps[:, 0]
    weighted = complex_times(
        sensitivity[:, None].astype(jnp.float32), gathered.astype(jnp.float32), False
    ).astype(jnp.bfloat16)
    halfway = column_section(weighted[:, :, None], forward_block).astype(jnp.bfloat16)
    backward = coil_side(halfway, kspace, sampling, row_table)[:, :, 0]
    restored = column_section(backward, adjoint_block)
    adjoint = summed_on_arrival(
        complex_times(sensitivity[:, None].astype(jnp.float32), restored, True).astype(
            jnp.bfloat16
        ),
        "coil",
        0,
    )
    weights = filters.reshape(filters.shape[0], 27, 2)
    padded = extended(rounded, (("coil", 0), ("read", 2)), 1)
    response = respond(padded, weights, row_count, slices)
    energy = lax.psum(jnp.sum(response * response, axis=2).astype(jnp.bfloat16), "echo").astype(
        jnp.float32
    )
    shrunk = shrink(response, energy, thresholds)
    shrunk_pad = extended(shrunk, (("coil", 1), ("read", 3)), 1)
    penalty = transposed(shrunk_pad, weights, row_count, slices)
    return image - dc_weight[None, :, None, None, None] * adjoint - penalty


def solution(mesh):
    return jax.shard_map(
        body,
        mesh=mesh,
        in_specs=(
            P(None, "echo", "coil", "read", None, None),
            P(None, "echo", None),
            P(None, "coil", "read", None, None),
            P("coil", "echo", "read", None, None),
            P(),
            P(),
            P("echo"),
        ),
        out_specs=P("coil", "echo", "read", None, None),
        check_vma=False,
    )
```

profile of v0, /device:TPU:1, one launch (start us, length us, event | category | flops | bytes accessed | tf_op | source)
XLA Modules:
  0.0 205.6 jit_solution(4025107050509815541)
XLA Ops:
  6.5 0.9 copy.1479
  7.5 4.9 %collective-permute-start = (bf16[1,1,2,2,192]{4,0,3,2,1:T(2,128)(2,1)S(1)}, bf16[1,1,2,2,192]{4,0,3,2,1:T(2,128)(2,1)S(1)}, u32[]{:S(2)}, u32[]{:S(2)}) collective-permute-start(bf16[1,1,2,2,192]{4,0,3,2,1:T(2,128)(2,1)S(1)} %get-tuple-element.57), channel_id=1, source_target_pairs={{0,2},{2,4},{4,6},{6,8},{8,10},{10,12},{12,14},{14,16},{16,18},{18... | collective-permute-start | bytes 4616 | tf_op jit(solution)/shard_map/ppermute | solution.py:42
  12.4 1.9 collective-permute-start.1
  14.3 0.9 copy.1485
  15.4 2.0 collective-permute-done.1
  17.4 4.8 %collective-permute-start.2 = (bf16[26,1,1,2,192]{4,0,3,2,1:T(8,128)(2,1)S(1)}, bf16[26,1,1,2,192]{4,0,3,2,1:T(8,128)(2,1)S(1)}, u32[]{:S(2)}, u32[]{:S(2)}) collective-permute-start(bf16[26,1,1,2,192]{4,0,3,2,1:T(8,128)(2,1)S(1)} %get-tuple-element.51), channel_id=1, source_target_pairs={{0,1},{2,3},{4,5},{6,7},{8,9},{10,11},{12,13},{14,15},{16,17},{18,... | collective-permute-start | bytes 59912 | tf_op jit(solution)/shard_map/ppermute | solution.py:42
  22.2 1.3 collective-permute-start.3
  23.7 4.6 %collective-permute-done.3 = bf16[26,1,1,2,192]{4,0,3,2,1:T(8,128)(2,1)S(1)} collective-permute-done((bf16[26,1,1,2,192]{4,0,3,2,1:T(8,128)(2,1)S(1)}, bf16[26,1,1,2,192]{4,0,3,2,1:T(8,128)(2,1)S(1)}, u32[]{:S(2)}, u32[]{:S(2)}) %collective-permute-start.3) | collective-permute-done | bytes 20000 | tf_op jit(solution)/shard_map/ppermute | solution.py:45
  30.3 0.7 copy.1418
  31.0 0.7 copy.1419
  31.7 0.7 copy.1421
  32.4 0.7 copy.1422
  33.2 0.7 copy.1424
  33.9 0.7 copy.1425
  34.6 0.7 copy.1427
  35.3 6.7 %stack.141 = bf16[27,24,1,2,2,192]{5,0,4,3,1,2:T(8,128)(2,1)S(1)} concatenate(bf16[1,24,1,2,2,192]{5,0,4,3,1,2:T(2,128)(2,1)S(1)} %copy.1401, bf16[1,24,1,2,2,192]{5,0,4,3,1,2:T(2,128)(2,1)S(1)} %copy.1402, bf16[1,24,1,2,2,192]{5,0,4,3,1,2:T(2,128)(2,1)S(1)} %copy.1403, bf16[1,24,1,2,2,192]{5,0,4,3,1,2:T(2,128)(2,1)S(1)} %copy.1404, bf16[1,24,1,2,2,192]{5,0,4,3,1,2:T(2,128)(2,1)S(1)} %copy.1405, ...), dimensions={0} | concatenate | bytes 1990656 | tf_op jit(solution)/shard_map/stack | solution.py:119
  42.0 2.4 %fusion.8 = (bf16[48,24,2,192]{3,0,2,1:T(8,128)(2,1)}, f32[24,2,192,48,1]{2,3,4,1,0:T(8,128)}) fusion(bf16[48,27,2,1,1]{0,2,1,4,3:T(2,128)(2,1)S(1)} %bitcast.601, bf16[27,24,1,2,2,192]{5,0,4,3,1,2:T(8,128)(2,1)S(1)} %stack.141), kind=kOutput, calls=%fused_computation.14 | convolution fusion | flops 48660480 | bytes 3654720 | tf_op jit(solution)/shard_map/koc,oyercz->kyerz/dot_general | solution.py:134
  44.5 1.0 broadcast_in_dim.2
  45.5 9.6 %all-to-all-start = ((bf16[16,24,1,2,2,192]{5,1,4,3,2,0:T(8,128)(2,1)}), bf16[16,24,1,2,2,192]{5,1,4,3,2,0:T(8,128)(2,1)S(1)}, u32[]{:S(2)}, u32[]{:S(2)}) async-start(bf16[16,24,1,2,2,192]{5,1,4,3,2,0:T(8,128)(2,1)} %broadcast_in_dim.2), calls=%async_computation | async-start | bytes 1572864 | tf_op jit(solution)/shard_map/all_to_all | solution.py:18
  55.9 0.8 fusion.105
  56.7 0.8 negate_convert_fusion
  57.5 3.2 %multiply_convert_fusion = (bf16[384,384]{1,0:T(8,128)(2,1)S(1)}, bf16[384,384]{1,0:T(8,128)(2,1)}) fusion(), kind=kLoop, calls=%fused_computation.144 | loop fusion | flops 1916928 | bytes 589824 | tf_op jit(solution)/shard_map/convert.22
  60.7 1.0 fusion.98
  61.8 0.7 convert_bitcast_fusion
  62.5 62.9 %all-reduce.4.cloned.1.call-done = bf16[48,24,2,192]{3,0,2,1:T(8,128)(2,1)} async-done(((bf16[48,24,2,192]{3,0,2,1:T(8,128)(2,1)}), bf16[48,24,2,192]{3,0,2,1:T(8,128)(2,1)}) %all-reduce.4.cloned.1.call-update) | async-done | bytes 884752 | tf_op jit(solution)/shard_map/psum | solution.py:194
  125.4 3.0 %fusion.7 = bf16[48,24,2,192]{3,0,2,1:T(8,128)(2,1)S(1)} fusion(f32[24,2,192,48,1]{2,3,4,1,0:T(8,128)} %get-tuple-element.60, bf16[48,24,2,192]{3,0,2,1:T(8,128)(2,1)} %all-reduce.4.cloned.1.call-done, f32[48]{0:T(128)} %param.12), kind=kLoop, calls=%fused_computation.12 | loop fusion | flops 2211840 | bytes 3539136 | tf_op jit(solution)/shard_map/convert_element_type | solution.py:140
  128.5 6.8 %collective-permute-start.5 = (bf16[48,1,1,2,192]{4,0,3,1,2:T(8,128)(2,1)S(1)}, bf16[48,1,1,2,192]{4,0,3,1,2:T(8,128)(2,1)S(1)}, u32[]{:S(2)}, u32[]{:S(2)}) collective-permute-start(bf16[48,1,1,2,192]{4,0,3,1,2:T(8,128)(2,1)S(1)} %get-tuple-element.24), channel_id=1, source_target_pairs={{2,0},{4,2},{6,4},{8,6},{10,8},{12,10},{14,12},{16,14},{18,16},{20... | collective-permute-start | bytes 110600 | tf_op jit(solution)/shard_map/ppermute | solution.py:45
  135.3 3.1 %collective-permute-start.4 = (bf16[48,1,1,2,192]{4,0,3,1,2:T(8,128)(2,1)S(1)}, bf16[48,1,1,2,192]{4,0,3,1,2:T(8,128)(2,1)S(1)}, u32[]{:S(2)}, u32[]{:S(2)}) collective-permute-start(bf16[48,1,1,2,192]{4,0,3,1,2:T(8,128)(2,1)S(1)} %get-tuple-element.23), channel_id=1, source_target_pairs={{0,2},{2,4},{4,6},{6,8},{8,10},{10,12},{12,14},{14,16},{16,18},{18... | collective-permute-start | bytes 110600 | tf_op jit(solution)/shard_map/ppermute | solution.py:42
  138.3 0.9 fusion.115
  139.8 1.1 fusion.121
  140.9 5.4 %collective-permute-start.6 = (bf16[48,26,1,1,192]{4,0,3,1,2:T(8,128)(2,1)}, bf16[48,26,1,1,192]{4,0,3,1,2:T(8,128)(2,1)}, u32[]{:S(2)}, u32[]{:S(2)}) collective-permute-start(bf16[48,26,1,1,192]{4,0,3,1,2:T(8,128)(2,1)} %get-tuple-element.21), channel_id=1, source_target_pairs={{0,1},{2,3},{4,5},{6,7},{8,9},{10,11},{12,13},{14,15},{16,17},{18,... | collective-permute-start | bytes 1437704 | tf_op jit(solution)/shard_map/ppermute | solution.py:42
  146.3 1.5 collective-permute-start.7
  147.8 1.1 fusion.58
  148.8 1.0 fusion.36
  150.0 1.0 fusion.120
  151.1 2.2 %copy.1468 = f32[384,1,2,1,192]{0,4,3,2,1:T(8,128)} copy(f32[384,1,2,1,192]{4,0,3,2,1:T(8,128)} %get-tuple-element.18) | data formatting | bytes 1179648
  153.3 1.1 copy.1469
  154.3 1.4 subtract_convert_fusion.1
  155.8 0.9 copy-done.3
  156.7 0.5 convolution_convert_fusion
  157.2 0.8 fusion.96
  158.3 0.8 copy-done.4
  159.5 0.8 fusion.95
  160.8 0.9 copy-done.2
  161.6 0.5 convolution_bitcast_fusion
  162.9 1.0 copy.1397
  163.8 9.7 %all-to-all-start.1 = ((bf16[16,24,1,2,2,192]{5,1,3,4,2,0:T(8,128)(2,1)}), bf16[16,24,1,2,2,192]{5,1,3,4,2,0:T(8,128)(2,1)S(1)}, u32[]{:S(2)}, u32[]{:S(2)}) async-start(bf16[16,24,1,2,2,192]{5,1,3,4,2,0:T(8,128)(2,1)} %copy.1397), calls=%async_computation.1 | async-start | bytes 1572864 | tf_op jit(solution)/shard_map/all_to_all | solution.py:33
  173.6 1.9 pad_maximum_fusion
  176.0 3.5 %select_maximum_fusion = bf16[48,26,1,4,194]{4,0,3,1,2:T(8,128)(2,1)S(1)} fusion(bf16[48,26,1,1,192]{4,0,3,1,2:T(8,128)(2,1)} %collective-permute-done.7, bf16[48,26,1,1,192]{4,0,3,1,2:T(8,128)(2,1)} %collective-permute-done.6, bf16[48,1,1,2,192]{4,0,3,1,2:T(8,128)(2,1)S(1)} %copy-done.9, bf16[48,24,1,2,192]{4,0,3,1,2:T(8,128)(2,1)S(1)} %bitcast.587, ...), kind=kLoop, calls=%fused_computation.4 | loop fusion | flops 17432064 | bytes 3853824 | tf_op jit(solution)/shard_map/concatenate | solution.py:46
  179.6 0.5 fusion.27
  180.4 0.5 fusion.30
  181.1 0.5 fusion.33
  182.2 0.3 fusion.52
  182.5 0.3 fusion.55
  183.0 0.3 fusion.53
  183.3 0.5 fusion.54
  184.0 0.5 fusion.57
  184.8 0.5 fusion.62
  185.3 0.3 fusion.64
  185.6 0.5 fusion.39
  186.4 0.5 fusion.25
  187.1 0.6 fusion.73
  187.6 8.6 %all-to-all-done.1 = bf16[16,24,1,2,2,192]{5,1,3,4,2,0:T(8,128)(2,1)S(1)} async-done(((bf16[16,24,1,2,2,192]{5,1,3,4,2,0:T(8,128)(2,1)}), bf16[16,24,1,2,2,192]{5,1,3,4,2,0:T(8,128)(2,1)S(1)}, u32[]{:S(2)}, u32[]{:S(2)}) %all-to-all-start.1) | async-done | bytes 589856 | tf_op jit(solution)/shard_map/all_to_all | solution.py:33
  196.4 2.4 %fusion.87 = f32[24,1,2,2,192]{4,3,2,1,0:T(2,128)} fusion(f32[24,1,2,2,192]{4,3,2,0,1:T(2,128)S(1)} %fusion.64, f32[24,1,2,2,192]{4,3,2,0,1:T(2,128)S(1)} %fusion.63, f32[24,1,2,2,192]{4,3,2,0,1:T(2,128)S(1)} %fusion.62, f32[24,1,2,2,192]{4,3,2,0,1:T(2,128)S(1)} %fusion.61, f32[24,1,2,2,192]{4,3,2,0,1:T(2,128)S(1)} %copy-done.15, ...), kind=kOutput, calls=%fused_computation.126 | convolution fusion | flops 2045952 | bytes 2728448 | tf_op jit(solution)/shard_map/kc,kyerz->yercz/dot_general | solution.py:158
  (96 shorter events, 7.7 us)
Async XLA Ops:
  6.5 118.9 %all-reduce.4.cloned.1.call-start = ((), (), s32[]{:S(2)}) async-start(), calls=%async_computation.2 | async-start | bytes 2359296 | tf_op jit(solution)/shard_map/psum | solution.py:194
  7.5 7.9 %collective-permute-start = (bf16[1,1,2,2,192]{4,0,3,2,1:T(2,128)(2,1)S(1)}, bf16[1,1,2,2,192]{4,0,3,2,1:T(2,128)(2,1)S(1)}, u32[]{:S(2)}, u32[]{:S(2)}) collective-permute-start(bf16[1,1,2,2,192]{4,0,3,2,1:T(2,128)(2,1)S(1)} %get-tuple-element.57), channel_id=1, source_target_pairs={{0,2},{2,4},{4,6},{6,8},{8,10},{10,12},{12,14},{14,16},{16,18},{18... | collective-permute-start | bytes 4616 | tf_op jit(solution)/shard_map/ppermute | solution.py:42
  12.4 4.9 %collective-permute-start.1 = (bf16[1,1,2,2,192]{4,0,3,2,1:T(2,128)(2,1)S(1)}, bf16[1,1,2,2,192]{4,0,3,2,1:T(2,128)(2,1)S(1)}, u32[]{:S(2)}, u32[]{:S(2)}) collective-permute-start(bf16[1,1,2,2,192]{4,0,3,2,1:T(2,128)(2,1)S(1)} %get-tuple-element.58), channel_id=1, source_target_pairs={{2,0},{4,2},{6,4},{8,6},{10,8},{12,10},{14,12},{16,14},{18,16},{20... | collective-permute-start | bytes 4616 | tf_op jit(solution)/shard_map/ppermute | solution.py:45
  17.4 6.3 %collective-permute-start.2 = (bf16[26,1,1,2,192]{4,0,3,2,1:T(8,128)(2,1)S(1)}, bf16[26,1,1,2,192]{4,0,3,2,1:T(8,128)(2,1)S(1)}, u32[]{:S(2)}, u32[]{:S(2)}) collective-permute-start(bf16[26,1,1,2,192]{4,0,3,2,1:T(8,128)(2,1)S(1)} %get-tuple-element.51), channel_id=1, source_target_pairs={{0,1},{2,3},{4,5},{6,7},{8,9},{10,11},{12,13},{14,15},{16,17},{18,... | collective-permute-start | bytes 59912 | tf_op jit(solution)/shard_map/ppermute | solution.py:42
  22.2 6.2 %collective-permute-start.3 = (bf16[26,1,1,2,192]{4,0,3,2,1:T(8,128)(2,1)S(1)}, bf16[26,1,1,2,192]{4,0,3,2,1:T(8,128)(2,1)S(1)}, u32[]{:S(2)}, u32[]{:S(2)}) collective-permute-start(bf16[26,1,1,2,192]{4,0,3,2,1:T(8,128)(2,1)S(1)} %get-tuple-element.52), channel_id=1, source_target_pairs={{1,0},{3,2},{5,4},{7,6},{9,8},{11,10},{13,12},{15,14},{17,16},{19,... | collective-permute-start | bytes 59912 | tf_op jit(solution)/shard_map/ppermute | solution.py:45
  35.3 6.7 %copy-start.14 = (bf16[48,3,3,3,2]{0,4,3,2,1:T(2,128)(2,1)S(1)}, bf16[48,3,3,3,2]{0,4,3,2,1:T(2,128)(2,1)}, u32[]{:S(2)}) copy-start(bf16[48,3,3,3,2]{0,4,3,2,1:T(2,128)(2,1)} %param.11) | copy-start | bytes 15556
  42.0 2.4 %copy-start.5 = (f32[24,1,2,2,192]{4,3,2,1,0:T(2,128)S(1)}, f32[24,1,2,2,192]{4,3,2,1,0:T(2,128)}, u32[]{:S(2)}) copy-start(f32[24,1,2,2,192]{4,3,2,1,0:T(2,128)} %param.10) | copy-start | bytes 221188
  44.4 10.7 %copy-start.6 = (bf16[384,1,2,2,192]{0,4,3,2,1:T(8,128)(2,1)S(1)}, bf16[384,1,2,2,192]{0,4,3,2,1:T(8,128)(2,1)}, u32[]{:S(2)}) copy-start(bf16[384,1,2,2,192]{0,4,3,2,1:T(8,128)(2,1)} %param.9) | copy-start | bytes 1769476
  45.5 104.4 %all-to-all-start = ((bf16[16,24,1,2,2,192]{5,1,4,3,2,0:T(8,128)(2,1)}), bf16[16,24,1,2,2,192]{5,1,4,3,2,0:T(8,128)(2,1)S(1)}, u32[]{:S(2)}, u32[]{:S(2)}) async-start(bf16[16,24,1,2,2,192]{5,1,4,3,2,0:T(8,128)(2,1)} %broadcast_in_dim.2), calls=%async_computation | async-start | bytes 1572864 | tf_op jit(solution)/shard_map/all_to_all | solution.py:18
  55.2 6.6 %copy-start.12 = (s32[384,1,192]{0,2,1:T(8,128)S(1)}, s32[384,1,192]{0,2,1:T(8,128)}, u32[]{:S(2)}) copy-start(s32[384,1,192]{0,2,1:T(8,128)} %param.8) | copy-start | bytes 884740
  128.5 10.8 %collective-permute-start.5 = (bf16[48,1,1,2,192]{4,0,3,1,2:T(8,128)(2,1)S(1)}, bf16[48,1,1,2,192]{4,0,3,1,2:T(8,128)(2,1)S(1)}, u32[]{:S(2)}, u32[]{:S(2)}) collective-permute-start(bf16[48,1,1,2,192]{4,0,3,1,2:T(8,128)(2,1)S(1)} %get-tuple-element.24), channel_id=1, source_target_pairs={{2,0},{4,2},{6,4},{8,6},{10,8},{12,10},{14,12},{16,14},{18,16},{20... | collective-permute-start | bytes 110600 | tf_op jit(solution)/shard_map/ppermute | solution.py:45
  135.3 4.2 %collective-permute-start.4 = (bf16[48,1,1,2,192]{4,0,3,1,2:T(8,128)(2,1)S(1)}, bf16[48,1,1,2,192]{4,0,3,1,2:T(8,128)(2,1)S(1)}, u32[]{:S(2)}, u32[]{:S(2)}) collective-permute-start(bf16[48,1,1,2,192]{4,0,3,1,2:T(8,128)(2,1)S(1)} %get-tuple-element.23), channel_id=1, source_target_pairs={{0,2},{2,4},{4,6},{6,8},{8,10},{10,12},{12,14},{14,16},{16,18},{18... | collective-permute-start | bytes 110600 | tf_op jit(solution)/shard_map/ppermute | solution.py:42
  139.3 9.6 %copy-start.8 = (bf16[48,1,1,2,192]{4,0,3,1,2:T(8,128)(2,1)}, bf16[48,1,1,2,192]{4,0,3,1,2:T(8,128)(2,1)S(1)}, u32[]{:S(2)}) copy-start(bf16[48,1,1,2,192]{4,0,3,1,2:T(8,128)(2,1)S(1)} %collective-permute-done.5) | copy-start | bytes 110596
  139.5 8.3 %copy-start.10 = (bf16[48,1,1,2,192]{4,0,3,1,2:T(8,128)(2,1)}, bf16[48,1,1,2,192]{4,0,3,1,2:T(8,128)(2,1)S(1)}, u32[]{:S(2)}) copy-start(bf16[48,1,1,2,192]{4,0,3,1,2:T(8,128)(2,1)S(1)} %collective-permute-done.4) | copy-start | bytes 110596
  140.9 32.6 %collective-permute-start.6 = (bf16[48,26,1,1,192]{4,0,3,1,2:T(8,128)(2,1)}, bf16[48,26,1,1,192]{4,0,3,1,2:T(8,128)(2,1)}, u32[]{:S(2)}, u32[]{:S(2)}) collective-permute-start(bf16[48,26,1,1,192]{4,0,3,1,2:T(8,128)(2,1)} %get-tuple-element.21), channel_id=1, source_target_pairs={{0,1},{2,3},{4,5},{6,7},{8,9},{10,11},{12,13},{14,15},{16,17},{18,... | collective-permute-start | bytes 1437704 | tf_op jit(solution)/shard_map/ppermute | solution.py:42
  146.3 27.3 %collective-permute-start.7 = (bf16[48,26,1,1,192]{4,0,3,1,2:T(8,128)(2,1)}, bf16[48,26,1,1,192]{4,0,3,1,2:T(8,128)(2,1)}, u32[]{:S(2)}, u32[]{:S(2)}) collective-permute-start(bf16[48,26,1,1,192]{4,0,3,1,2:T(8,128)(2,1)} %get-tuple-element.22), channel_id=1, source_target_pairs={{1,0},{3,2},{5,4},{7,6},{9,8},{11,10},{13,12},{15,14},{17,16},{19,... | collective-permute-start | bytes 1437704 | tf_op jit(solution)/shard_map/ppermute | solution.py:45
  155.7 1.0 copy-start.3
  155.7 1.4 copy-start
  158.2 1.0 copy-start.4
  158.2 1.1 copy-start.7
  160.7 1.0 copy-start.2
  162.8 10.7 %copy-start.9 = (bf16[48,1,1,2,192]{4,0,3,1,2:T(8,128)(2,1)S(1)}, bf16[48,1,1,2,192]{4,0,3,1,2:T(8,128)(2,1)}, u32[]{:S(2)}) copy-start(bf16[48,1,1,2,192]{4,0,3,1,2:T(8,128)(2,1)} %copy-done.8) | copy-start | bytes 110596
  162.9 10.7 %copy-start.11 = (bf16[48,1,1,2,192]{4,0,3,1,2:T(8,128)(2,1)S(1)}, bf16[48,1,1,2,192]{4,0,3,1,2:T(8,128)(2,1)}, u32[]{:S(2)}) copy-start(bf16[48,1,1,2,192]{4,0,3,1,2:T(8,128)(2,1)} %copy-done.10) | copy-start | bytes 110596
  163.8 32.3 %all-to-all-start.1 = ((bf16[16,24,1,2,2,192]{5,1,3,4,2,0:T(8,128)(2,1)}), bf16[16,24,1,2,2,192]{5,1,3,4,2,0:T(8,128)(2,1)S(1)}, u32[]{:S(2)}, u32[]{:S(2)}) async-start(bf16[16,24,1,2,2,192]{5,1,3,4,2,0:T(8,128)(2,1)} %copy.1397), calls=%async_computation.1 | async-start | bytes 1572864 | tf_op jit(solution)/shard_map/all_to_all | solution.py:33
  179.6 7.3 %copy-start.1 = (bf16[48,26,1,4,194]{4,0,3,1,2:T(8,128)(2,1)}, bf16[48,26,1,4,194]{4,0,3,1,2:T(8,128)(2,1)S(1)}, u32[]{:S(2)}) copy-start(bf16[48,26,1,4,194]{4,0,3,1,2:T(8,128)(2,1)S(1)} %select_maximum_fusion) | copy-start | bytes 5810692
  186.1 0.9 copy-start.13
  186.1 0.9 copy-start.16
  187.1 9.3 %copy-start.15 = (f32[24,1,2,2,192]{4,3,2,0,1:T(2,128)S(1)}, f32[24,1,2,2,192]{4,3,2,0,1:T(2,128)}, u32[]{:S(2)}) copy-start(f32[24,1,2,2,192]{4,3,2,0,1:T(2,128)} %fusion.58) | copy-start | bytes 221188
Sparse Core Ops, SparseCore 0:
  44.5 80.8 all-reduce.3
where the time goes:
time: 207 us; the launch traced here: 206 us
  waiting for transfers between devices  78.4 us (38%)
  starting transfers between devices  49 us (24%)
  local copies, waits for them, and re-layouts  26.6 us (13%)
  matrix products  18.7 us (9%)
  other arithmetic  18.1 us (9%)
  between operations  14.7 us (7%)
    psum x1, waiting for transfers between devices, body(): lax.psum(jnp.sum(response * response, axis=2).astype(jnp.bfloat16), 'echo')  62.9 us
    ppermute x4, starting transfers between devices, extended(): lax.ppermute(lax.slice_in_dim(block, block.shape[dim] - width, None, axis...  18.2 us
    dot_general x27, matrix products, transposed(): jnp.einsum('kc,kyerz->yercz', weights[:, offset], window, preferred_eleme...  13.8 us
    another operation x30, local copies, waits for them, and re-layouts, respond(): jnp.stack([z_padded[shift_y:shift_y + row_count, :, shift_r:shift_r + sli...  13.5 us
    ppermute x4, starting transfers between devices, extended(): lax.ppermute(lax.slice_in_dim(block, 0, width, axis=dim), axis, backward)  11.5 us
    all_to_all x1, starting transfers between devices, summed_on_arrival(): lax.all_to_all(cut_along(array, dim, length), axis, 0, 0, tiled=True)  9.68 us
    all_to_all x1, starting transfers between devices, from_everyone(): return lax.all_to_all(copies, axis, split_axis=0, concat_axis=0, tiled=True)  9.64 us
    all_to_all x1, waiting for transfers between devices, summed_on_arrival(): lax.all_to_all(cut_along(array, dim, length), axis, 0, 0, tiled=True)  8.58 us
  transfers between devices with their start and end apart: 11, of which 5 were waited for; matrix products, arithmetic and copies ran while one was open for 20% of the time, Pallas kernels for 0%

commit v1 on v0

v1 whole, which is shorter than its diff:
```python
import functools

import jax
import jax.numpy as jnp
import ml_dtypes
import numpy as np
from jax import lax
from jax.experimental import pallas as pl
from jax.experimental.pallas import tpu as pltpu
from jax.sharding import PartitionSpec as P

NY = 384
NZ = 192
FILTERS = 48
ECHOES = 8
COILS = 16
ROWS = NY // COILS
HALO = 2
BAND = 8
WINDOW = BAND + 2
SITES = 3 * FILTERS
BASES = (0, 8, 16, 18)
FIRST = (0, 0, 0, 6)

bf16 = jnp.bfloat16
f32 = jnp.float32


def np_tables(length):
    positions = np.arange(length, dtype=np.int32)
    product = positions[:, None] * positions[None, :] % length
    phases = product.astype(np.float32) * np.float32(2.0 * np.pi / length)
    normalize = np.float32(length ** (-0.5))
    cos = (np.cos(phases) * normalize).astype(ml_dtypes.bfloat16)
    sin = (np.sin(phases) * normalize).astype(ml_dtypes.bfloat16)
    return cos, sin


def np_expansions():
    respond = np.zeros((2, BAND * 3, 54, 256), np.float32)
    spread = np.zeros((2, BAND * 3, 54, 128), np.float32)
    for read in range(2):
        for t in range(BAND):
            for site in range(3):
                for a in range(3):
                    for b in range(3):
                        for d in range(3):
                            for p in range(2):
                                tap = ((a * 3 + b) * 3 + d) * 2 + p
                                sigma = read + site + b - 1
                                if 0 <= sigma < 4:
                                    column = ((d * 2 + sigma // 2) * WINDOW + t + a) * 4
                                    column += (sigma % 2) * 2 + p
                                    respond[read, t * 3 + site, tap, column] = 1
                                own = b + site - read - 1
                                if 0 <= own < 2:
                                    row = (d * WINDOW + t + a) * 4 + own * 2 + p
                                    spread[read, t * 3 + site, tap, row] = 1
    return respond.astype(ml_dtypes.bfloat16), spread.astype(ml_dtypes.bfloat16)


def consistency_kernel(x_ref, mine_ref, other_ref, sampling_ref, row_ref, col_ref, out_ref):
    def dot(left, right):
        return jnp.dot(left, right, preferred_element_type=f32)

    x_real = x_ref[:, 0].astype(f32).reshape(NY, NZ)
    x_imag = x_ref[:, 1].astype(f32).reshape(NY, NZ)
    sampled = sampling_ref[...].astype(f32)
    row = row_ref[...]
    col_cos = col_ref[0]
    col_sin = col_ref[1]
    sum_real = jnp.zeros((NY, NZ), f32)
    sum_imag = jnp.zeros((NY, NZ), f32)
    for ref in (mine_ref, other_ref):
        map_real = ref[2].astype(f32)
        map_imag = ref[3].astype(f32)
        w_real = (map_real * x_real - map_imag * x_imag).astype(bf16)
        w_imag = (map_real * x_imag + map_imag * x_real).astype(bf16)
        h_real = (dot(w_real, col_cos) + dot(w_imag, col_sin)).astype(bf16)
        h_imag = (dot(w_imag, col_cos) - dot(w_real, col_sin)).astype(bf16)
        s_real = dot(row, jnp.concatenate([h_real, h_imag], 0))
        s_imag = dot(row, jnp.concatenate([h_imag, -h_real], 0))
        r_real = (sampled * (s_real - ref[0].astype(f32))).astype(bf16)
        r_imag = (sampled * (s_imag - ref[1].astype(f32))).astype(bf16)
        b_real = dot(row, jnp.concatenate([r_real, -r_imag], 0)).astype(bf16)
        b_imag = dot(row, jnp.concatenate([r_imag, r_real], 0)).astype(bf16)
        o_real = dot(b_real, col_cos) - dot(b_imag, col_sin)
        o_imag = dot(b_real, col_sin) + dot(b_imag, col_cos)
        sum_real = sum_real + map_real * o_real + map_imag * o_imag
        sum_imag = sum_imag + map_real * o_imag - map_imag * o_real
    out_ref[:, 0] = sum_real.reshape(COILS, ROWS, NZ).astype(bf16)
    out_ref[:, 1] = sum_imag.reshape(COILS, ROWS, NZ).astype(bf16)


def consistency(x, mine, other, sampling, row, col):
    return pl.pallas_call(
        consistency_kernel,
        out_shape=jax.ShapeDtypeStruct((COILS, 2, ROWS, NZ), bf16),
        in_specs=[pl.BlockSpec(memory_space=pltpu.VMEM)] * 6,
        out_specs=pl.BlockSpec(memory_space=pltpu.VMEM),
        compiler_params=pltpu.CompilerParams(vmem_limit_bytes=40 << 20),
        cost_estimate=pl.CostEstimate(
            flops=4_000_000_000, bytes_accessed=3_000_000, transcendentals=0
        ),
        name="consistency",
    )(x, mine, other, sampling, row, col)


def regularizer_kernel(
    place_ref, x_ref, weights_ref, spread_ref, thresholds_ref, out_ref, shifted_ref, total_ref
):
    me = place_ref[0]
    for e in range(ECHOES):
        x = x_ref[e].astype(f32)
        zero = jnp.zeros((2, 28 * 4, 1), f32)
        shifted_ref[e, 0] = jnp.concatenate([zero, x[:, :, : NZ - 1]], 2).astype(bf16)
        shifted_ref[e, 1] = x_ref[e]
        shifted_ref[e, 2] = jnp.concatenate([x[:, :, 1:], zero], 2).astype(bf16)
    total_ref[...] = jnp.zeros_like(total_ref)

    def windows(e, base):
        block = shifted_ref[e, :, :, base * 4 : (base + WINDOW) * 4, :]
        return block.reshape(3 * 2 * WINDOW * 4, NZ)

    for base, first in zip(BASES, FIRST):
        weights = weights_ref[first * SITES :, : 3 * 2 * WINDOW * 4]
        energy = None
        for e in range(ECHOES):
            response = jnp.dot(weights, windows(e, base), preferred_element_type=f32)
            square = response * response
            energy = square if energy is None else energy + square
        response = jnp.dot(weights, windows(me, base), preferred_element_type=f32)
        magnitude = jnp.sqrt(energy)
        factor = magnitude / (magnitude + thresholds_ref[first * SITES :, :])
        shrunk = response * factor
        if base == 0:
            top = shrunk[:SITES] * place_ref[1].astype(f32)
            shrunk = jnp.concatenate([top, shrunk[SITES:]], 0)
        if base == BASES[-1]:
            bottom = shrunk[-SITES:] * place_ref[2].astype(f32)
            shrunk = jnp.concatenate([shrunk[:-SITES], bottom], 0)
        part = jnp.dot(
            spread_ref[:, first * SITES :], shrunk.astype(bf16), preferred_element_type=f32
        )
        for d in range(3):
            rows = slice(base * 4, (base + WINDOW) * 4)
            total_ref[d, rows, :] += part[d * WINDOW * 4 : (d + 1) * WINDOW * 4]
    inner = slice(HALO * 4, (HALO + ROWS) * 4)
    zero = jnp.zeros((ROWS * 4, 1), f32)
    out_ref[...] = (
        total_ref[1, inner, :]
        + jnp.concatenate([total_ref[0, inner, 1:], zero], 1)
        + jnp.concatenate([zero, total_ref[2, inner, : NZ - 1]], 1)
    )


def regularizer(place, x, weights, spread, thresholds):
    vmem = pl.BlockSpec(memory_space=pltpu.VMEM)
    return pl.pallas_call(
        regularizer_kernel,
        out_shape=jax.ShapeDtypeStruct((ROWS * 4, NZ), f32),
        in_specs=[pl.BlockSpec(memory_space=pltpu.SMEM), vmem, vmem, vmem, vmem],
        out_specs=vmem,
        scratch_shapes=[
            pltpu.VMEM((ECHOES, 3, 2, 28 * 4, NZ), bf16),
            pltpu.VMEM((3, 28 * 4, NZ), f32),
        ],
        compiler_params=pltpu.CompilerParams(vmem_limit_bytes=40 << 20),
        cost_estimate=pl.CostEstimate(
            flops=9_000_000_000, bytes_accessed=2_000_000, transcendentals=1_000_000
        ),
        name="regularizer",
    )(place, x, weights, spread, thresholds)


def body(kspace, sampling, coil_maps, image, filters, thresholds, dc_weight):
    row_cos, row_sin = np_tables(NY)
    row = jnp.asarray(np.concatenate([row_cos, row_sin], 1))
    col = jnp.asarray(np.stack(np_tables(NZ)))
    coil = lax.axis_index("coil")
    core = lax.rem(coil, 2)
    echo = lax.axis_index("echo")
    read = lax.axis_index("read")

    lines = image.reshape(ROWS * 4, NZ)
    rounded = lines.astype(bf16)
    planes = rounded.reshape(ROWS, 2, 2, NZ).transpose(1, 2, 0, 3)
    sent = jnp.broadcast_to(planes[None], (COILS // 2, 2, 2, ROWS, NZ))
    gathered = lax.all_to_all(sent.reshape(COILS, 2, ROWS, NZ), "coil", 0, 0, tiled=True)

    first = rounded[: HALO * 4]
    last = rounded[-HALO * 4 :]
    even = core == 0
    on_chip = [(i, i ^ 1) for i in range(COILS)]
    next_chip = [(i, i + 1) for i in range(1, COILS - 1, 2)]
    next_chip += [(j, i) for i, j in next_chip]
    near = lax.ppermute(jnp.where(even, last, first), "coil", on_chip)
    far = lax.ppermute(jnp.where(even, first, last), "coil", next_chip)
    above = jnp.where(even, far, near)
    below = jnp.where(even, near, far)
    extended = jnp.concatenate([above, rounded, below], 0)
    echoes = lax.all_to_all(
        jnp.broadcast_to(extended[None], (2 * ECHOES, *extended.shape)),
        ("echo", "read"),
        0,
        0,
        tiled=True,
    ).reshape(ECHOES, 2, 28 * 4, NZ)

    both = jnp.concatenate(
        [kspace[:, 0, 0].transpose(1, 2, 0, 3), coil_maps[:, 0].transpose(1, 2, 0, 3)], 1
    )
    mine = lax.dynamic_index_in_dim(both, core, 0, keepdims=False)
    other = lax.ppermute(
        lax.dynamic_index_in_dim(both, 1 - core, 0, keepdims=False), "coil", on_chip
    )
    partial = consistency(gathered, mine, other, sampling[:, 0], row, col)
    arrived = lax.all_to_all(partial, "coil", 0, 0, tiled=True)

    respond, spread = np_expansions()
    taps = filters.reshape(FILTERS, 54)
    respond = lax.dynamic_index_in_dim(jnp.asarray(respond), read, 0, keepdims=False)
    spread = lax.dynamic_index_in_dim(jnp.asarray(spread), read, 0, keepdims=False)
    weights = jnp.einsum("kc,ycl->ykl", taps, respond, preferred_element_type=f32)
    weights = weights.astype(bf16).reshape(BAND * SITES, 256)
    spread = jnp.einsum("ycl,kc->lyk", spread, taps, preferred_element_type=f32)
    spread = spread.astype(bf16).reshape(128, BAND * SITES)
    levels = jnp.broadcast_to(
        jnp.tile(thresholds, BAND * 3)[:, None], (BAND * SITES, NZ)
    )
    place = jnp.stack([echo, (coil > 0).astype(jnp.int32), (coil < COILS - 1).astype(jnp.int32)])
    penalty = regularizer(place.astype(jnp.int32), echoes, weights, spread, levels)

    summed = jnp.sum(arrived.reshape(COILS // 2, 2, 2, ROWS, NZ).astype(f32), axis=0)
    adjoint = summed.transpose(2, 0, 1, 3).reshape(ROWS * 4, NZ)
    updated = lines - dc_weight[0] * adjoint - penalty
    return updated.reshape(image.shape)


def solution(mesh):
    return jax.shard_map(
        body,
        mesh=mesh,
        in_specs=(
            P(None, "echo", "coil", "read", None, None),
            P(None, "echo", None),
            P(None, "coil", "read", None, None),
            P("coil", "echo", "read", None, None),
            P(),
            P(),
            P("echo"),
        ),
        out_specs=P("coil", "echo", "read", None, None),
        check_vma=False,
    )
```

time: 207 us -> 74.2 us (0.36)
  waiting for transfers between devices: 78.4 us -> 24.1 us
  starting transfers between devices: 49 us -> 24.1 us
  local copies, waits for them, and re-layouts: 26.6 us -> 8.94 us
  other arithmetic: 18.1 us -> 2.12 us
  matrix products: 18.7 us -> 2.76 us
  between operations: 14.7 us -> 0.94 us
  Pallas kernels: 0 us -> 10.6 us
    psum x1 -> x0, waiting for transfers between devices: 62.9 us -> none  [body(): lax.psum(jnp.sum(response * response, axis=2).astype(jnp.bfloat16), 'echo')]
    ppermute x8 -> x3, starting transfers between devices: 29.7 us -> 5.14 us  [the longest x1 4.94 us: body(): far = lax.ppermute(jnp.where(even, first, last), 'coil', next_chip)]
    all_to_all x2 -> x3, waiting for transfers between devices: 8.58 us -> 24.1 us  [the longest x1 11.9 us: body(): lax.all_to_all(sent.reshape(COILS, 2, ROWS, NZ), 'coil', 0, 0, tiled=True)]
    another operation x33 -> x1, local copies, waits for them, and re-layouts: 14.8 us -> 0.01 us  [body(): jnp.tile(thresholds, BAND * 3)[:, None]]
    dot_general x30 -> x2, matrix products: 17.1 us -> 2.76 us  [the longest x1 1.5 us: body(): jnp.einsum('kc,ycl->ykl', taps, respond, preferred_element_type=f32)]
    pallas_call x0 -> x2, Pallas kernels: none -> 10.6 us  [the longest x1 6.98 us: regularizer(): pl.pallas_call(regularizer_kernel, out_shape=jax.ShapeDtypeStruct((ROWS *...]
    concatenate x7 -> x1, other arithmetic: 6.95 us -> 0.01 us  [body(): extended = jnp.concatenate([above, rounded, below], 0)]
    ppermute x8 -> x3, waiting for transfers between devices: 6.87 us -> 0.01 us  [the longest x1 0.01 us: body(): far = lax.ppermute(jnp.where(even, first, last), 'coil', next_chip)]
  transfers between devices with their start and end apart: 11 -> 6, of which waited for: 5 -> 3; matrix products, arithmetic and copies ran while one was open for 20% -> 14% of each run, Pallas kernels for 0% -> 14%
where the time goes in v1:
time: 74.2 us; the launch traced here: 73.6 us
  starting transfers between devices  24.1 us (32%)
  waiting for transfers between devices  24.1 us (32%)
  Pallas kernels  10.6 us (14%)
  local copies, waits for them, and re-layouts  8.94 us (12%)
  matrix products  2.76 us (4%)
  other arithmetic  2.12 us (3%)
  between operations  0.94 us (1%)
    all_to_all x1, waiting for transfers between devices, body(): lax.all_to_all(sent.reshape(COILS, 2, ROWS, NZ), 'coil', 0, 0, tiled=True)  11.9 us
    all_to_all x1, starting transfers between devices, body(): lax.all_to_all(sent.reshape(COILS, 2, ROWS, NZ), 'coil', 0, 0, tiled=True)  8.07 us
    pallas_call x1, Pallas kernels, regularizer(): pl.pallas_call(regularizer_kernel, out_shape=jax.ShapeDtypeStruct((ROWS *...  6.98 us
    all_to_all x1, starting transfers between devices, body(): lax.all_to_all(jnp.broadcast_to(extended[None], (2 * ECHOES, *extended.sh...  6.93 us
    all_to_all x1, waiting for transfers between devices, body(): lax.all_to_all(jnp.broadcast_to(extended[None], (2 * ECHOES, *extended.sh...  6.3 us
    all_to_all x1, waiting for transfers between devices, body(): arrived = lax.all_to_all(partial, 'coil', 0, 0, tiled=True)  5.85 us
    ppermute x1, starting transfers between devices, body(): far = lax.ppermute(jnp.where(even, first, last), 'coil', next_chip)  4.94 us
    all_to_all x1, starting transfers between devices, body(): arrived = lax.all_to_all(partial, 'coil', 0, 0, tiled=True)  4 us
  transfers between devices with their start and end apart: 6, of which 3 were waited for; matrix products, arithmetic and copies ran while one was open for 14% of the time, Pallas kernels for 14%

profile of v1, /device:TPU:1, one launch (start us, length us, event | category | flops | bytes accessed | tf_op | source)
XLA Modules:
  0.0 73.6 jit_solution(15742090127331720119)
XLA Ops:
  0.0 0.0 copy-start.2
  0.0 0.0 copy-start.3
  0.0 1.1 %reshape.34 = f32[96,192]{1,0:T(8,128)S(1)} reshape(f32[24,1,2,2,192]{4,3,2,1,0:T(2,128)} %param.14) | data formatting | bytes 147456 | tf_op jit(solution)/shard_map/reshape | solution.py:185
  1.1 4.9 %collective-permute-start.1 = (bf16[8,192]{1,0:T(8,128)(2,1)S(1)}, bf16[8,192]{1,0:T(8,128)(2,1)S(1)}, u32[]{:S(2)}, u32[]{:S(2)}) collective-permute-start(bf16[8,192]{1,0:T(8,128)(2,1)S(1)} %get-tuple-element.7), channel_id=1, source_target_pairs={{2,4},{6,8},{10,12},{14,16},{18,20},{22,24},{26,28},{4,2},{8,6},{1... | collective-permute-start | bytes 9224 | tf_op jit(solution)/shard_map/ppermute | solution.py:198
  6.0 0.1 collective-permute-start.2
  6.1 0.9 %convert_bitcast_fusion = bf16[2,2,24,192]{3,1,0,2:T(2,128)(2,1)S(1)} fusion(f32[24,1,2,2,192]{4,3,2,1,0:T(2,128)} %param.14), kind=kLoop, calls=%fused_computation.17 | loop fusion | flops 18432 | bytes 110592 | tf_op jit(solution)/shard_map/transpose | solution.py:187
  7.1 0.8 %broadcast_in_dim.8 = bf16[8,2,2,24,192]{4,3,2,1,0:T(8,128)(2,1)} broadcast(bf16[2,2,24,192]{3,2,1,0:T(8,128)(2,1)S(1)} %copy.28), dimensions={1,2,3,4} | broadcast | bytes 331776 | tf_op jit(solution)/shard_map/broadcast_in_dim | solution.py:188
  7.9 8.1 %all-to-all-start = ((bf16[16,2,24,192]{3,2,1,0:T(8,128)(2,1)}), bf16[16,2,24,192]{3,2,1,0:T(8,128)(2,1)S(1)}, u32[]{:S(2)}, u32[]{:S(2)}) async-start(bf16[16,2,24,192]{3,2,1,0:T(8,128)(2,1)} %bitcast.3), calls=%async_computation | async-start | bytes 786432 | tf_op jit(solution)/shard_map/all_to_all | solution.py:189
  15.9 0.0 copy-done.2
  16.0 0.0 copy-done.3
  16.0 0.0 copy-start.6
  16.0 1.0 %fusion.3 = (bf16[4,384,192]{1,2,0:T(8,128)(2,1)}, bf16[1,4,384,192]{2,3,1,0:T(8,128)(2,1)S(1)}) fusion(s32[]{:T(128)S(6)} %select_n.34, bf16[2,2,384,192]{2,3,1,0:T(8,128)(2,1)S(1)} %bitcast.52, bf16[2,2,384,192]{2,3,1,0:T(8,128)(2,1)S(1)} %bitcast.53, s32[]{:T(128)S(6)} %select_n.33), kind=kLoop, calls=%fused_computation.10 | loop fusion | flops 589824 | bytes 2359304 | tf_op jit(solution)/shard_map/jit(dynamic_index_in_dim)/squeeze | solution.py:215
  16.9 0.1 collective-permute-start
  17.1 0.0 copy-done.6
  17.1 0.0 copy-start.5
  17.1 1.3 %convolution_convert_fusion.1 = bf16[24,128,48]{1,2,0:T(8,128)(2,1)S(1)} fusion(bf16[2,24,54,128]{3,2,1,0:T(8,128)(2,1)} %constant.53.clone, s32[]{:T(128)S(6)} %select_n.40, bf16[48,54]{0,1:T(8,128)(2,1)S(1)} %reshape.37), kind=kOutput, calls=%fused_computation.5 | convolution fusion | flops 16072704 | bytes 644164 | tf_op jit(solution)/shard_map/ycl,kc->lyk/dot_general | solution.py:226
  18.4 0.0 collective-permute-done.1
  18.4 0.0 collective-permute-done.2
  18.4 0.0 copy-done.5
  18.4 0.1 copy.33
  18.6 11.9 %all-to-all-done.x_ref = bf16[16,2,24,192]{3,2,1,0:T(8,128)(2,1)S(1)} async-done(((bf16[16,2,24,192]{3,2,1,0:T(8,128)(2,1)}), bf16[16,2,24,192]{3,2,1,0:T(8,128)(2,1)S(1)}, u32[]{:S(2)}, u32[]{:S(2)}) %all-to-all-start) | async-done | bytes 294944 | tf_op jit(solution)/shard_map/all_to_all | solution.py:189
  30.5 1.1 %broadcast_in_dim.9 = bf16[16,112,192]{1,2,0:T(8,128)(2,1)} broadcast(bf16[112,192]{0,1:T(8,128)(2,1)S(1)} %copy.33), dimensions={1,2} | broadcast | bytes 731136 | tf_op jit(solution)/shard_map/broadcast_in_dim | solution.py:203
  31.6 0.0 copy-start.7
  31.6 6.9 %all-to-all-start.2 = ((bf16[16,112,192]{1,2,0:T(8,128)(2,1)}), bf16[16,112,192]{1,2,0:T(8,128)(2,1)}, u32[]{:S(2)}, u32[]{:S(2)}) async-start(bf16[16,112,192]{1,2,0:T(8,128)(2,1)} %broadcast_in_dim.9), calls=%async_computation.2 | async-start | bytes 1572864 | tf_op jit(solution)/shard_map/all_to_all | solution.py:202
  38.5 0.0 copy-start.4
  38.5 0.1 pad_add_fusion.place_ref
  38.6 0.2 copy.37.spread_ref
  38.8 0.0 copy-done.7
  38.8 0.1 broadcast_in_dim.10
  38.9 0.3 copy.29
  39.2 0.3 copy-done.4
  39.5 0.2 copy.30
  40.3 0.0 copy-start.1
  40.3 1.5 %convolution_convert_fusion = bf16[24,256,48]{1,2,0:T(8,128)(2,1)S(1)} fusion(bf16[2,24,54,256]{3,2,1,0:T(8,128)(2,1)} %constant.52.clone, s32[]{:T(128)S(6)} %select_n.40, bf16[48,54]{0,1:T(8,128)(2,1)} %copy-done.5), kind=kOutput, calls=%fused_computation.4 | convolution fusion | flops 32145408 | bytes 1292292 | tf_op jit(solution)/shard_map/kc,ycl->ykl/dot_general | solution.py:224
  41.8 0.0 collective-permute-done
  41.8 1.3 %copy.31.other_ref = bf16[4,384,192]{2,1,0:T(8,128)(2,1)S(1)} copy(bf16[4,384,192]{1,2,0:T(8,128)(2,1)} %collective-permute-done) | data formatting | bytes 1179648 | tf_op jit(solution)/shard_map/ppermute | solution.py:214
  43.2 0.0 copy-done.1
  43.2 0.0 copy-start
  43.2 1.1 %copy-done = bf16[384,768]{1,0:T(8,128)(2,1)S(1)} copy-done((bf16[384,768]{1,0:T(8,128)(2,1)S(1)}, bf16[384,768]{1,0:T(8,128)(2,1)}, u32[]{:S(2)}) %copy-start) | copy-done | bytes 589848
  44.2 3.6 %consistency.1 = bf16[16,2,24,192]{3,2,1,0:T(8,128)(2,1)} custom-call(bf16[16,2,24,192]{3,2,1,0:T(8,128)(2,1)S(1)} %all-to-all-done.x_ref, bf16[4,384,192]{2,1,0:T(8,128)(2,1)S(1)} %bitcast.47, bf16[4,384,192]{2,1,0:T(8,128)(2,1)S(1)} %copy.31.other_ref, s32[384,192]{1,0:T(8,128)S(1)} %bitcast.49, bf16[384,768]{1,0:T(8,128)(2,1)S(1)} %copy-done, ...), custom_call_target="tpu_custom_call" | custom-call | flops 4000000000 | bytes 3000000 | tf_op jit(solution)/shard_map/consistency/pallas_call | solution.py:96
  47.9 6.3 %all-to-all-done.2 = bf16[16,112,192]{1,2,0:T(8,128)(2,1)} async-done(((bf16[16,112,192]{1,2,0:T(8,128)(2,1)}), bf16[16,112,192]{1,2,0:T(8,128)(2,1)}, u32[]{:S(2)}, u32[]{:S(2)}) %all-to-all-start.2) | async-done | bytes 688160 | tf_op jit(solution)/shard_map/all_to_all | solution.py:202
  54.2 4.0 %all-to-all-start.1 = ((bf16[16,2,24,192]{3,2,1,0:T(8,128)(2,1)}), bf16[16,2,24,192]{3,2,1,0:T(8,128)(2,1)S(1)}, u32[]{:S(2)}, u32[]{:S(2)}) async-start(bf16[16,2,24,192]{3,2,1,0:T(8,128)(2,1)} %consistency.1), calls=%async_computation.1 | async-start | bytes 786432 | tf_op jit(solution)/shard_map/all_to_all | solution.py:218
  58.2 1.4 %copy.34 = bf16[16,112,192]{2,1,0:T(8,128)(2,1)S(1)} copy(bf16[16,112,192]{1,2,0:T(8,128)(2,1)} %all-to-all-done.2) | data formatting | bytes 1376256 | tf_op jit(solution)/shard_map/all_to_all | solution.py:202
  59.6 0.2 broadcast_in_dim.22.thresholds_ref
  59.8 7.0 %regularizer.1 = f32[96,192]{1,0:T(8,128)S(1)} custom-call(s32[3]{0:T(128)S(1)} %pad_add_fusion.place_ref, bf16[8,2,112,192]{3,2,1,0:T(8,128)(2,1)S(1)} %bitcast.46, bf16[1152,256]{1,0:T(8,128)(2,1)S(1)} %bitcast.48, bf16[128,1152]{1,0:T(8,128)(2,1)S(1)} %copy.37.spread_ref, f32[1152,192]{1,0:T(8,128)S(1)} %broadcast_in_dim.22.thresholds_ref), custom_call_target="tpu_custom_call" | custom-call | flops 8999999488 | bytes 2000000 | tf_op jit(solution)/shard_map/regularizer/pallas_call | solution.py:159
  66.8 5.8 %all-to-all-done.1 = bf16[16,2,24,192]{3,2,1,0:T(8,128)(2,1)S(1)} async-done(((bf16[16,2,24,192]{3,2,1,0:T(8,128)(2,1)}), bf16[16,2,24,192]{3,2,1,0:T(8,128)(2,1)S(1)}, u32[]{:S(2)}, u32[]{:S(2)}) %all-to-all-start.1) | async-done | bytes 294944 | tf_op jit(solution)/shard_map/all_to_all | solution.py:218
  72.7 0.1 convert_reduce_fusion
  72.7 0.1 copy.32
  72.8 0.1 mul.15
  72.9 0.7 reshape.40
  (9 shorter events, 0.1 us)
Async XLA Ops:
  0.0 15.9 %copy-start.2 = (bf16[384,1,1,2,2,192]{0,5,4,3,2,1:T(8,128)(2,1)S(1)}, bf16[384,1,1,2,2,192]{0,5,4,3,2,1:T(8,128)(2,1)}, u32[]{:S(2)}) copy-start(bf16[384,1,1,2,2,192]{0,5,4,3,2,1:T(8,128)(2,1)} %param.11) | copy-start | bytes 1769476
  0.0 15.9 %copy-start.3 = (bf16[384,1,2,2,192]{0,4,3,2,1:T(8,128)(2,1)S(1)}, bf16[384,1,2,2,192]{0,4,3,2,1:T(8,128)(2,1)}, u32[]{:S(2)}) copy-start(bf16[384,1,2,2,192]{0,4,3,2,1:T(8,128)(2,1)} %param.13) | copy-start | bytes 1769476
  1.1 17.3 %collective-permute-start.1 = (bf16[8,192]{1,0:T(8,128)(2,1)S(1)}, bf16[8,192]{1,0:T(8,128)(2,1)S(1)}, u32[]{:S(2)}, u32[]{:S(2)}) collective-permute-start(bf16[8,192]{1,0:T(8,128)(2,1)S(1)} %get-tuple-element.7), channel_id=1, source_target_pairs={{2,4},{6,8},{10,12},{14,16},{18,20},{22,24},{26,28},{4,2},{8,6},{1... | collective-permute-start | bytes 9224 | tf_op jit(solution)/shard_map/ppermute | solution.py:198
  6.0 12.4 %collective-permute-start.2 = (bf16[8,192]{1,0:T(8,128)(2,1)S(1)}, bf16[8,192]{1,0:T(8,128)(2,1)S(1)}, u32[]{:S(2)}, u32[]{:S(2)}) collective-permute-start(bf16[8,192]{1,0:T(8,128)(2,1)S(1)} %get-tuple-element.8), channel_id=1, source_target_pairs={{0,2},{2,0},{4,6},{6,4},{8,10},{10,8},{12,14},{14,12},{16,18},{18,... | collective-permute-start | bytes 9224 | tf_op jit(solution)/shard_map/ppermute | solution.py:197
  7.9 22.6 %all-to-all-start = ((bf16[16,2,24,192]{3,2,1,0:T(8,128)(2,1)}), bf16[16,2,24,192]{3,2,1,0:T(8,128)(2,1)S(1)}, u32[]{:S(2)}, u32[]{:S(2)}) async-start(bf16[16,2,24,192]{3,2,1,0:T(8,128)(2,1)} %bitcast.3), calls=%async_computation | async-start | bytes 786432 | tf_op jit(solution)/shard_map/all_to_all | solution.py:189
  16.0 1.1 %copy-start.6 = (bf16[48,3,3,3,2]{0,4,3,2,1:T(2,128)(2,1)S(1)}, bf16[48,3,3,3,2]{0,4,3,2,1:T(2,128)(2,1)}, u32[]{:S(2)}) copy-start(bf16[48,3,3,3,2]{0,4,3,2,1:T(2,128)(2,1)} %param.15) | copy-start | bytes 15556
  16.9 24.9 %collective-permute-start = (bf16[4,384,192]{1,2,0:T(8,128)(2,1)}, bf16[4,384,192]{1,2,0:T(8,128)(2,1)}, u32[]{:S(2)}, u32[]{:S(2)}) collective-permute-start(bf16[4,384,192]{1,2,0:T(8,128)(2,1)} %get-tuple-element.5), channel_id=1, source_target_pairs={{0,2},{2,0},{4,6},{6,4},{8,10},{10,8},{12,14},{14,12},{16,18},{18,... | collective-permute-start | bytes 1769480 | tf_op jit(solution)/shard_map/ppermute | solution.py:214
  17.1 1.3 %copy-start.5 = (bf16[48,54]{0,1:T(8,128)(2,1)}, bf16[48,54]{0,1:T(8,128)(2,1)S(1)}, u32[]{:S(2)}) copy-start(bf16[48,54]{0,1:T(8,128)(2,1)S(1)} %reshape.37) | copy-start | bytes 15556
  31.6 7.2 %copy-start.7 = (f32[48]{0:T(128)S(1)}, f32[48]{0:T(128)}, u32[]{:S(2)}) copy-start(f32[48]{0:T(128)} %param.16) | copy-start | bytes 580
  31.6 22.6 %all-to-all-start.2 = ((bf16[16,112,192]{1,2,0:T(8,128)(2,1)}), bf16[16,112,192]{1,2,0:T(8,128)(2,1)}, u32[]{:S(2)}, u32[]{:S(2)}) async-start(bf16[16,112,192]{1,2,0:T(8,128)(2,1)} %broadcast_in_dim.9), calls=%async_computation.2 | async-start | bytes 1572864 | tf_op jit(solution)/shard_map/all_to_all | solution.py:202
  38.5 1.0 %copy-start.4 = (s32[384,1,192]{0,2,1:T(8,128)S(1)}, s32[384,1,192]{0,2,1:T(8,128)}, u32[]{:S(2)}) copy-start(s32[384,1,192]{0,2,1:T(8,128)} %param.12) | copy-start | bytes 884740
  40.3 2.9 %copy-start.1 = (bf16[2,192,192]{2,1,0:T(8,128)(2,1)S(1)}, bf16[2,192,192]{2,1,0:T(8,128)(2,1)}, u32[]{:S(2)}) copy-start(bf16[2,192,192]{2,1,0:T(8,128)(2,1)} %constant.51.clone.col_ref) | copy-start | bytes 442372
  43.2 1.1 %copy-start = (bf16[384,768]{1,0:T(8,128)(2,1)S(1)}, bf16[384,768]{1,0:T(8,128)(2,1)}, u32[]{:S(2)}) copy-start(bf16[384,768]{1,0:T(8,128)(2,1)} %constant.50.clone.row_ref) | copy-start | bytes 1769476
  54.2 18.5 %all-to-all-start.1 = ((bf16[16,2,24,192]{3,2,1,0:T(8,128)(2,1)}), bf16[16,2,24,192]{3,2,1,0:T(8,128)(2,1)S(1)}, u32[]{:S(2)}, u32[]{:S(2)}) async-start(bf16[16,2,24,192]{3,2,1,0:T(8,128)(2,1)} %consistency.1), calls=%async_computation.1 | async-start | bytes 786432 | tf_op jit(solution)/shard_map/all_to_all | solution.py:218

commit v2 on v1

v2 whole, which is shorter than its diff:
```python
import functools

import jax
import jax.numpy as jnp
import ml_dtypes
import numpy as np
from jax import lax
from jax.experimental import pallas as pl
from jax.experimental.pallas import tpu as pltpu
from jax.sharding import PartitionSpec as P

NY = 384
NZ = 192
FILTERS = 48
ECHOES = 8
COILS = 16
ROWS = NY // COILS
HALO = 2
BAND = 8
WINDOW = BAND + 2
SITES = 3 * FILTERS
PAIR = 2
LINES = ROWS + 2 * HALO
BASES = (0, 8, 16, 18)
FIRST = (0, 0, 0, 6)

bf16 = jnp.bfloat16
f32 = jnp.float32


def np_tables(length):
    positions = np.arange(length, dtype=np.int32)
    product = positions[:, None] * positions[None, :] % length
    phases = product.astype(np.float32) * np.float32(2.0 * np.pi / length)
    normalize = np.float32(length ** (-0.5))
    cos = (np.cos(phases) * normalize).astype(ml_dtypes.bfloat16)
    sin = (np.sin(phases) * normalize).astype(ml_dtypes.bfloat16)
    return cos, sin


def np_expansions():
    respond = np.zeros((2, 3, 54, 256), np.float32)
    spread = np.zeros((2, PAIR * 3, 54, 48), np.float32)
    for read in range(2):
        for site in range(3):
            for a in range(3):
                for b in range(3):
                    for d in range(3):
                        for p in range(2):
                            tap = ((a * 3 + b) * 3 + d) * 2 + p
                            sigma = read + site + b - 1
                            if 0 <= sigma < 4:
                                half = (sigma // 2) ^ read
                                column = ((d * 2 + half) * WINDOW + a) * 4
                                column += (sigma % 2) * 2 + p
                                respond[read, site, tap, column] = 1
                            own = b + site - read - 1
                            if 0 <= own < 2:
                                for t in range(PAIR):
                                    row = (d * (PAIR + 2) + t + a) * 4 + own * 2 + p
                                    spread[read, t * 3 + site, tap, row] = 1
    return respond.astype(ml_dtypes.bfloat16), spread.astype(ml_dtypes.bfloat16)


def prepare_kernel(place_ref, image_ref, sent_ref, lines_ref, near_ref, far_ref, rows_ref):
    pad = jnp.zeros((ROWS, 256 - NZ), f32)
    for s in range(2):
        for p in range(2):
            plane = image_ref[:, 0, s, p, :]
            rows = pl.ds(s * 2 + p, ROWS, stride=4)
            rows_ref[0, rows, :] = plane[:, :128]
            rows_ref[1, rows, :] = jnp.concatenate([plane[:, 128:], pad], 1)
            plane = plane.astype(bf16)
            for z in range(COILS // 2):
                sent_ref[2 * z + s, p] = plane
    lines = jnp.concatenate([rows_ref[0], rows_ref[1, :, : NZ - 128]], 1)
    lines_ref[...] = lines.astype(bf16)
    first = lines[: HALO * 4]
    last = lines[(ROWS - HALO) * 4 :]
    even = place_ref[0] == 0
    near_ref[...] = jnp.where(even, last, first).astype(bf16)
    far_ref[...] = jnp.where(even, first, last).astype(bf16)


def prepare(place, image):
    vmem = pl.BlockSpec(memory_space=pltpu.VMEM)
    return pl.pallas_call(
        prepare_kernel,
        out_shape=(
            jax.ShapeDtypeStruct((COILS, 2, ROWS, NZ), bf16),
            jax.ShapeDtypeStruct((ROWS * 4, NZ), bf16),
            jax.ShapeDtypeStruct((HALO * 4, NZ), bf16),
            jax.ShapeDtypeStruct((HALO * 4, NZ), bf16),
        ),
        in_specs=[pl.BlockSpec(memory_space=pltpu.SMEM), vmem],
        out_specs=(vmem, vmem, vmem, vmem),
        scratch_shapes=[pltpu.VMEM((2, ROWS * 4, 128), f32)],
        compiler_params=pltpu.CompilerParams(vmem_limit_bytes=8 << 20),
        name="prepare",
    )(place, image)


def consistency_kernel(
    x_ref, sampling_ref, mine, other_hbm, row_hbm, col_hbm, out_ref, other, row_v, col_v, sem
):
    copies = [
        pltpu.make_async_copy(source, target, sem.at[i])
        for i, (source, target) in enumerate(
            ((col_hbm, col_v), (row_hbm, row_v), (other_hbm, other))
        )
    ]
    for copy in copies:
        copy.start()

    def dot(left, right):
        return jnp.dot(left, right, preferred_element_type=f32)

    x_real = x_ref[:, 0].astype(f32).reshape(NY, NZ)
    x_imag = x_ref[:, 1].astype(f32).reshape(NY, NZ)
    sampled = sampling_ref[...].astype(f32)
    sum_real = jnp.zeros((NY, NZ), f32)
    sum_imag = jnp.zeros((NY, NZ), f32)
    copies[0].wait()
    for ref in (mine, other):
        if ref is other:
            copies[2].wait()
        map_real = ref[2].astype(f32)
        map_imag = ref[3].astype(f32)
        w_real = (map_real * x_real - map_imag * x_imag).astype(bf16)
        w_imag = (map_real * x_imag + map_imag * x_real).astype(bf16)
        h_real = (dot(w_real, col_v[0]) + dot(w_imag, col_v[1])).astype(bf16)
        h_imag = (dot(w_imag, col_v[0]) - dot(w_real, col_v[1])).astype(bf16)
        if ref is mine:
            copies[1].wait()
        row = row_v[...]
        s_real = dot(row, jnp.concatenate([h_real, h_imag], 0))
        s_imag = dot(row, jnp.concatenate([h_imag, -h_real], 0))
        r_real = (sampled * (s_real - ref[0].astype(f32))).astype(bf16)
        r_imag = (sampled * (s_imag - ref[1].astype(f32))).astype(bf16)
        b_real = dot(row, jnp.concatenate([r_real, -r_imag], 0)).astype(bf16)
        b_imag = dot(row, jnp.concatenate([r_imag, r_real], 0)).astype(bf16)
        o_real = dot(b_real, col_v[0]) - dot(b_imag, col_v[1])
        o_imag = dot(b_real, col_v[1]) + dot(b_imag, col_v[0])
        sum_real = sum_real + map_real * o_real + map_imag * o_imag
        sum_imag = sum_imag + map_real * o_imag - map_imag * o_real
    out_ref[:, 0] = sum_real.reshape(COILS, ROWS, NZ).astype(bf16)
    out_ref[:, 1] = sum_imag.reshape(COILS, ROWS, NZ).astype(bf16)


def consistency(x, sampling, mine, other, row, col):
    vmem = pl.BlockSpec(memory_space=pltpu.VMEM)
    hbm = pl.BlockSpec(memory_space=pltpu.HBM)
    return pl.pallas_call(
        consistency_kernel,
        out_shape=jax.ShapeDtypeStruct((COILS, 2, ROWS, NZ), bf16),
        in_specs=[vmem, vmem, vmem, hbm, hbm, hbm],
        out_specs=vmem,
        scratch_shapes=[
            pltpu.VMEM((4, NY, NZ), bf16),
            pltpu.VMEM((NY, 2 * NY), bf16),
            pltpu.VMEM((2, NZ, NZ), bf16),
            pltpu.SemaphoreType.DMA((3,)),
        ],
        compiler_params=pltpu.CompilerParams(vmem_limit_bytes=20 << 20),
        cost_estimate=pl.CostEstimate(
            flops=4_000_000_000, bytes_accessed=3_000_000, transcendentals=0
        ),
        name="consistency",
    )(x, sampling, mine, other, row, col)


def regularizer_kernel(
    place_ref,
    x0_ref,
    x1_ref,
    x2_ref,
    x3_ref,
    taps_ref,
    respond_ref,
    spread_ref,
    thresholds_ref,
    out_ref,
    weights_ref,
    shifted_ref,
    total_ref,
):
    for site in range(3):
        taps = jnp.dot(taps_ref[...], respond_ref[site], preferred_element_type=f32)
        for t in range(BAND):
            rolled = pltpu.roll(taps, 4 * t, 1) if t else taps
            start = (t * 3 + site) * FILTERS
            weights_ref[start : start + FILTERS, :] = rolled.astype(bf16)
    zero = jnp.zeros((2, LINES * 4, 1), f32)
    for e in range(ECHOES):
        ref = (x0_ref, x1_ref, x2_ref, x3_ref)[e // 2]
        x = ref[e % 2].astype(f32)
        shifted_ref[e, 0] = jnp.concatenate([zero, x[:, :, : NZ - 1]], 2).astype(bf16)
        shifted_ref[e, 1] = ref[e % 2]
        shifted_ref[e, 2] = jnp.concatenate([x[:, :, 1:], zero], 2).astype(bf16)
    total_ref[...] = jnp.zeros_like(total_ref)
    spread = spread_ref[...]

    for base, first in zip(BASES, FIRST):
        weights = weights_ref[first * SITES :, : 3 * 2 * WINDOW * 4]
        energy = None
        for e in reversed(range(ECHOES)):
            block = shifted_ref[e, :, :, base * 4 : (base + WINDOW) * 4, :]
            window = block.reshape(3 * 2 * WINDOW * 4, NZ)
            response = jnp.dot(weights, window, preferred_element_type=f32)
            square = response * response
            energy = square if energy is None else energy + square
        magnitude = jnp.sqrt(energy)
        factor = magnitude / (magnitude + thresholds_ref[first * SITES :, :])
        shrunk = response * factor
        if base == 0:
            top = shrunk[:SITES] * place_ref[1].astype(f32)
            shrunk = jnp.concatenate([top, shrunk[SITES:]], 0)
        if base == BASES[-1]:
            bottom = shrunk[-SITES:] * place_ref[2].astype(f32)
            shrunk = jnp.concatenate([shrunk[:-SITES], bottom], 0)
        shrunk = shrunk.astype(bf16)
        for t in range(0, BAND - first, PAIR):
            pair = shrunk[t * SITES : (t + PAIR) * SITES]
            part = jnp.dot(spread, pair, preferred_element_type=f32)
            size = (PAIR + 2) * 4
            start = (base + first + t) * 4
            for d in range(3):
                total_ref[d, start : start + size, :] += part[d * size : (d + 1) * size]
    inner = slice(HALO * 4, (HALO + ROWS) * 4)
    zero = jnp.zeros((ROWS * 4, 1), f32)
    penalty = (
        total_ref[1, inner, :]
        + jnp.concatenate([total_ref[0, inner, 1:], zero], 1)
        + jnp.concatenate([zero, total_ref[2, inner, : NZ - 1]], 1)
    )
    pad = jnp.zeros((ROWS * 4, 256 - NZ), f32)
    out_ref[0] = penalty[:, :128]
    out_ref[1] = jnp.concatenate([penalty[:, 128:], pad], 1)


def regularizer(place, blocks, taps, respond, spread, thresholds):
    vmem = pl.BlockSpec(memory_space=pltpu.VMEM)
    return pl.pallas_call(
        regularizer_kernel,
        out_shape=jax.ShapeDtypeStruct((2, ROWS * 4, 128), f32),
        in_specs=[pl.BlockSpec(memory_space=pltpu.SMEM)] + [vmem] * 8,
        out_specs=vmem,
        scratch_shapes=[
            pltpu.VMEM((BAND * SITES, 256), bf16),
            pltpu.VMEM((ECHOES, 3, 2, LINES * 4, NZ), bf16),
            pltpu.VMEM((3, LINES * 4, NZ), f32),
        ],
        compiler_params=pltpu.CompilerParams(vmem_limit_bytes=20 << 20),
        cost_estimate=pl.CostEstimate(
            flops=9_000_000_000, bytes_accessed=2_000_000, transcendentals=1_000_000
        ),
        name="regularizer",
    )(place, *blocks, taps, respond, spread, thresholds)


def update_kernel(weight_ref, image_ref, arrived_ref, penalty_ref, out_ref):
    for s in range(2):
        for p in range(2):
            total = arrived_ref[s, p].astype(f32)
            for z in range(1, COILS // 2):
                total = total + arrived_ref[2 * z + s, p].astype(f32)
            rows = pl.ds(s * 2 + p, ROWS, stride=4)
            penalty = jnp.concatenate(
                [penalty_ref[0, rows, :], penalty_ref[1, rows, :][:, : NZ - 128]], 1
            )
            out_ref[:, 0, s, p, :] = image_ref[:, 0, s, p, :] - weight_ref[0] * total - penalty


def update(weight, image, arrived, penalty):
    vmem = pl.BlockSpec(memory_space=pltpu.VMEM)
    return pl.pallas_call(
        update_kernel,
        out_shape=jax.ShapeDtypeStruct(image.shape, f32),
        in_specs=[pl.BlockSpec(memory_space=pltpu.SMEM), vmem, vmem, vmem],
        out_specs=vmem,
        compiler_params=pltpu.CompilerParams(vmem_limit_bytes=8 << 20),
        name="update",
    )(weight, image, arrived, penalty)


def body(kspace, sampling, coil_maps, image, filters, thresholds, dc_weight):
    row_cos, row_sin = np_tables(NY)
    row = jnp.asarray(np.concatenate([row_cos, row_sin], 1))
    col = jnp.asarray(np.stack(np_tables(NZ)))
    coil = lax.axis_index("coil")
    core = lax.rem(coil, 2)
    read = lax.axis_index("read")
    place = jnp.stack([core, (coil > 0).astype(jnp.int32), (coil < COILS - 1).astype(jnp.int32)])

    sent, lines, near, far = prepare(place, image)
    gathered = lax.all_to_all(sent, "coil", 0, 0, tiled=True)

    even = core == 0
    on_chip = [(i, i ^ 1) for i in range(COILS)]
    next_chip = [(i, i + 1) for i in range(1, COILS - 1, 2)]
    next_chip += [(j, i) for i, j in next_chip]
    near = lax.ppermute(near, "coil", on_chip)
    far = lax.ppermute(far, "coil", next_chip)
    above = jnp.where(even, far, near)
    below = jnp.where(even, near, far)
    extended = jnp.concatenate([above, lines, below], 0)

    def swap(block, flip):
        pairs = [(i, i ^ flip) for i in range(2 * ECHOES)]
        return lax.ppermute(block, ("echo", "read"), pairs)

    quad = jnp.stack([extended] + [swap(extended, flip) for flip in (1, 8, 9)])
    quad = quad.reshape(2, 2, LINES * 4, NZ)
    blocks = [quad] + [swap(quad, flip) for flip in (2, 4, 6)]

    both = jnp.concatenate(
        [kspace[:, 0, 0].transpose(1, 2, 0, 3), coil_maps[:, 0].transpose(1, 2, 0, 3)], 1
    )
    mine = lax.dynamic_index_in_dim(both, core, 0, keepdims=False)
    other = lax.ppermute(
        lax.dynamic_index_in_dim(both, 1 - core, 0, keepdims=False), "coil", on_chip
    )
    partial = consistency(gathered, sampling[:, 0], mine, other, row, col)
    arrived = lax.all_to_all(partial, "coil", 0, 0, tiled=True)

    respond, spread = np_expansions()
    taps = filters.reshape(FILTERS, 54)
    respond = lax.dynamic_index_in_dim(jnp.asarray(respond), read, 0, keepdims=False)
    spread = lax.dynamic_index_in_dim(jnp.asarray(spread), read, 0, keepdims=False)
    spread = jnp.einsum("ycl,kc->lyk", spread, taps, preferred_element_type=f32)
    spread = spread.astype(bf16).reshape(48, PAIR * SITES)
    levels = jnp.broadcast_to(jnp.tile(thresholds, BAND * 3)[:, None], (BAND * SITES, NZ))
    penalty = regularizer(place, blocks, taps, respond, spread, levels)
    return update(dc_weight, image, arrived, penalty)


def solution(mesh):
    return jax.shard_map(
        body,
        mesh=mesh,
        in_specs=(
            P(None, "echo", "coil", "read", None, None),
            P(None, "echo", None),
            P(None, "coil", "read", None, None),
            P("coil", "echo", "read", None, None),
            P(),
            P(),
            P("echo"),
        ),
        out_specs=P("coil", "echo", "read", None, None),
        check_vma=False,
    )
```

time: 74.2 us -> 66.3 us (0.89)
  waiting for transfers between devices: 24.1 us -> 12.9 us
  starting transfers between devices: 24.1 us -> 31.6 us
  local copies, waits for them, and re-layouts: 8.94 us -> 5.3 us
  Pallas kernels: 10.6 us -> 13.4 us
  matrix products: 2.76 us -> 0.15 us
    all_to_all x2 -> x1, waiting for transfers between devices: 18.2 us -> 0.01 us  [body(): gathered = lax.all_to_all(sent, 'coil', 0, 0, tiled=True)]
    ppermute x2 -> x8, starting transfers between devices: 5.03 us -> 13.5 us  [the longest x6 8.52 us: swap(): return lax.ppermute(block, ('echo', 'read'), pairs)]
    all_to_all x2 -> x1, starting transfers between devices: 15 us -> 7.69 us  [body(): gathered = lax.all_to_all(sent, 'coil', 0, 0, tiled=True)]
    all_to_all x1, starting transfers between devices: 4 us -> 9.77 us  [body(): arrived = lax.all_to_all(partial, 'coil', 0, 0, tiled=True)]
    ppermute x2 -> x8, waiting for transfers between devices: 0.01 us -> 5.4 us  [the longest x6 5.39 us: swap(): return lax.ppermute(block, ('echo', 'read'), pairs)]
    pallas_call x1 -> x3, Pallas kernels: 6.98 us -> 8.96 us  [the longest x1 6.76 us: regularizer(): pl.pallas_call(regularizer_kernel, out_shape=jax.ShapeDtypeStruct((2, ROW...]
    broadcast_in_dim x2 -> x0, local copies, waits for them, and re-layouts: 1.85 us -> none  [the longest x1 1.07 us: body(): jnp.broadcast_to(extended[None], (2 * ECHOES, *extended.shape))]
    reshape x3 -> x1, local copies, waits for them, and re-layouts: 1.96 us -> 0.12 us  [body(): spread = spread.astype(bf16).reshape(48, PAIR * SITES)]
  transfers between devices with their start and end apart: 6 -> 11, of which waited for: 3 -> 3; matrix products, arithmetic and copies ran while one was open for 14% -> 6% of each run, Pallas kernels for 14% -> 17%
where the time goes in v2:
time: 66.3 us; the launch traced here: 65.8 us
  starting transfers between devices  31.6 us (48%)
  Pallas kernels  13.4 us (20%)
  waiting for transfers between devices  12.9 us (19%)
  local copies, waits for them, and re-layouts  5.3 us (8%)
  other arithmetic  1.56 us (2%)
  between operations  0.92 us (1%)
    all_to_all x1, starting transfers between devices, body(): arrived = lax.all_to_all(partial, 'coil', 0, 0, tiled=True)  9.77 us
    ppermute x6, starting transfers between devices, swap(): return lax.ppermute(block, ('echo', 'read'), pairs)  8.52 us
    all_to_all x1, starting transfers between devices, body(): gathered = lax.all_to_all(sent, 'coil', 0, 0, tiled=True)  7.69 us
    all_to_all x1, waiting for transfers between devices, body(): arrived = lax.all_to_all(partial, 'coil', 0, 0, tiled=True)  7.53 us
    pallas_call x1, Pallas kernels, regularizer(): pl.pallas_call(regularizer_kernel, out_shape=jax.ShapeDtypeStruct((2, ROW...  6.76 us
    ppermute x6, waiting for transfers between devices, swap(): return lax.ppermute(block, ('echo', 'read'), pairs)  5.39 us
    ppermute x1, starting transfers between devices, body(): far = lax.ppermute(far, 'coil', next_chip)  4.92 us
    pallas_call x1, Pallas kernels, consistency(): pl.pallas_call(consistency_kernel, out_shape=jax.ShapeDtypeStruct((COILS,...  4.45 us
  transfers between devices with their start and end apart: 11, of which 3 were waited for; matrix products, arithmetic and copies ran while one was open for 6% of the time, Pallas kernels for 17%

profile of v2, /device:TPU:1, one launch (start us, length us, event | category | flops | bytes accessed | tf_op | source)
XLA Modules:
  0.0 65.8 jit_solution(4905164259351418837)
XLA Ops:
  0.0 0.1 pad_add_fusion.place_ref
  0.1 0.0 copy-start
  0.1 0.9 %copy-done = f32[24,1,2,2,192]{4,3,2,1,0:T(2,128)S(1)} copy-done((f32[24,1,2,2,192]{4,3,2,1,0:T(2,128)S(1)}, f32[24,1,2,2,192]{4,3,2,1,0:T(2,128)}, u32[]{:S(2)}) %copy-start) | copy-done | bytes 73752
  1.0 1.4 %prepare.1 = (bf16[16,2,24,192]{3,2,1,0:T(8,128)(2,1)}, bf16[96,192]{1,0:T(8,128)(2,1)S(1)}, bf16[8,192]{1,0:T(8,128)(2,1)S(1)}, bf16[8,192]{1,0:T(8,128)(2,1)S(1)}) custom-call(s32[3]{0:T(128)S(1)} %pad_add_fusion.place_ref, f32[24,1,2,2,192]{4,3,2,1,0:T(2,128)S(1)} %copy-done), custom_call_target="tpu_custom_call" | custom-call | tf_op jit(solution)/shard_map/prepare/pallas_call | solution.py:87
  2.4 4.9 %collective-permute-start.1 = (bf16[8,192]{1,0:T(8,128)(2,1)S(1)}, bf16[8,192]{1,0:T(8,128)(2,1)S(1)}, u32[]{:S(2)}, u32[]{:S(2)}) collective-permute-start(bf16[8,192]{1,0:T(8,128)(2,1)S(1)} %get-tuple-element.10), channel_id=1, source_target_pairs={{2,4},{6,8},{10,12},{14,16},{18,20},{22,24},{26,28},{4,2},{8,6},{1... | collective-permute-start | bytes 9224 | tf_op jit(solution)/shard_map/ppermute | solution.py:303
  7.3 0.1 collective-permute-start.2
  7.4 0.0 copy-start.5
  7.5 0.0 copy-start.7
  7.5 1.4 %fusion.2 = (bf16[4,384,192]{1,2,0:T(8,128)(2,1)S(1)}, bf16[1,4,384,192]{2,3,1,0:T(8,128)(2,1)S(1)}) fusion(s32[]{:T(128)S(6)} %select_n.26, bf16[2,2,384,192]{2,3,1,0:T(8,128)(2,1)} %bitcast.37, bf16[2,2,384,192]{2,3,1,0:T(8,128)(2,1)} %bitcast.38, s32[]{:T(128)S(6)} %select_n.25), kind=kLoop, calls=%fused_computation.7 | loop fusion | flops 589824 | bytes 2359304 | tf_op jit(solution)/shard_map/jit(dynamic_index_in_dim)/squeeze | solution.py:321
  8.9 0.0 copy-start.6
  8.9 0.0 copy-start.8
  8.9 0.6 collective-permute-start
  9.5 7.7 %all-to-all-start = ((bf16[16,2,24,192]{3,2,1,0:T(8,128)(2,1)}), bf16[16,2,24,192]{3,2,1,0:T(8,128)(2,1)S(1)}, u32[]{:S(2)}, u32[]{:S(2)}) async-start(bf16[16,2,24,192]{3,2,1,0:T(8,128)(2,1)} %get-tuple-element.9), calls=%async_computation | async-start | bytes 786432 | tf_op jit(solution)/shard_map/all_to_all | solution.py:296
  17.1 0.0 copy-start.4
  17.2 0.0 copy-done.5
  17.2 0.0 copy-done.7
  17.2 0.1 fusion
  17.4 0.0 collective-permute-done.1
  17.4 0.0 collective-permute-done.2
  17.4 3.0 %collective-permute-start.3 = (bf16[112,192]{1,0:T(8,128)(2,1)S(1)}, bf16[112,192]{1,0:T(8,128)(2,1)S(1)}, u32[]{:S(2)}, u32[]{:S(2)}) collective-permute-start(bf16[112,192]{1,0:T(8,128)(2,1)S(1)} %get-tuple-element.16), channel_id=1, source_target_pairs={{0,1},{1,0},{32,33},{33,32},{64,65},{65,64},{96,97},{97,96},{128,1... | collective-permute-start | bytes 129032 | tf_op jit(solution)/shard_map/ppermute | solution.py:310
  20.4 2.7 %collective-permute-start.4 = (bf16[112,192]{1,0:T(8,128)(2,1)S(1)}, bf16[112,192]{1,0:T(8,128)(2,1)S(1)}, u32[]{:S(2)}, u32[]{:S(2)}) collective-permute-start(bf16[112,192]{1,0:T(8,128)(2,1)S(1)} %get-tuple-element.16), channel_id=1, source_target_pairs={{0,128},{1,129},{32,160},{33,161},{64,192},{65,193},{96,224},{97,2... | collective-permute-start | bytes 129032 | tf_op jit(solution)/shard_map/ppermute | solution.py:310
  23.2 0.0 collective-permute-start.5
  23.2 0.0 copy-done.6
  23.3 0.1 reshape.13.spread_ref
  23.4 0.0 copy-done.8
  23.4 0.1 broadcast_in_dim.7
  23.5 0.1 copy.26.taps_ref
  23.6 0.3 copy.23
  23.9 0.0 copy-done.4
  23.9 0.2 copy.22
  24.7 0.0 collective-permute-done.3
  24.7 0.5 collective-permute-done.4
  25.3 4.9 %collective-permute-done.5 = bf16[112,192]{1,0:T(8,128)(2,1)S(1)} collective-permute-done((bf16[112,192]{1,0:T(8,128)(2,1)S(1)}, bf16[112,192]{1,0:T(8,128)(2,1)S(1)}, u32[]{:S(2)}, u32[]{:S(2)}) %collective-permute-start.5) | collective-permute-done | bytes 43040 | tf_op jit(solution)/shard_map/ppermute | solution.py:310
  30.1 0.1 pad_maximum_fusion
  30.2 0.5 collective-permute-start.6
  30.7 0.3 collective-permute-start.7
  31.0 1.9 %collective-permute-start.8 = (bf16[2,2,112,192]{3,2,1,0:T(8,128)(2,1)S(1)}, bf16[2,2,112,192]{3,2,1,0:T(8,128)(2,1)S(1)}, u32[]{:S(2)}, u32[]{:S(2)}) collective-permute-start(bf16[2,2,112,192]{3,2,1,0:T(8,128)(2,1)S(1)} %bitcast.35), channel_id=1, source_target_pairs={{0,96},{1,97},{32,64},{33,65},{64,32},{65,33},{96,0},{97,1},{128,2... | collective-permute-start | bytes 516104 | tf_op jit(solution)/shard_map/ppermute | solution.py:310
  32.9 0.0 collective-permute-done
  32.9 1.3 %copy.24.other_hbm = bf16[4,384,192]{2,1,0:T(8,128)(2,1)S(1)} copy(bf16[4,384,192]{1,2,0:T(8,128)(2,1)} %collective-permute-done) | data formatting | bytes 1179648 | tf_op jit(solution)/shard_map/ppermute | solution.py:320
  34.3 0.0 all-to-all-done.x_ref
  34.3 0.0 copy-start.2
  34.3 1.1 %copy-done.2 = bf16[384,768]{1,0:T(8,128)(2,1)S(1)} copy-done((bf16[384,768]{1,0:T(8,128)(2,1)S(1)}, bf16[384,768]{1,0:T(8,128)(2,1)}, u32[]{:S(2)}) %copy-start.2) | copy-done | bytes 589848
  35.3 0.0 copy-start.3
  35.3 0.9 %copy-done.3 = bf16[2,192,192]{2,1,0:T(8,128)(2,1)S(1)} copy-done((bf16[2,192,192]{2,1,0:T(8,128)(2,1)S(1)}, bf16[2,192,192]{2,1,0:T(8,128)(2,1)}, u32[]{:S(2)}) %copy-start.3) | copy-done | bytes 147480
  36.3 4.5 %consistency.1 = bf16[16,2,24,192]{3,2,1,0:T(8,128)(2,1)} custom-call(bf16[16,2,24,192]{3,2,1,0:T(8,128)(2,1)S(1)} %all-to-all-done.x_ref, s32[384,192]{1,0:T(8,128)S(1)} %bitcast.32, bf16[4,384,192]{2,1,0:T(8,128)(2,1)S(1)} %bitcast.31, bf16[4,384,192]{2,1,0:T(8,128)(2,1)S(1)} %copy.24.other_hbm, bf16[384,768]{1,0:T(8,128)(2,1)S(1)} %copy-done.2, ...), custom_call_target="tpu_custom_call" | custom-call | flops 4000000000 | bytes 3000000 | tf_op jit(solution)/shard_map/consistency/pallas_call | solution.py:153
  40.7 9.8 %all-to-all-start.1 = ((bf16[16,2,24,192]{3,2,1,0:T(8,128)(2,1)}), bf16[16,2,24,192]{3,2,1,0:T(8,128)(2,1)S(1)}, u32[]{:S(2)}, u32[]{:S(2)}) async-start(bf16[16,2,24,192]{3,2,1,0:T(8,128)(2,1)} %consistency.1), calls=%async_computation.1 | async-start | bytes 786432 | tf_op jit(solution)/shard_map/all_to_all | solution.py:324
  50.5 0.0 collective-permute-done.6.x1_ref
  50.5 0.0 collective-permute-done.7.x2_ref
  50.5 0.0 collective-permute-done.8.x3_ref
  50.5 0.2 broadcast_in_dim.8.thresholds_ref
  50.8 0.0 copy-start.1
  50.8 6.8 %regularizer.1.penalty_ref = f32[2,96,128]{2,1,0:T(8,128)S(1)} custom-call(s32[3]{0:T(128)S(1)} %pad_add_fusion.place_ref, bf16[2,2,112,192]{3,2,1,0:T(8,128)(2,1)S(1)} %bitcast.36, bf16[2,2,112,192]{3,2,1,0:T(8,128)(2,1)S(1)} %collective-permute-done.6.x1_ref, bf16[2,2,112,192]{3,2,1,0:T(8,128)(2,1)S(1)} %collective-permute-done.7.x2_ref, ...), custom_call_target="tpu_custom_call" | custom-call | flops 8999999488 | bytes 2000000 | tf_op jit(solution)/shard_map/regularizer/pallas_call | solution.py:243
  57.5 7.5 %all-to-all-done.1.arrived_ref = bf16[16,2,24,192]{3,2,1,0:T(8,128)(2,1)S(1)} async-done(((bf16[16,2,24,192]{3,2,1,0:T(8,128)(2,1)}), bf16[16,2,24,192]{3,2,1,0:T(8,128)(2,1)S(1)}, u32[]{:S(2)}, u32[]{:S(2)}) %all-to-all-start.1) | async-done | bytes 294944 | tf_op jit(solution)/shard_map/all_to_all | solution.py:324
  65.1 0.0 copy-done.1
  65.1 0.8 %update.1 = f32[24,1,2,2,192]{4,3,2,1,0:T(2,128)} custom-call(f32[1]{0:T(128)S(6)} %copy.27.weight_ref, f32[24,1,2,2,192]{4,3,2,1,0:T(2,128)S(1)} %copy-done.1, bf16[16,2,24,192]{3,2,1,0:T(8,128)(2,1)S(1)} %all-to-all-done.1.arrived_ref, f32[2,96,128]{2,1,0:T(8,128)S(1)} %regularizer.1.penalty_ref), custom_call_target="tpu_custom_call" | custom-call | tf_op jit(solution)/shard_map/update/pallas_call | solution.py:276
  (7 shorter events, 0.1 us)
Async XLA Ops:
  0.1 0.9 %copy-start = (f32[24,1,2,2,192]{4,3,2,1,0:T(2,128)S(1)}, f32[24,1,2,2,192]{4,3,2,1,0:T(2,128)}, u32[]{:S(2)}) copy-start(f32[24,1,2,2,192]{4,3,2,1,0:T(2,128)} %image_ref.3) | copy-start | bytes 221188
  2.4 15.0 %collective-permute-start.1 = (bf16[8,192]{1,0:T(8,128)(2,1)S(1)}, bf16[8,192]{1,0:T(8,128)(2,1)S(1)}, u32[]{:S(2)}, u32[]{:S(2)}) collective-permute-start(bf16[8,192]{1,0:T(8,128)(2,1)S(1)} %get-tuple-element.10), channel_id=1, source_target_pairs={{2,4},{6,8},{10,12},{14,16},{18,20},{22,24},{26,28},{4,2},{8,6},{1... | collective-permute-start | bytes 9224 | tf_op jit(solution)/shard_map/ppermute | solution.py:303
  7.3 10.0 %collective-permute-start.2 = (bf16[8,192]{1,0:T(8,128)(2,1)S(1)}, bf16[8,192]{1,0:T(8,128)(2,1)S(1)}, u32[]{:S(2)}, u32[]{:S(2)}) collective-permute-start(bf16[8,192]{1,0:T(8,128)(2,1)S(1)} %get-tuple-element.11), channel_id=1, source_target_pairs={{0,2},{2,0},{4,6},{6,4},{8,10},{10,8},{12,14},{14,12},{16,18},{18,... | collective-permute-start | bytes 9224 | tf_op jit(solution)/shard_map/ppermute | solution.py:302
  7.4 9.7 %copy-start.5 = (bf16[48,3,3,3,2]{0,4,3,2,1:T(2,128)(2,1)S(1)}, bf16[48,3,3,3,2]{0,4,3,2,1:T(2,128)(2,1)}, u32[]{:S(2)}) copy-start(bf16[48,3,3,3,2]{0,4,3,2,1:T(2,128)(2,1)} %param.15) | copy-start | bytes 15556
  7.5 9.7 %copy-start.7 = (bf16[2,6,54,48]{2,3,1,0:T(8,128)(2,1)S(1)}, bf16[2,6,54,48]{2,3,1,0:T(8,128)(2,1)}, u32[]{:S(2)}) copy-start(bf16[2,6,54,48]{2,3,1,0:T(8,128)(2,1)} %constant.45.clone) | copy-start | bytes 186628
  8.9 14.3 %copy-start.6 = (bf16[2,3,54,256]{3,2,1,0:T(8,128)(2,1)S(1)}, bf16[2,3,54,256]{3,2,1,0:T(8,128)(2,1)}, u32[]{:S(2)}) copy-start(bf16[2,3,54,256]{3,2,1,0:T(8,128)(2,1)} %constant.44.clone) | copy-start | bytes 497668
  8.9 14.5 %copy-start.8 = (f32[48]{0:T(128)S(1)}, f32[48]{0:T(128)}, u32[]{:S(2)}) copy-start(f32[48]{0:T(128)} %param.16) | copy-start | bytes 580
  8.9 24.0 %collective-permute-start = (bf16[4,384,192]{1,2,0:T(8,128)(2,1)S(1)}, bf16[4,384,192]{1,2,0:T(8,128)(2,1)}, u32[]{:S(2)}, u32[]{:S(2)}) collective-permute-start(bf16[4,384,192]{1,2,0:T(8,128)(2,1)S(1)} %get-tuple-element.13), channel_id=1, source_target_pairs={{0,2},{2,0},{4,6},{6,4},{8,10},{10,8},{12,14},{14,12},{16,18},{18,... | collective-permute-start | bytes 1769480 | tf_op jit(solution)/shard_map/ppermute | solution.py:320
  9.5 24.8 %all-to-all-start = ((bf16[16,2,24,192]{3,2,1,0:T(8,128)(2,1)}), bf16[16,2,24,192]{3,2,1,0:T(8,128)(2,1)S(1)}, u32[]{:S(2)}, u32[]{:S(2)}) async-start(bf16[16,2,24,192]{3,2,1,0:T(8,128)(2,1)} %get-tuple-element.9), calls=%async_computation | async-start | bytes 786432 | tf_op jit(solution)/shard_map/all_to_all | solution.py:296
  17.1 6.8 %copy-start.4 = (s32[384,1,192]{0,2,1:T(8,128)S(1)}, s32[384,1,192]{0,2,1:T(8,128)}, u32[]{:S(2)}) copy-start(s32[384,1,192]{0,2,1:T(8,128)} %param.12) | copy-start | bytes 884740
  17.4 7.3 %collective-permute-start.3 = (bf16[112,192]{1,0:T(8,128)(2,1)S(1)}, bf16[112,192]{1,0:T(8,128)(2,1)S(1)}, u32[]{:S(2)}, u32[]{:S(2)}) collective-permute-start(bf16[112,192]{1,0:T(8,128)(2,1)S(1)} %get-tuple-element.16), channel_id=1, source_target_pairs={{0,1},{1,0},{32,33},{33,32},{64,65},{65,64},{96,97},{97,96},{128,1... | collective-permute-start | bytes 129032 | tf_op jit(solution)/shard_map/ppermute | solution.py:310
  20.4 4.8 %collective-permute-start.4 = (bf16[112,192]{1,0:T(8,128)(2,1)S(1)}, bf16[112,192]{1,0:T(8,128)(2,1)S(1)}, u32[]{:S(2)}, u32[]{:S(2)}) collective-permute-start(bf16[112,192]{1,0:T(8,128)(2,1)S(1)} %get-tuple-element.16), channel_id=1, source_target_pairs={{0,128},{1,129},{32,160},{33,161},{64,192},{65,193},{96,224},{97,2... | collective-permute-start | bytes 129032 | tf_op jit(solution)/shard_map/ppermute | solution.py:310
  23.2 6.9 %collective-permute-start.5 = (bf16[112,192]{1,0:T(8,128)(2,1)S(1)}, bf16[112,192]{1,0:T(8,128)(2,1)S(1)}, u32[]{:S(2)}, u32[]{:S(2)}) collective-permute-start(bf16[112,192]{1,0:T(8,128)(2,1)S(1)} %get-tuple-element.16), channel_id=1, source_target_pairs={{0,129},{1,128},{32,161},{33,160},{64,193},{65,192},{96,225},{97,2... | collective-permute-start | bytes 129032 | tf_op jit(solution)/shard_map/ppermute | solution.py:310
  30.2 20.3 %collective-permute-start.6 = (bf16[2,2,112,192]{3,2,1,0:T(8,128)(2,1)S(1)}, bf16[2,2,112,192]{3,2,1,0:T(8,128)(2,1)S(1)}, u32[]{:S(2)}, u32[]{:S(2)}) collective-permute-start(bf16[2,2,112,192]{3,2,1,0:T(8,128)(2,1)S(1)} %bitcast.33), channel_id=1, source_target_pairs={{0,32},{1,33},{32,0},{33,1},{64,96},{65,97},{96,64},{97,65},{128,1... | collective-permute-start | bytes 516104 | tf_op jit(solution)/shard_map/ppermute | solution.py:310
  30.7 19.8 %collective-permute-start.7 = (bf16[2,2,112,192]{3,2,1,0:T(8,128)(2,1)S(1)}, bf16[2,2,112,192]{3,2,1,0:T(8,128)(2,1)S(1)}, u32[]{:S(2)}, u32[]{:S(2)}) collective-permute-start(bf16[2,2,112,192]{3,2,1,0:T(8,128)(2,1)S(1)} %bitcast.34), channel_id=1, source_target_pairs={{0,64},{1,65},{32,96},{33,97},{64,0},{65,1},{96,32},{97,33},{128,1... | collective-permute-start | bytes 516104 | tf_op jit(solution)/shard_map/ppermute | solution.py:310
  31.0 19.5 %collective-permute-start.8 = (bf16[2,2,112,192]{3,2,1,0:T(8,128)(2,1)S(1)}, bf16[2,2,112,192]{3,2,1,0:T(8,128)(2,1)S(1)}, u32[]{:S(2)}, u32[]{:S(2)}) collective-permute-start(bf16[2,2,112,192]{3,2,1,0:T(8,128)(2,1)S(1)} %bitcast.35), channel_id=1, source_target_pairs={{0,96},{1,97},{32,64},{33,65},{64,32},{65,33},{96,0},{97,1},{128,2... | collective-permute-start | bytes 516104 | tf_op jit(solution)/shard_map/ppermute | solution.py:310
  34.3 1.1 %copy-start.2 = (bf16[384,768]{1,0:T(8,128)(2,1)S(1)}, bf16[384,768]{1,0:T(8,128)(2,1)}, u32[]{:S(2)}) copy-start(bf16[384,768]{1,0:T(8,128)(2,1)} %constant.42.clone.row_hbm) | copy-start | bytes 1769476
  35.3 0.9 %copy-start.3 = (bf16[2,192,192]{2,1,0:T(8,128)(2,1)S(1)}, bf16[2,192,192]{2,1,0:T(8,128)(2,1)}, u32[]{:S(2)}) copy-start(bf16[2,192,192]{2,1,0:T(8,128)(2,1)} %constant.43.clone.col_hbm) | copy-start | bytes 442372
  40.7 24.3 %all-to-all-start.1 = ((bf16[16,2,24,192]{3,2,1,0:T(8,128)(2,1)}), bf16[16,2,24,192]{3,2,1,0:T(8,128)(2,1)S(1)}, u32[]{:S(2)}, u32[]{:S(2)}) async-start(bf16[16,2,24,192]{3,2,1,0:T(8,128)(2,1)} %consistency.1), calls=%async_computation.1 | async-start | bytes 786432 | tf_op jit(solution)/shard_map/all_to_all | solution.py:324
  50.8 14.3 %copy-start.1 = (f32[24,1,2,2,192]{4,3,2,1,0:T(2,128)S(1)}, f32[24,1,2,2,192]{4,3,2,1,0:T(2,128)}, u32[]{:S(2)}) copy-start(f32[24,1,2,2,192]{4,3,2,1,0:T(2,128)} %image_ref.3) | copy-start | bytes 221188

commit v3 on v2

--- a/solution.py
+++ b/solution.py
@@ -101,12 +101,21 @@
 
 
 def consistency_kernel(
-    x_ref, sampling_ref, mine, other_hbm, row_hbm, col_hbm, out_ref, other, row_v, col_v, sem
+    place_ref, x_ref, kspace_hbm, maps_hbm, other_hbm, sampling_hbm, row_hbm, col_hbm, out_ref,
+    mine, other, sampling, row, col, sem
 ):
+    core = place_ref[0]
     copies = [
         pltpu.make_async_copy(source, target, sem.at[i])
         for i, (source, target) in enumerate(
-            ((col_hbm, col_v), (row_hbm, row_v), (other_hbm, other))
+            (
+                (maps_hbm.at[core], mine.at[2:4]),
+                (col_hbm, col),
+                (row_hbm, row),
+                (kspace_hbm.at[core], mine.at[0:2]),
+                (sampling_hbm, sampling),
+                (other_hbm, other),
+            )
         )
     ]
     for copy in copies:
@@ -115,58 +124,61 @@
     def dot(left, right):
         return jnp.dot(left, right, preferred_element_type=f32)
 
-    x_real = x_ref[:, 0].astype(f32).reshape(NY, NZ)
-    x_imag = x_ref[:, 1].astype(f32).reshape(NY, NZ)
-    sampled = sampling_ref[...].astype(f32)
-    sum_real = jnp.zeros((NY, NZ), f32)
-    sum_imag = jnp.zeros((NY, NZ), f32)
+    x_real = x_ref[:, 0].astype(f32).reshape(NY, NZ).T
+    x_imag = x_ref[:, 1].astype(f32).reshape(NY, NZ).T
+    sum_real = jnp.zeros((NZ, NY), f32)
+    sum_imag = jnp.zeros((NZ, NY), f32)
     copies[0].wait()
+    copies[1].wait()
     for ref in (mine, other):
         if ref is other:
-            copies[2].wait()
+            copies[5].wait()
         map_real = ref[2].astype(f32)
         map_imag = ref[3].astype(f32)
         w_real = (map_real * x_real - map_imag * x_imag).astype(bf16)
         w_imag = (map_real * x_imag + map_imag * x_real).astype(bf16)
-        h_real = (dot(w_real, col_v[0]) + dot(w_imag, col_v[1])).astype(bf16)
-        h_imag = (dot(w_imag, col_v[0]) - dot(w_real, col_v[1])).astype(bf16)
+        h_real = dot(col[...], jnp.concatenate([w_real, w_imag], 0)).astype(bf16)
+        h_imag = dot(col[...], jnp.concatenate([w_imag, -w_real], 0)).astype(bf16)
         if ref is mine:
-            copies[1].wait()
-        row = row_v[...]
-        s_real = dot(row, jnp.concatenate([h_real, h_imag], 0))
-        s_imag = dot(row, jnp.concatenate([h_imag, -h_real], 0))
+            for copy in copies[2:5]:
+                copy.wait()
+        sampled = sampling[...].astype(f32)
+        s_real = dot(jnp.concatenate([h_real, h_imag], 1), row[...])
+        s_imag = dot(jnp.concatenate([h_imag, -h_real], 1), row[...])
         r_real = (sampled * (s_real - ref[0].astype(f32))).astype(bf16)
         r_imag = (sampled * (s_imag - ref[1].astype(f32))).astype(bf16)
-        b_real = dot(row, jnp.concatenate([r_real, -r_imag], 0)).astype(bf16)
-        b_imag = dot(row, jnp.concatenate([r_imag, r_real], 0)).astype(bf16)
-        o_real = dot(b_real, col_v[0]) - dot(b_imag, col_v[1])
-        o_imag = dot(b_real, col_v[1]) + dot(b_imag, col_v[0])
+        b_real = dot(jnp.concatenate([r_real, -r_imag], 1), row[...]).astype(bf16)
+        b_imag = dot(jnp.concatenate([r_imag, r_real], 1), row[...]).astype(bf16)
+        o_real = dot(col[...], jnp.concatenate([b_real, -b_imag], 0))
+        o_imag = dot(col[...], jnp.concatenate([b_imag, b_real], 0))
         sum_real = sum_real + map_real * o_real + map_imag * o_imag
         sum_imag = sum_imag + map_real * o_imag - map_imag * o_real
-    out_ref[:, 0] = sum_real.reshape(COILS, ROWS, NZ).astype(bf16)
-    out_ref[:, 1] = sum_imag.reshape(COILS, ROWS, NZ).astype(bf16)
-
-
-def consistency(x, sampling, mine, other, row, col):
+    out_ref[:, 0] = sum_real.T.reshape(COILS, ROWS, NZ).astype(bf16)
+    out_ref[:, 1] = sum_imag.T.reshape(COILS, ROWS, NZ).astype(bf16)
+
+
+def consistency(place, x, kspace, maps, other, sampling, row, col):
     vmem = pl.BlockSpec(memory_space=pltpu.VMEM)
-    hbm = pl.BlockSpec(memory_space=pltpu.HBM)
     return pl.pallas_call(
         consistency_kernel,
         out_shape=jax.ShapeDtypeStruct((COILS, 2, ROWS, NZ), bf16),
-        in_specs=[vmem, vmem, vmem, hbm, hbm, hbm],
+        in_specs=[pl.BlockSpec(memory_space=pltpu.SMEM), vmem]
+        + [pl.BlockSpec(memory_space=pl.ANY)] * 6,
         out_specs=vmem,
         scratch_shapes=[
-            pltpu.VMEM((4, NY, NZ), bf16),
-            pltpu.VMEM((NY, 2 * NY), bf16),
-            pltpu.VMEM((2, NZ, NZ), bf16),
-            pltpu.SemaphoreType.DMA((3,)),
+            pltpu.VMEM((4, NZ, NY), bf16),
+            pltpu.VMEM((4, NZ, NY), bf16),
+            pltpu.VMEM((NZ, NY), jnp.int32),
+            pltpu.VMEM((2 * NY, NY), bf16),
+            pltpu.VMEM((NZ, 2 * NZ), bf16),
+            pltpu.SemaphoreType.DMA((6,)),
         ],
-        compiler_params=pltpu.CompilerParams(vmem_limit_bytes=20 << 20),
+        compiler_params=pltpu.CompilerParams(vmem_limit_bytes=52 << 20),
         cost_estimate=pl.CostEstimate(
             flops=4_000_000_000, bytes_accessed=3_000_000, transcendentals=0
         ),
         name="consistency",
-    )(x, sampling, mine, other, row, col)
+    )(place, x, kspace, maps, other, sampling, row, col)
 
 
 def regularizer_kernel(
@@ -284,9 +296,8 @@
 
 
 def body(kspace, sampling, coil_maps, image, filters, thresholds, dc_weight):
-    row_cos, row_sin = np_tables(NY)
-    row = jnp.asarray(np.concatenate([row_cos, row_sin], 1))
-    col = jnp.asarray(np.stack(np_tables(NZ)))
+    row = jnp.asarray(np.concatenate(np_tables(NY), 0))
+    col = jnp.asarray(np.concatenate(np_tables(NZ), 1))
     coil = lax.axis_index("coil")
     core = lax.rem(coil, 2)
     read = lax.axis_index("read")
@@ -295,8 +306,25 @@
     sent, lines, near, far = prepare(place, image)
     gathered = lax.all_to_all(sent, "coil", 0, 0, tiled=True)
 
+    on_chip = [(i, i ^ 1) for i in range(COILS)]
+    measured = kspace[:, 0, 0].transpose(1, 2, 3, 0)
+    maps = coil_maps[:, 0].transpose(1, 2, 3, 0)
+    other = jnp.concatenate(
+        [lax.dynamic_index_in_dim(a, 1 - core, 0, keepdims=False) for a in (measured, maps)], 0
+    )
+
+    respond, spread = np_expansions()
+    taps = filters.reshape(FILTERS, 54)
+    respond = lax.dynamic_index_in_dim(jnp.asarray(respond), read, 0, keepdims=False)
+    spread = lax.dynamic_index_in_dim(jnp.asarray(spread), read, 0, keepdims=False)
+    spread = jnp.einsum("ycl,kc->lyk", spread, taps, preferred_element_type=f32)
+    spread = spread.astype(bf16).reshape(48, PAIR * SITES)
+    levels = jnp.broadcast_to(jnp.tile(thresholds, BAND * 3)[:, None], (BAND * SITES, NZ))
+
+    near, far, other = lax.optimization_barrier((near, far, other))
+    other = lax.ppermute(other, "coil", on_chip)
+
     even = core == 0
-    on_chip = [(i, i ^ 1) for i in range(COILS)]
     next_chip = [(i, i + 1) for i in range(1, COILS - 1, 2)]
     next_chip += [(j, i) for i, j in next_chip]
     near = lax.ppermute(near, "coil", on_chip)
@@ -309,27 +337,17 @@
         pairs = [(i, i ^ flip) for i in range(2 * ECHOES)]
         return lax.ppermute(block, ("echo", "read"), pairs)
 
-    quad = jnp.stack([extended] + [swap(extended, flip) for flip in (1, 8, 9)])
+    quad = jnp.stack([extended] + [swap(extended, flip) for flip in (1, 2, 3)])
     quad = quad.reshape(2, 2, LINES * 4, NZ)
-    blocks = [quad] + [swap(quad, flip) for flip in (2, 4, 6)]
-
-    both = jnp.concatenate(
-        [kspace[:, 0, 0].transpose(1, 2, 0, 3), coil_maps[:, 0].transpose(1, 2, 0, 3)], 1
-    )
-    mine = lax.dynamic_index_in_dim(both, core, 0, keepdims=False)
-    other = lax.ppermute(
-        lax.dynamic_index_in_dim(both, 1 - core, 0, keepdims=False), "coil", on_chip
-    )
-    partial = consistency(gathered, sampling[:, 0], mine, other, row, col)
+    gathered, quad, taps, respond, spread, levels = lax.optimization_barrier(
+        (gathered, quad, taps, respond, spread, levels)
+    )
+    partial = consistency(
+        place, gathered, measured, maps, other, sampling[:, 0].T, row, col
+    )
+    quad, partial = lax.optimization_barrier((quad, partial))
+    blocks = [quad] + [swap(quad, flip) for flip in (4, 8, 12)]
     arrived = lax.all_to_all(partial, "coil", 0, 0, tiled=True)
-
-    respond, spread = np_expansions()
-    taps = filters.reshape(FILTERS, 54)
-    respond = lax.dynamic_index_in_dim(jnp.asarray(respond), read, 0, keepdims=False)
-    spread = lax.dynamic_index_in_dim(jnp.asarray(spread), read, 0, keepdims=False)
-    spread = jnp.einsum("ycl,kc->lyk", spread, taps, preferred_element_type=f32)
-    spread = spread.astype(bf16).reshape(48, PAIR * SITES)
-    levels = jnp.broadcast_to(jnp.tile(thresholds, BAND * 3)[:, None], (BAND * SITES, NZ))
     penalty = regularizer(place, blocks, taps, respond, spread, levels)
     return update(dc_weight, image, arrived, penalty)
 

time: 66.3 us -> 66 us (level)
  waiting for transfers between devices: 12.9 us -> 16.8 us
  local copies, waits for them, and re-layouts: 5.3 us -> 2.58 us
  starting transfers between devices: 31.6 us -> 29.9 us
  Pallas kernels: 13.4 us -> 14.2 us
    ppermute x1, waiting for transfers between devices: 0.01 us -> 4.97 us  [body(): far = lax.ppermute(far, 'coil', next_chip)]
    all_to_all x1, starting transfers between devices: 7.69 us -> 9.98 us  [body(): gathered = lax.all_to_all(sent, 'coil', 0, 0, tiled=True)]
    unnamed x19 -> x20, local copies, waits for them, and re-layouts: 3.08 us -> 0.94 us
    ppermute x6, waiting for transfers between devices: 5.39 us -> 3.98 us  [swap(): return lax.ppermute(block, ('echo', 'read'), pairs)]
    squeeze x1 -> x0, other arithmetic: 1.4 us -> none  [body(): lax.dynamic_index_in_dim(both, 1 - core, 0, keepdims=False)]
    ppermute x1, starting transfers between devices: 4.92 us -> 3.53 us  [body(): far = lax.ppermute(far, 'coil', next_chip)]
    ppermute x1 -> x0, local copies, waits for them, and re-layouts: 1.33 us -> none  [body(): lax.ppermute(lax.dynamic_index_in_dim(both, 1 - core, 0, keepdims=False),...]
    all_to_all x1, starting transfers between devices: 9.77 us -> 8.48 us  [body(): arrived = lax.all_to_all(partial, 'coil', 0, 0, tiled=True)]
  transfers between devices with their start and end apart: 11 -> 11, of which waited for: 3 -> 4; matrix products, arithmetic and copies ran while one was open for 6% -> 4% of each run, Pallas kernels for 17% -> 10%
where the time goes in v3:
time: 66 us; the launch traced here: 65.7 us
  starting transfers between devices  29.9 us (45%)
  waiting for transfers between devices  16.8 us (25%)
  Pallas kernels  14.2 us (22%)
  local copies, waits for them, and re-layouts  2.58 us (4%)
  other arithmetic  1.06 us (2%)
  between operations  0.89 us (1%)
    all_to_all x1, starting transfers between devices, body(): gathered = lax.all_to_all(sent, 'coil', 0, 0, tiled=True)  9.98 us
    all_to_all x1, starting transfers between devices, body(): arrived = lax.all_to_all(partial, 'coil', 0, 0, tiled=True)  8.48 us
    all_to_all x1, waiting for transfers between devices, body(): arrived = lax.all_to_all(partial, 'coil', 0, 0, tiled=True)  7.84 us
    ppermute x6, starting transfers between devices, swap(): return lax.ppermute(block, ('echo', 'read'), pairs)  7.35 us
    pallas_call x1, Pallas kernels, regularizer(): pl.pallas_call(regularizer_kernel, out_shape=jax.ShapeDtypeStruct((2, ROW...  6.67 us
    pallas_call x1, Pallas kernels, consistency(): pl.pallas_call(consistency_kernel, out_shape=jax.ShapeDtypeStruct((COILS,...  5.38 us
    ppermute x1, waiting for transfers between devices, body(): far = lax.ppermute(far, 'coil', next_chip)  4.97 us
    ppermute x6, waiting for transfers between devices, swap(): return lax.ppermute(block, ('echo', 'read'), pairs)  3.98 us
  transfers between devices with their start and end apart: 11, of which 4 were waited for; matrix products, arithmetic and copies ran while one was open for 4% of the time, Pallas kernels for 10%

profile of v3, /device:TPU:1, one launch (start us, length us, event | category | flops | bytes accessed | tf_op | source)
XLA Modules:
  0.0 65.7 jit_solution(6550618126688336017)
XLA Ops:
  0.0 0.1 pad_add_fusion.place_ref
  0.1 0.0 copy-start
  0.1 0.9 %copy-done = f32[24,1,2,2,192]{4,3,2,1,0:T(2,128)S(1)} copy-done((f32[24,1,2,2,192]{4,3,2,1,0:T(2,128)S(1)}, f32[24,1,2,2,192]{4,3,2,1,0:T(2,128)}, u32[]{:S(2)}) %copy-start) | copy-done | bytes 73752
  1.0 0.0 copy-start.5
  1.0 1.4 %prepare.1 = (bf16[16,2,24,192]{3,2,1,0:T(8,128)(2,1)}, bf16[96,192]{1,0:T(8,128)(2,1)S(1)}, bf16[8,192]{1,0:T(8,128)(2,1)S(1)}, bf16[8,192]{1,0:T(8,128)(2,1)S(1)}) custom-call(s32[3]{0:T(128)S(1)} %pad_add_fusion.place_ref, f32[24,1,2,2,192]{4,3,2,1,0:T(2,128)S(1)} %copy-done), custom_call_target="tpu_custom_call" | custom-call | tf_op jit(solution)/shard_map/prepare/pallas_call | solution.py:87
  2.4 10.0 %all-to-all-start = ((bf16[16,2,24,192]{3,2,1,0:T(8,128)(2,1)}), bf16[16,2,24,192]{3,2,1,0:T(8,128)(2,1)S(1)}, u32[]{:S(2)}, u32[]{:S(2)}) async-start(bf16[16,2,24,192]{3,2,1,0:T(8,128)(2,1)} %get-tuple-element.20), calls=%async_computation | async-start | bytes 786432 | tf_op jit(solution)/shard_map/all_to_all | solution.py:307
  12.4 0.0 copy-start.8
  12.4 0.0 copy-start.7
  12.4 1.0 %dynamic-slice_bitcast_fusion.1 = bf16[2,192,384]{2,1,0:T(8,128)(2,1)S(1)} fusion(bf16[384,1,1,2,2,192]{0,5,4,3,2,1:T(8,128)(2,1)} %param.11, s32[]{:T(128)S(6)} %select_n.24), kind=kLoop, calls=%fused_computation.4 | loop fusion | bytes 589828 | tf_op jit(solution)/shard_map/jit(dynamic_index_in_dim)/squeeze | solution.py:313
  13.4 0.0 copy-done.5
  13.5 0.0 copy-start.6
  13.5 0.0 copy-start.9
  13.5 0.9 %pad_maximum_fusion = bf16[4,192,384]{2,1,0:T(8,128)(2,1)} fusion(bf16[2,192,384]{2,1,0:T(8,128)(2,1)S(1)} %dynamic-slice_bitcast_fusion, bf16[2,192,384]{2,1,0:T(8,128)(2,1)S(1)} %dynamic-slice_bitcast_fusion.1), kind=kLoop, calls=%fused_computation.2 | loop fusion | flops 294912 | bytes 1179648 | tf_op jit(solution)/shard_map/concatenate | solution.py:312
  14.4 3.5 %collective-permute-start = (bf16[8,192]{1,0:T(8,128)(2,1)S(1)}, bf16[8,192]{1,0:T(8,128)(2,1)S(1)}, u32[]{:S(2)}, u32[]{:S(2)}) collective-permute-start(bf16[8,192]{1,0:T(8,128)(2,1)S(1)} %get-tuple-element.23), channel_id=1, source_target_pairs={{2,4},{6,8},{10,12},{14,16},{18,20},{22,24},{26,28},{4,2},{8,6},{1... | collective-permute-start | bytes 9224 | tf_op jit(solution)/shard_map/ppermute | solution.py:331
  18.0 0.1 collective-permute-start.1
  18.1 0.5 collective-permute-start.5
  18.6 0.0 copy-done.8
  18.6 0.0 copy-done.7
  18.6 0.2 fusion
  18.8 5.0 %collective-permute-done = bf16[8,192]{1,0:T(8,128)(2,1)S(1)} collective-permute-done((bf16[8,192]{1,0:T(8,128)(2,1)S(1)}, bf16[8,192]{1,0:T(8,128)(2,1)S(1)}, u32[]{:S(2)}, u32[]{:S(2)}) %collective-permute-start) | collective-permute-done | bytes 3104 | tf_op jit(solution)/shard_map/ppermute | solution.py:331
  23.7 0.0 collective-permute-done.1
  23.7 0.0 copy-start.2
  23.8 0.0 copy-start.3
  23.8 0.0 copy-start.4
  23.8 1.4 %collective-permute-start.3 = (bf16[112,192]{1,0:T(8,128)(2,1)S(1)}, bf16[112,192]{1,0:T(8,128)(2,1)S(1)}, u32[]{:S(2)}, u32[]{:S(2)}) collective-permute-start(bf16[112,192]{1,0:T(8,128)(2,1)S(1)} %get-tuple-element.36), channel_id=1, source_target_pairs={{0,32},{1,33},{32,0},{33,1},{64,96},{65,97},{96,64},{97,65},{128,1... | collective-permute-start | bytes 129032 | tf_op jit(solution)/shard_map/ppermute | solution.py:338
  25.2 2.6 %collective-permute-start.2 = (bf16[112,192]{1,0:T(8,128)(2,1)S(1)}, bf16[112,192]{1,0:T(8,128)(2,1)S(1)}, u32[]{:S(2)}, u32[]{:S(2)}) collective-permute-start(bf16[112,192]{1,0:T(8,128)(2,1)S(1)} %get-tuple-element.36), channel_id=1, source_target_pairs={{0,1},{1,0},{32,33},{33,32},{64,65},{65,64},{96,97},{97,96},{128,1... | collective-permute-start | bytes 129032 | tf_op jit(solution)/shard_map/ppermute | solution.py:338
  27.8 0.0 collective-permute-start.4
  27.8 0.0 copy-done.6
  27.8 0.0 copy-done.9
  27.9 0.1 broadcast_in_dim.7
  28.0 0.1 reshape.21.spread_ref
  28.1 0.0 collective-permute-done.3
  28.1 1.9 %collective-permute-done.2 = bf16[112,192]{1,0:T(8,128)(2,1)S(1)} collective-permute-done((bf16[112,192]{1,0:T(8,128)(2,1)S(1)}, bf16[112,192]{1,0:T(8,128)(2,1)S(1)}, u32[]{:S(2)}, u32[]{:S(2)}) %collective-permute-start.2) | collective-permute-done | bytes 43040 | tf_op jit(solution)/shard_map/ppermute | solution.py:338
  30.0 2.1 %collective-permute-done.4 = bf16[112,192]{1,0:T(8,128)(2,1)S(1)} collective-permute-done((bf16[112,192]{1,0:T(8,128)(2,1)S(1)}, bf16[112,192]{1,0:T(8,128)(2,1)S(1)}, u32[]{:S(2)}, u32[]{:S(2)}) %collective-permute-start.4) | collective-permute-done | bytes 43040 | tf_op jit(solution)/shard_map/ppermute | solution.py:338
  32.1 0.1 pad_maximum_fusion.1
  32.1 0.0 all-to-all-done.x_ref
  32.1 0.2 broadcast_in_dim.8.thresholds_ref
  32.3 0.0 collective-permute-done.5.other_hbm
  32.4 0.0 copy-done.2
  32.4 0.0 copy-done.3
  32.4 0.0 copy-done.4
  32.4 5.4 %consistency.1 = bf16[16,2,24,192]{3,2,1,0:T(8,128)(2,1)} custom-call(s32[3]{0:T(128)S(1)} %pad_add_fusion.place_ref, bf16[16,2,24,192]{3,2,1,0:T(8,128)(2,1)S(1)} %all-to-all-done.x_ref, bf16[2,2,192,384]{3,2,1,0:T(8,128)(2,1)S(1)} %bitcast.46, bf16[2,2,192,384]{3,2,1,0:T(8,128)(2,1)} %bitcast.48, bf16[4,192,384]{2,1,0:T(8,128)(2,1)} %collective-permute-done.5.other_hbm, ...), custom_call_target="tpu_custom_call" | custom-call | flops 4000000000 | bytes 3000000 | tf_op jit(solution)/shard_map/consistency/pallas_call | solution.py:162
  37.8 2.6 %collective-permute-start.8 = (bf16[2,2,112,192]{3,2,1,0:T(8,128)(2,1)S(1)}, bf16[2,2,112,192]{3,2,1,0:T(8,128)(2,1)S(1)}, u32[]{:S(2)}, u32[]{:S(2)}) collective-permute-start(bf16[2,2,112,192]{3,2,1,0:T(8,128)(2,1)S(1)} %bitcast.42), channel_id=1, source_target_pairs={{0,192},{1,193},{32,224},{33,225},{64,128},{65,129},{96,160},{97,1... | collective-permute-start | bytes 516104 | tf_op jit(solution)/shard_map/ppermute | solution.py:338
  40.3 0.5 collective-permute-start.7
  40.9 0.3 collective-permute-start.6
  41.8 0.1 copy.16.taps_ref
  41.9 8.5 %all-to-all-start.1 = ((bf16[16,2,24,192]{3,2,1,0:T(8,128)(2,1)}), bf16[16,2,24,192]{3,2,1,0:T(8,128)(2,1)S(1)}, u32[]{:S(2)}, u32[]{:S(2)}) async-start(bf16[16,2,24,192]{3,2,1,0:T(8,128)(2,1)} %consistency.1), calls=%async_computation.1 | async-start | bytes 786432 | tf_op jit(solution)/shard_map/all_to_all | solution.py:350
  50.3 0.0 copy-start.1
  50.4 0.0 collective-permute-done.8.x3_ref
  50.4 0.0 collective-permute-done.7.x2_ref
  50.4 0.0 collective-permute-done.6.x1_ref
  50.4 6.7 %regularizer.1.penalty_ref = f32[2,96,128]{2,1,0:T(8,128)S(1)} custom-call(s32[3]{0:T(128)S(1)} %pad_add_fusion.place_ref, bf16[2,2,112,192]{3,2,1,0:T(8,128)(2,1)S(1)} %bitcast.45, bf16[2,2,112,192]{3,2,1,0:T(8,128)(2,1)S(1)} %collective-permute-done.6.x1_ref, bf16[2,2,112,192]{3,2,1,0:T(8,128)(2,1)S(1)} %collective-permute-done.7.x2_ref, ...), custom_call_target="tpu_custom_call" | custom-call | flops 8999999488 | bytes 2000000 | tf_op jit(solution)/shard_map/regularizer/pallas_call | solution.py:255
  57.1 7.8 %all-to-all-done.1.arrived_ref = bf16[16,2,24,192]{3,2,1,0:T(8,128)(2,1)S(1)} async-done(((bf16[16,2,24,192]{3,2,1,0:T(8,128)(2,1)}), bf16[16,2,24,192]{3,2,1,0:T(8,128)(2,1)S(1)}, u32[]{:S(2)}, u32[]{:S(2)}) %all-to-all-start.1) | async-done | bytes 294944 | tf_op jit(solution)/shard_map/all_to_all | solution.py:350
  64.9 0.0 copy-done.1
  64.9 0.8 %update.1 = f32[24,1,2,2,192]{4,3,2,1,0:T(2,128)} custom-call(f32[1]{0:T(128)S(6)} %copy.19.weight_ref, f32[24,1,2,2,192]{4,3,2,1,0:T(2,128)S(1)} %copy-done.1, bf16[16,2,24,192]{3,2,1,0:T(8,128)(2,1)S(1)} %all-to-all-done.1.arrived_ref, f32[2,96,128]{2,1,0:T(8,128)S(1)} %regularizer.1.penalty_ref), custom_call_target="tpu_custom_call" | custom-call | tf_op jit(solution)/shard_map/update/pallas_call | solution.py:288
  (7 shorter events, 0.1 us)
Async XLA Ops:
  0.1 0.9 %copy-start = (f32[24,1,2,2,192]{4,3,2,1,0:T(2,128)S(1)}, f32[24,1,2,2,192]{4,3,2,1,0:T(2,128)}, u32[]{:S(2)}) copy-start(f32[24,1,2,2,192]{4,3,2,1,0:T(2,128)} %image_ref.3) | copy-start | bytes 221188
  1.0 12.5 %copy-start.5 = (bf16[384,1,2,2,192]{0,4,3,2,1:T(8,128)(2,1)S(1)}, bf16[384,1,2,2,192]{0,4,3,2,1:T(8,128)(2,1)}, u32[]{:S(2)}) copy-start(bf16[384,1,2,2,192]{0,4,3,2,1:T(8,128)(2,1)} %param.13) | copy-start | bytes 1769476
  2.4 29.7 %all-to-all-start = ((bf16[16,2,24,192]{3,2,1,0:T(8,128)(2,1)}), bf16[16,2,24,192]{3,2,1,0:T(8,128)(2,1)S(1)}, u32[]{:S(2)}, u32[]{:S(2)}) async-start(bf16[16,2,24,192]{3,2,1,0:T(8,128)(2,1)} %get-tuple-element.20), calls=%async_computation | async-start | bytes 786432 | tf_op jit(solution)/shard_map/all_to_all | solution.py:307
  12.4 6.2 %copy-start.8 = (bf16[48,3,3,3,2]{0,4,3,2,1:T(2,128)(2,1)S(1)}, bf16[48,3,3,3,2]{0,4,3,2,1:T(2,128)(2,1)}, u32[]{:S(2)}) copy-start(bf16[48,3,3,3,2]{0,4,3,2,1:T(2,128)(2,1)} %param.15) | copy-start | bytes 15556
  12.4 6.2 %copy-start.7 = (bf16[2,6,54,48]{2,3,1,0:T(8,128)(2,1)S(1)}, bf16[2,6,54,48]{2,3,1,0:T(8,128)(2,1)}, u32[]{:S(2)}) copy-start(bf16[2,6,54,48]{2,3,1,0:T(8,128)(2,1)} %constant.47.clone) | copy-start | bytes 186628
  13.5 14.4 %copy-start.6 = (bf16[2,3,54,256]{3,2,1,0:T(8,128)(2,1)S(1)}, bf16[2,3,54,256]{3,2,1,0:T(8,128)(2,1)}, u32[]{:S(2)}) copy-start(bf16[2,3,54,256]{3,2,1,0:T(8,128)(2,1)} %constant.46.clone) | copy-start | bytes 497668
  13.5 14.4 %copy-start.9 = (f32[48]{0:T(128)S(1)}, f32[48]{0:T(128)}, u32[]{:S(2)}) copy-start(f32[48]{0:T(128)} %param.16) | copy-start | bytes 580
  14.4 9.3 %collective-permute-start = (bf16[8,192]{1,0:T(8,128)(2,1)S(1)}, bf16[8,192]{1,0:T(8,128)(2,1)S(1)}, u32[]{:S(2)}, u32[]{:S(2)}) collective-permute-start(bf16[8,192]{1,0:T(8,128)(2,1)S(1)} %get-tuple-element.23), channel_id=1, source_target_pairs={{2,4},{6,8},{10,12},{14,16},{18,20},{22,24},{26,28},{4,2},{8,6},{1... | collective-permute-start | bytes 9224 | tf_op jit(solution)/shard_map/ppermute | solution.py:331
  18.0 5.8 %collective-permute-start.1 = (bf16[8,192]{1,0:T(8,128)(2,1)S(1)}, bf16[8,192]{1,0:T(8,128)(2,1)S(1)}, u32[]{:S(2)}, u32[]{:S(2)}) collective-permute-start(bf16[8,192]{1,0:T(8,128)(2,1)S(1)} %get-tuple-element.24), channel_id=1, source_target_pairs={{0,2},{2,0},{4,6},{6,4},{8,10},{10,8},{12,14},{14,12},{16,18},{18,... | collective-permute-start | bytes 9224 | tf_op jit(solution)/shard_map/ppermute | solution.py:330
  18.1 14.3 %collective-permute-start.5 = (bf16[4,192,384]{2,1,0:T(8,128)(2,1)}, bf16[4,192,384]{2,1,0:T(8,128)(2,1)}, u32[]{:S(2)}, u32[]{:S(2)}) collective-permute-start(bf16[4,192,384]{2,1,0:T(8,128)(2,1)} %pad_maximum_fusion), channel_id=1, source_target_pairs={{0,2},{2,0},{4,6},{6,4},{8,10},{10,8},{12,14},{14,12},{16,18},{18,... | collective-permute-start | bytes 1769480 | tf_op jit(solution)/shard_map/ppermute | solution.py:325
  23.7 8.6 %copy-start.2 = (bf16[384,1,1,2,2,192]{0,5,4,3,2,1:T(8,128)(2,1)S(1)}, bf16[384,1,1,2,2,192]{0,5,4,3,2,1:T(8,128)(2,1)}, u32[]{:S(2)}) copy-start(bf16[384,1,1,2,2,192]{0,5,4,3,2,1:T(8,128)(2,1)} %param.11) | copy-start | bytes 1769476
  23.8 8.6 %copy-start.3 = (s32[384,1,192]{0,2,1:T(8,128)S(1)}, s32[384,1,192]{0,2,1:T(8,128)}, u32[]{:S(2)}) copy-start(s32[384,1,192]{0,2,1:T(8,128)} %param.12) | copy-start | bytes 884740
  23.8 8.6 %copy-start.4 = (bf16[192,384]{1,0:T(8,128)(2,1)S(1)}, bf16[192,384]{1,0:T(8,128)(2,1)}, u32[]{:S(2)}) copy-start(bf16[192,384]{1,0:T(8,128)(2,1)} %constant.45.clone.col_hbm) | copy-start | bytes 442372
  23.8 4.3 %collective-permute-start.3 = (bf16[112,192]{1,0:T(8,128)(2,1)S(1)}, bf16[112,192]{1,0:T(8,128)(2,1)S(1)}, u32[]{:S(2)}, u32[]{:S(2)}) collective-permute-start(bf16[112,192]{1,0:T(8,128)(2,1)S(1)} %get-tuple-element.36), channel_id=1, source_target_pairs={{0,32},{1,33},{32,0},{33,1},{64,96},{65,97},{96,64},{97,65},{128,1... | collective-permute-start | bytes 129032 | tf_op jit(solution)/shard_map/ppermute | solution.py:338
  25.2 4.8 %collective-permute-start.2 = (bf16[112,192]{1,0:T(8,128)(2,1)S(1)}, bf16[112,192]{1,0:T(8,128)(2,1)S(1)}, u32[]{:S(2)}, u32[]{:S(2)}) collective-permute-start(bf16[112,192]{1,0:T(8,128)(2,1)S(1)} %get-tuple-element.36), channel_id=1, source_target_pairs={{0,1},{1,0},{32,33},{33,32},{64,65},{65,64},{96,97},{97,96},{128,1... | collective-permute-start | bytes 129032 | tf_op jit(solution)/shard_map/ppermute | solution.py:338
  27.8 4.2 %collective-permute-start.4 = (bf16[112,192]{1,0:T(8,128)(2,1)S(1)}, bf16[112,192]{1,0:T(8,128)(2,1)S(1)}, u32[]{:S(2)}, u32[]{:S(2)}) collective-permute-start(bf16[112,192]{1,0:T(8,128)(2,1)S(1)} %get-tuple-element.36), channel_id=1, source_target_pairs={{0,33},{1,32},{32,1},{33,0},{64,97},{65,96},{96,65},{97,64},{128,1... | collective-permute-start | bytes 129032 | tf_op jit(solution)/shard_map/ppermute | solution.py:338
  37.8 12.6 %collective-permute-start.8 = (bf16[2,2,112,192]{3,2,1,0:T(8,128)(2,1)S(1)}, bf16[2,2,112,192]{3,2,1,0:T(8,128)(2,1)S(1)}, u32[]{:S(2)}, u32[]{:S(2)}) collective-permute-start(bf16[2,2,112,192]{3,2,1,0:T(8,128)(2,1)S(1)} %bitcast.42), channel_id=1, source_target_pairs={{0,192},{1,193},{32,224},{33,225},{64,128},{65,129},{96,160},{97,1... | collective-permute-start | bytes 516104 | tf_op jit(solution)/shard_map/ppermute | solution.py:338
  40.3 10.0 %collective-permute-start.7 = (bf16[2,2,112,192]{3,2,1,0:T(8,128)(2,1)S(1)}, bf16[2,2,112,192]{3,2,1,0:T(8,128)(2,1)S(1)}, u32[]{:S(2)}, u32[]{:S(2)}) collective-permute-start(bf16[2,2,112,192]{3,2,1,0:T(8,128)(2,1)S(1)} %bitcast.43), channel_id=1, source_target_pairs={{0,128},{1,129},{32,160},{33,161},{64,192},{65,193},{96,224},{97,2... | collective-permute-start | bytes 516104 | tf_op jit(solution)/shard_map/ppermute | solution.py:338
  40.9 9.5 %collective-permute-start.6 = (bf16[2,2,112,192]{3,2,1,0:T(8,128)(2,1)S(1)}, bf16[2,2,112,192]{3,2,1,0:T(8,128)(2,1)S(1)}, u32[]{:S(2)}, u32[]{:S(2)}) collective-permute-start(bf16[2,2,112,192]{3,2,1,0:T(8,128)(2,1)S(1)} %bitcast.44), channel_id=1, source_target_pairs={{0,64},{1,65},{32,96},{33,97},{64,0},{65,1},{96,32},{97,33},{128,1... | collective-permute-start | bytes 516104 | tf_op jit(solution)/shard_map/ppermute | solution.py:338
  41.9 23.0 %all-to-all-start.1 = ((bf16[16,2,24,192]{3,2,1,0:T(8,128)(2,1)}), bf16[16,2,24,192]{3,2,1,0:T(8,128)(2,1)S(1)}, u32[]{:S(2)}, u32[]{:S(2)}) async-start(bf16[16,2,24,192]{3,2,1,0:T(8,128)(2,1)} %consistency.1), calls=%async_computation.1 | async-start | bytes 786432 | tf_op jit(solution)/shard_map/all_to_all | solution.py:350
  50.3 14.6 %copy-start.1 = (f32[24,1,2,2,192]{4,3,2,1,0:T(2,128)S(1)}, f32[24,1,2,2,192]{4,3,2,1,0:T(2,128)}, u32[]{:S(2)}) copy-start(f32[24,1,2,2,192]{4,3,2,1,0:T(2,128)} %image_ref.3) | copy-start | bytes 221188

commit v4 on v3

--- a/solution.py
+++ b/solution.py
@@ -101,7 +101,7 @@
 
 
 def consistency_kernel(
-    place_ref, x_ref, kspace_hbm, maps_hbm, other_hbm, sampling_hbm, row_hbm, col_hbm, out_ref,
+    place_ref, x_ref, kspace_hbm, maps_hbm, other_k_hbm, other_m_hbm, sampling_hbm, row_hbm, col_hbm, out_ref,
     mine, other, sampling, row, col, sem
 ):
     core = place_ref[0]
@@ -114,7 +114,8 @@
                 (row_hbm, row),
                 (kspace_hbm.at[core], mine.at[0:2]),
                 (sampling_hbm, sampling),
-                (other_hbm, other),
+                (other_m_hbm, other.at[2:4]),
+                (other_k_hbm, other.at[0:2]),
             )
         )
     ]
@@ -133,6 +134,7 @@
     for ref in (mine, other):
         if ref is other:
             copies[5].wait()
+            copies[6].wait()
         map_real = ref[2].astype(f32)
         map_imag = ref[3].astype(f32)
         w_real = (map_real * x_real - map_imag * x_imag).astype(bf16)
@@ -157,13 +159,13 @@
     out_ref[:, 1] = sum_imag.T.reshape(COILS, ROWS, NZ).astype(bf16)
 
 
-def consistency(place, x, kspace, maps, other, sampling, row, col):
+def consistency(place, x, kspace, maps, other_k, other_m, sampling, row, col):
     vmem = pl.BlockSpec(memory_space=pltpu.VMEM)
     return pl.pallas_call(
         consistency_kernel,
         out_shape=jax.ShapeDtypeStruct((COILS, 2, ROWS, NZ), bf16),
         in_specs=[pl.BlockSpec(memory_space=pltpu.SMEM), vmem]
-        + [pl.BlockSpec(memory_space=pl.ANY)] * 6,
+        + [pl.BlockSpec(memory_space=pl.ANY)] * 7,
         out_specs=vmem,
         scratch_shapes=[
             pltpu.VMEM((4, NZ, NY), bf16),
@@ -171,14 +173,14 @@
             pltpu.VMEM((NZ, NY), jnp.int32),
             pltpu.VMEM((2 * NY, NY), bf16),
             pltpu.VMEM((NZ, 2 * NZ), bf16),
-            pltpu.SemaphoreType.DMA((6,)),
+            pltpu.SemaphoreType.DMA((7,)),
         ],
         compiler_params=pltpu.CompilerParams(vmem_limit_bytes=52 << 20),
         cost_estimate=pl.CostEstimate(
             flops=4_000_000_000, bytes_accessed=3_000_000, transcendentals=0
         ),
         name="consistency",
-    )(place, x, kspace, maps, other, sampling, row, col)
+    )(place, x, kspace, maps, other_k, other_m, sampling, row, col)
 
 
 def regularizer_kernel(
@@ -211,6 +213,7 @@
         shifted_ref[e, 2] = jnp.concatenate([x[:, :, 1:], zero], 2).astype(bf16)
     total_ref[...] = jnp.zeros_like(total_ref)
     spread = spread_ref[...]
+    levels = jnp.concatenate([thresholds_ref[...]] * (BAND * 3), 0)
 
     for base, first in zip(BASES, FIRST):
         weights = weights_ref[first * SITES :, : 3 * 2 * WINDOW * 4]
@@ -222,7 +225,7 @@
             square = response * response
             energy = square if energy is None else energy + square
         magnitude = jnp.sqrt(energy)
-        factor = magnitude / (magnitude + thresholds_ref[first * SITES :, :])
+        factor = magnitude / (magnitude + levels[first * SITES :, :])
         shrunk = response * factor
         if base == 0:
             top = shrunk[:SITES] * place_ref[1].astype(f32)
@@ -306,32 +309,34 @@
     sent, lines, near, far = prepare(place, image)
     gathered = lax.all_to_all(sent, "coil", 0, 0, tiled=True)
 
-    on_chip = [(i, i ^ 1) for i in range(COILS)]
-    measured = kspace[:, 0, 0].transpose(1, 2, 3, 0)
-    maps = coil_maps[:, 0].transpose(1, 2, 3, 0)
-    other = jnp.concatenate(
-        [lax.dynamic_index_in_dim(a, 1 - core, 0, keepdims=False) for a in (measured, maps)], 0
-    )
-
     respond, spread = np_expansions()
     taps = filters.reshape(FILTERS, 54)
     respond = lax.dynamic_index_in_dim(jnp.asarray(respond), read, 0, keepdims=False)
     spread = lax.dynamic_index_in_dim(jnp.asarray(spread), read, 0, keepdims=False)
     spread = jnp.einsum("ycl,kc->lyk", spread, taps, preferred_element_type=f32)
     spread = spread.astype(bf16).reshape(48, PAIR * SITES)
-    levels = jnp.broadcast_to(jnp.tile(thresholds, BAND * 3)[:, None], (BAND * SITES, NZ))
-
-    near, far, other = lax.optimization_barrier((near, far, other))
-    other = lax.ppermute(other, "coil", on_chip)
+    levels = jnp.broadcast_to(thresholds[:, None], (FILTERS, NZ))
 
     even = core == 0
+    on_chip = [(i, i ^ 1) for i in range(COILS)]
     next_chip = [(i, i + 1) for i in range(1, COILS - 1, 2)]
     next_chip += [(j, i) for i, j in next_chip]
     near = lax.ppermute(near, "coil", on_chip)
     far = lax.ppermute(far, "coil", next_chip)
+
+    measured = kspace[:, 0, 0].transpose(1, 2, 3, 0)
+    maps = coil_maps[:, 0].transpose(1, 2, 3, 0)
+    own_k, own_m = measured, maps
     above = jnp.where(even, far, near)
     below = jnp.where(even, near, far)
     extended = jnp.concatenate([above, lines, below], 0)
+    extended, own_k, own_m = lax.optimization_barrier((extended, own_k, own_m))
+    other_k = lax.ppermute(
+        lax.dynamic_index_in_dim(own_k, 1 - core, 0, keepdims=False), "coil", on_chip
+    )
+    other_m = lax.ppermute(
+        lax.dynamic_index_in_dim(own_m, 1 - core, 0, keepdims=False), "coil", on_chip
+    )
 
     def swap(block, flip):
         pairs = [(i, i ^ flip) for i in range(2 * ECHOES)]
@@ -339,14 +344,13 @@
 
     quad = jnp.stack([extended] + [swap(extended, flip) for flip in (1, 2, 3)])
     quad = quad.reshape(2, 2, LINES * 4, NZ)
-    gathered, quad, taps, respond, spread, levels = lax.optimization_barrier(
-        (gathered, quad, taps, respond, spread, levels)
+    blocks = [quad] + [swap(quad, flip) for flip in (4, 8, 12)]
+    gathered, taps, respond, spread, levels = lax.optimization_barrier(
+        (gathered, taps, respond, spread, levels)
     )
     partial = consistency(
-        place, gathered, measured, maps, other, sampling[:, 0].T, row, col
-    )
-    quad, partial = lax.optimization_barrier((quad, partial))
-    blocks = [quad] + [swap(quad, flip) for flip in (4, 8, 12)]
+        place, gathered, measured, maps, other_k, other_m, sampling[:, 0].T, row, col
+    )
     arrived = lax.all_to_all(partial, "coil", 0, 0, tiled=True)
     penalty = regularizer(place, blocks, taps, respond, spread, levels)
     return update(dc_weight, image, arrived, penalty)

time: 66 us -> 58.5 us (0.89)
  waiting for transfers between devices: 16.8 us -> 12.8 us
  starting transfers between devices: 29.9 us -> 28.4 us
  local copies, waits for them, and re-layouts: 2.58 us -> 1.53 us
  other arithmetic: 1.06 us -> 0.15 us
    ppermute x1, waiting for transfers between devices: 4.97 us -> 0.01 us  [body(): far = lax.ppermute(far, 'coil', next_chip)]
    all_to_all x1, waiting for transfers between devices: 0.01 us -> 2.24 us  [body(): gathered = lax.all_to_all(sent, 'coil', 0, 0, tiled=True)]
    all_to_all x1, starting transfers between devices: 9.98 us -> 8.19 us  [body(): gathered = lax.all_to_all(sent, 'coil', 0, 0, tiled=True)]
    all_to_all x1, starting transfers between devices: 8.48 us -> 7.05 us  [body(): arrived = lax.all_to_all(partial, 'coil', 0, 0, tiled=True)]
    ppermute x1, starting transfers between devices: 3.53 us -> 4.92 us  [body(): far = lax.ppermute(far, 'coil', next_chip)]
    ppermute x6, waiting for transfers between devices: 3.98 us -> 2.75 us  [swap(): return lax.ppermute(block, ('echo', 'read'), pairs)]
    squeeze x2, local copies, waits for them, and re-layouts: 1.08 us -> 0.07 us  [the longest x1 0.04 us: body(): lax.dynamic_index_in_dim(own_m, 1 - core, 0, keepdims=False)]
    concatenate x1, other arithmetic: 0.9 us -> 0.01 us  [body(): extended = jnp.concatenate([above, lines, below], 0)]
  transfers between devices with their start and end apart: 11 -> 12, of which waited for: 4 -> 4; matrix products, arithmetic and copies ran while one was open for 4% -> 1% of each run, Pallas kernels for 10% -> 21%
where the time goes in v4:
time: 58.5 us; the launch traced here: 58.2 us
  starting transfers between devices  28.4 us (49%)
  Pallas kernels  14.3 us (24%)
  waiting for transfers between devices  12.8 us (22%)
  local copies, waits for them, and re-layouts  1.53 us (3%)
  between operations  0.86 us (1%)
    all_to_all x1, starting transfers between devices, body(): gathered = lax.all_to_all(sent, 'coil', 0, 0, tiled=True)  8.19 us
    all_to_all x1, waiting for transfers between devices, body(): arrived = lax.all_to_all(partial, 'coil', 0, 0, tiled=True)  7.81 us
    ppermute x6, starting transfers between devices, swap(): return lax.ppermute(block, ('echo', 'read'), pairs)  7.44 us
    all_to_all x1, starting transfers between devices, body(): arrived = lax.all_to_all(partial, 'coil', 0, 0, tiled=True)  7.05 us
    pallas_call x1, Pallas kernels, regularizer(): pl.pallas_call(regularizer_kernel, out_shape=jax.ShapeDtypeStruct((2, ROW...  6.7 us
    pallas_call x1, Pallas kernels, consistency(): pl.pallas_call(consistency_kernel, out_shape=jax.ShapeDtypeStruct((COILS,...  5.4 us
    ppermute x1, starting transfers between devices, body(): far = lax.ppermute(far, 'coil', next_chip)  4.92 us
    ppermute x6, waiting for transfers between devices, swap(): return lax.ppermute(block, ('echo', 'read'), pairs)  2.75 us
  transfers between devices with their start and end apart: 12, of which 4 were waited for; matrix products, arithmetic and copies ran while one was open for 1% of the time, Pallas kernels for 21%

profile of v4, /device:TPU:1, one launch (start us, length us, event | category | flops | bytes accessed | tf_op | source)
XLA Modules:
  0.0 58.2 jit_solution(10791059011610791048)
XLA Ops:
  0.0 0.1 pad_add_fusion.place_ref
  0.1 0.0 copy-start
  0.1 0.9 %copy-done = f32[24,1,2,2,192]{4,3,2,1,0:T(2,128)S(1)} copy-done((f32[24,1,2,2,192]{4,3,2,1,0:T(2,128)S(1)}, f32[24,1,2,2,192]{4,3,2,1,0:T(2,128)}, u32[]{:S(2)}) %copy-start) | copy-done | bytes 73752
  1.0 0.0 copy-start.5
  1.0 1.4 %prepare.1 = (bf16[16,2,24,192]{3,2,1,0:T(8,128)(2,1)}, bf16[96,192]{1,0:T(8,128)(2,1)S(1)}, bf16[8,192]{1,0:T(8,128)(2,1)S(1)}, bf16[8,192]{1,0:T(8,128)(2,1)S(1)}) custom-call(s32[3]{0:T(128)S(1)} %pad_add_fusion.place_ref, f32[24,1,2,2,192]{4,3,2,1,0:T(2,128)S(1)} %copy-done), custom_call_target="tpu_custom_call" | custom-call | tf_op jit(solution)/shard_map/prepare/pallas_call | solution.py:87
  2.4 4.9 %collective-permute-start = (bf16[8,192]{1,0:T(8,128)(2,1)S(1)}, bf16[8,192]{1,0:T(8,128)(2,1)S(1)}, u32[]{:S(2)}, u32[]{:S(2)}) collective-permute-start(bf16[8,192]{1,0:T(8,128)(2,1)S(1)} %get-tuple-element.19), channel_id=1, source_target_pairs={{2,4},{6,8},{10,12},{14,16},{18,20},{22,24},{26,28},{4,2},{8,6},{1... | collective-permute-start | bytes 9224 | tf_op jit(solution)/shard_map/ppermute | solution.py:325
  7.3 0.1 collective-permute-start.1
  7.4 0.0 copy-start.8
  7.4 0.0 copy-start.4
  7.5 8.2 %all-to-all-start = ((bf16[16,2,24,192]{3,2,1,0:T(8,128)(2,1)}), bf16[16,2,24,192]{3,2,1,0:T(8,128)(2,1)S(1)}, u32[]{:S(2)}, u32[]{:S(2)}) async-start(bf16[16,2,24,192]{3,2,1,0:T(8,128)(2,1)} %get-tuple-element.17), calls=%async_computation | async-start | bytes 786432 | tf_op jit(solution)/shard_map/all_to_all | solution.py:310
  15.6 0.0 copy-done.8
  15.7 0.0 collective-permute-done
  15.7 0.0 collective-permute-done.1
  15.7 0.0 copy-done.5
  15.8 0.0 copy-start.7
  15.8 0.2 collective-permute-start.3
  16.0 0.0 copy-done.4
  16.0 0.0 copy-start.6
  16.0 0.5 collective-permute-start.2
  16.5 0.2 copy-done.7
  16.7 0.1 fusion
  16.9 2.9 %collective-permute-start.6 = (bf16[112,192]{1,0:T(8,128)(2,1)S(1)}, bf16[112,192]{1,0:T(8,128)(2,1)S(1)}, u32[]{:S(2)}, u32[]{:S(2)}) collective-permute-start(bf16[112,192]{1,0:T(8,128)(2,1)S(1)} %pad_maximum_fusion.1), channel_id=1, source_target_pairs={{0,33},{1,32},{32,1},{33,0},{64,97},{65,96},{96,65},{97,64},{128,1... | collective-permute-start | bytes 129032 | tf_op jit(solution)/shard_map/ppermute | solution.py:343
  19.7 0.0 collective-permute-start.5
  19.7 1.3 %collective-permute-start.4 = (bf16[112,192]{1,0:T(8,128)(2,1)S(1)}, bf16[112,192]{1,0:T(8,128)(2,1)S(1)}, u32[]{:S(2)}, u32[]{:S(2)}) collective-permute-start(bf16[112,192]{1,0:T(8,128)(2,1)S(1)} %pad_maximum_fusion.1), channel_id=1, source_target_pairs={{0,1},{1,0},{32,33},{33,32},{64,65},{65,64},{96,97},{97,96},{128,1... | collective-permute-start | bytes 129032 | tf_op jit(solution)/shard_map/ppermute | solution.py:343
  21.0 0.0 copy-done.6
  21.7 0.0 copy-start.2
  21.7 0.1 reshape.11.spread_ref
  21.8 0.0 collective-permute-done.6
  21.8 1.2 %collective-permute-done.5 = bf16[112,192]{1,0:T(8,128)(2,1)S(1)} collective-permute-done((bf16[112,192]{1,0:T(8,128)(2,1)S(1)}, bf16[112,192]{1,0:T(8,128)(2,1)S(1)}, u32[]{:S(2)}, u32[]{:S(2)}) %collective-permute-start.5) | collective-permute-done | bytes 43040 | tf_op jit(solution)/shard_map/ppermute | solution.py:343
  23.0 1.5 %collective-permute-done.4 = bf16[112,192]{1,0:T(8,128)(2,1)S(1)} collective-permute-done((bf16[112,192]{1,0:T(8,128)(2,1)S(1)}, bf16[112,192]{1,0:T(8,128)(2,1)S(1)}, u32[]{:S(2)}, u32[]{:S(2)}) %collective-permute-start.4) | collective-permute-done | bytes 43040 | tf_op jit(solution)/shard_map/ppermute | solution.py:343
  24.5 0.0 copy-start.3
  24.5 0.1 pad_maximum_fusion
  24.6 0.0 copy-start.9
  24.6 2.6 %collective-permute-start.9 = (bf16[2,2,112,192]{3,2,1,0:T(8,128)(2,1)S(1)}, bf16[2,2,112,192]{3,2,1,0:T(8,128)(2,1)S(1)}, u32[]{:S(2)}, u32[]{:S(2)}) collective-permute-start(bf16[2,2,112,192]{3,2,1,0:T(8,128)(2,1)S(1)} %bitcast.33), channel_id=1, source_target_pairs={{0,192},{1,193},{32,224},{33,225},{64,128},{65,129},{96,160},{97,1... | collective-permute-start | bytes 516104 | tf_op jit(solution)/shard_map/ppermute | solution.py:343
  27.2 0.5 collective-permute-start.8
  27.7 0.3 collective-permute-start.7
  28.0 2.2 %all-to-all-done.x_ref = bf16[16,2,24,192]{3,2,1,0:T(8,128)(2,1)S(1)} async-done(((bf16[16,2,24,192]{3,2,1,0:T(8,128)(2,1)}), bf16[16,2,24,192]{3,2,1,0:T(8,128)(2,1)S(1)}, u32[]{:S(2)}, u32[]{:S(2)}) %all-to-all-start) | async-done | bytes 294944 | tf_op jit(solution)/shard_map/all_to_all | solution.py:310
  30.2 0.0 copy-done.9
  30.2 0.1 broadcast_in_dim.2.thresholds_ref
  30.3 0.0 collective-permute-done.3.other_m_hbm
  30.3 0.0 collective-permute-done.2.other_k_hbm
  30.3 0.0 copy-done.2
  30.3 0.0 copy-done.3
  30.3 5.4 %consistency.1 = bf16[16,2,24,192]{3,2,1,0:T(8,128)(2,1)} custom-call(s32[3]{0:T(128)S(1)} %pad_add_fusion.place_ref, bf16[16,2,24,192]{3,2,1,0:T(8,128)(2,1)S(1)} %all-to-all-done.x_ref, bf16[2,2,192,384]{3,2,1,0:T(8,128)(2,1)} %bitcast.39, bf16[2,2,192,384]{3,2,1,0:T(8,128)(2,1)} %bitcast.41, bf16[2,192,384]{2,1,0:T(8,128)(2,1)S(1)} %collective-permute-done.2.other_k_hbm, ...), custom_call_target="tpu_custom_call" | custom-call | flops 4000000000 | bytes 3000000 | tf_op jit(solution)/shard_map/consistency/pallas_call | solution.py:164
  35.7 0.1 copy.16.taps_ref
  35.8 7.1 %all-to-all-start.1 = ((bf16[16,2,24,192]{3,2,1,0:T(8,128)(2,1)}), bf16[16,2,24,192]{3,2,1,0:T(8,128)(2,1)S(1)}, u32[]{:S(2)}, u32[]{:S(2)}) async-start(bf16[16,2,24,192]{3,2,1,0:T(8,128)(2,1)} %consistency.1), calls=%async_computation.1 | async-start | bytes 786432 | tf_op jit(solution)/shard_map/all_to_all | solution.py:354
  42.9 0.0 copy-start.1
  42.9 0.0 collective-permute-done.9.x3_ref
  42.9 0.0 collective-permute-done.8.x2_ref
  42.9 0.0 collective-permute-done.7.x1_ref
  42.9 6.7 %regularizer.1.penalty_ref = f32[2,96,128]{2,1,0:T(8,128)S(1)} custom-call(s32[3]{0:T(128)S(1)} %pad_add_fusion.place_ref, bf16[2,2,112,192]{3,2,1,0:T(8,128)(2,1)S(1)} %bitcast.36, bf16[2,2,112,192]{3,2,1,0:T(8,128)(2,1)S(1)} %collective-permute-done.7.x1_ref, bf16[2,2,112,192]{3,2,1,0:T(8,128)(2,1)S(1)} %collective-permute-done.8.x2_ref, ...), custom_call_target="tpu_custom_call" | custom-call | flops 8999999488 | bytes 2000000 | tf_op jit(solution)/shard_map/regularizer/pallas_call | solution.py:258
  49.6 7.8 %all-to-all-done.1.arrived_ref = bf16[16,2,24,192]{3,2,1,0:T(8,128)(2,1)S(1)} async-done(((bf16[16,2,24,192]{3,2,1,0:T(8,128)(2,1)}), bf16[16,2,24,192]{3,2,1,0:T(8,128)(2,1)S(1)}, u32[]{:S(2)}, u32[]{:S(2)}) %all-to-all-start.1) | async-done | bytes 294944 | tf_op jit(solution)/shard_map/all_to_all | solution.py:354
  57.4 0.0 copy-done.1
  57.4 0.8 %update.1 = f32[24,1,2,2,192]{4,3,2,1,0:T(2,128)} custom-call(f32[1]{0:T(128)S(6)} %copy.19.weight_ref, f32[24,1,2,2,192]{4,3,2,1,0:T(2,128)S(1)} %copy-done.1, bf16[16,2,24,192]{3,2,1,0:T(8,128)(2,1)S(1)} %all-to-all-done.1.arrived_ref, f32[2,96,128]{2,1,0:T(8,128)S(1)} %regularizer.1.penalty_ref), custom_call_target="tpu_custom_call" | custom-call | tf_op jit(solution)/shard_map/update/pallas_call | solution.py:291
  (7 shorter events, 0.2 us)
Async XLA Ops:
  0.1 0.9 %copy-start = (f32[24,1,2,2,192]{4,3,2,1,0:T(2,128)S(1)}, f32[24,1,2,2,192]{4,3,2,1,0:T(2,128)}, u32[]{:S(2)}) copy-start(f32[24,1,2,2,192]{4,3,2,1,0:T(2,128)} %image_ref.3) | copy-start | bytes 221188
  1.0 14.8 %copy-start.5 = (bf16[384,1,2,2,192]{0,4,3,2,1:T(8,128)(2,1)S(1)}, bf16[384,1,2,2,192]{0,4,3,2,1:T(8,128)(2,1)}, u32[]{:S(2)}) copy-start(bf16[384,1,2,2,192]{0,4,3,2,1:T(8,128)(2,1)} %param.13) | copy-start | bytes 1769476
  2.4 13.3 %collective-permute-start = (bf16[8,192]{1,0:T(8,128)(2,1)S(1)}, bf16[8,192]{1,0:T(8,128)(2,1)S(1)}, u32[]{:S(2)}, u32[]{:S(2)}) collective-permute-start(bf16[8,192]{1,0:T(8,128)(2,1)S(1)} %get-tuple-element.19), channel_id=1, source_target_pairs={{2,4},{6,8},{10,12},{14,16},{18,20},{22,24},{26,28},{4,2},{8,6},{1... | collective-permute-start | bytes 9224 | tf_op jit(solution)/shard_map/ppermute | solution.py:325
  7.3 8.4 %collective-permute-start.1 = (bf16[8,192]{1,0:T(8,128)(2,1)S(1)}, bf16[8,192]{1,0:T(8,128)(2,1)S(1)}, u32[]{:S(2)}, u32[]{:S(2)}) collective-permute-start(bf16[8,192]{1,0:T(8,128)(2,1)S(1)} %get-tuple-element.20), channel_id=1, source_target_pairs={{0,2},{2,0},{4,6},{6,4},{8,10},{10,8},{12,14},{14,12},{16,18},{18,... | collective-permute-start | bytes 9224 | tf_op jit(solution)/shard_map/ppermute | solution.py:324
  7.4 8.2 %copy-start.8 = (bf16[48,3,3,3,2]{0,4,3,2,1:T(2,128)(2,1)S(1)}, bf16[48,3,3,3,2]{0,4,3,2,1:T(2,128)(2,1)}, u32[]{:S(2)}) copy-start(bf16[48,3,3,3,2]{0,4,3,2,1:T(2,128)(2,1)} %param.15) | copy-start | bytes 15556
  7.4 8.6 %copy-start.4 = (bf16[384,1,1,2,2,192]{0,5,4,3,2,1:T(8,128)(2,1)S(1)}, bf16[384,1,1,2,2,192]{0,5,4,3,2,1:T(8,128)(2,1)}, u32[]{:S(2)}) copy-start(bf16[384,1,1,2,2,192]{0,5,4,3,2,1:T(8,128)(2,1)} %param.11) | copy-start | bytes 1769476
  7.5 22.7 %all-to-all-start = ((bf16[16,2,24,192]{3,2,1,0:T(8,128)(2,1)}), bf16[16,2,24,192]{3,2,1,0:T(8,128)(2,1)S(1)}, u32[]{:S(2)}, u32[]{:S(2)}) async-start(bf16[16,2,24,192]{3,2,1,0:T(8,128)(2,1)} %get-tuple-element.17), calls=%async_computation | async-start | bytes 786432 | tf_op jit(solution)/shard_map/all_to_all | solution.py:310
  15.8 0.9 %copy-start.7 = (bf16[2,6,54,48]{2,3,1,0:T(8,128)(2,1)S(1)}, bf16[2,6,54,48]{2,3,1,0:T(8,128)(2,1)}, u32[]{:S(2)}) copy-start(bf16[2,6,54,48]{2,3,1,0:T(8,128)(2,1)} %constant.45.clone) | copy-start | bytes 186628
  15.8 14.5 %collective-permute-start.3 = (bf16[2,192,384]{2,1,0:T(8,128)(2,1)S(1)}, bf16[2,192,384]{2,1,0:T(8,128)(2,1)S(1)}, u32[]{:S(2)}, u32[]{:S(2)}) collective-permute-start(bf16[2,192,384]{2,1,0:T(8,128)(2,1)S(1)} %dynamic-slice_bitcast_fusion), channel_id=1, source_target_pairs={{0,2},{2,0},{4,6},{6,4},{8,10},{10,8},{12,14},{14,12},{16,18},{18,... | collective-permute-start | bytes 884744 | tf_op jit(solution)/shard_map/ppermute | solution.py:337
  16.0 5.0 %copy-start.6 = (bf16[2,3,54,256]{3,2,1,0:T(8,128)(2,1)S(1)}, bf16[2,3,54,256]{3,2,1,0:T(8,128)(2,1)}, u32[]{:S(2)}) copy-start(bf16[2,3,54,256]{3,2,1,0:T(8,128)(2,1)} %constant.44.clone) | copy-start | bytes 497668
  16.0 14.2 %collective-permute-start.2 = (bf16[2,192,384]{2,1,0:T(8,128)(2,1)S(1)}, bf16[2,192,384]{2,1,0:T(8,128)(2,1)S(1)}, u32[]{:S(2)}, u32[]{:S(2)}) collective-permute-start(bf16[2,192,384]{2,1,0:T(8,128)(2,1)S(1)} %dynamic-slice_bitcast_fusion.1), channel_id=1, source_target_pairs={{0,2},{2,0},{4,6},{6,4},{8,10},{10,8},{12,14},{14,12},{16,18},{18,... | collective-permute-start | bytes 884744 | tf_op jit(solution)/shard_map/ppermute | solution.py:334
  16.9 4.9 %collective-permute-start.6 = (bf16[112,192]{1,0:T(8,128)(2,1)S(1)}, bf16[112,192]{1,0:T(8,128)(2,1)S(1)}, u32[]{:S(2)}, u32[]{:S(2)}) collective-permute-start(bf16[112,192]{1,0:T(8,128)(2,1)S(1)} %pad_maximum_fusion.1), channel_id=1, source_target_pairs={{0,33},{1,32},{32,1},{33,0},{64,97},{65,96},{96,65},{97,64},{128,1... | collective-permute-start | bytes 129032 | tf_op jit(solution)/shard_map/ppermute | solution.py:343
  19.7 3.3 %collective-permute-start.5 = (bf16[112,192]{1,0:T(8,128)(2,1)S(1)}, bf16[112,192]{1,0:T(8,128)(2,1)S(1)}, u32[]{:S(2)}, u32[]{:S(2)}) collective-permute-start(bf16[112,192]{1,0:T(8,128)(2,1)S(1)} %pad_maximum_fusion.1), channel_id=1, source_target_pairs={{0,32},{1,33},{32,0},{33,1},{64,96},{65,97},{96,64},{97,65},{128,1... | collective-permute-start | bytes 129032 | tf_op jit(solution)/shard_map/ppermute | solution.py:343
  19.7 4.8 %collective-permute-start.4 = (bf16[112,192]{1,0:T(8,128)(2,1)S(1)}, bf16[112,192]{1,0:T(8,128)(2,1)S(1)}, u32[]{:S(2)}, u32[]{:S(2)}) collective-permute-start(bf16[112,192]{1,0:T(8,128)(2,1)S(1)} %pad_maximum_fusion.1), channel_id=1, source_target_pairs={{0,1},{1,0},{32,33},{33,32},{64,65},{65,64},{96,97},{97,96},{128,1... | collective-permute-start | bytes 129032 | tf_op jit(solution)/shard_map/ppermute | solution.py:343
  21.7 8.6 %copy-start.2 = (s32[384,1,192]{0,2,1:T(8,128)S(1)}, s32[384,1,192]{0,2,1:T(8,128)}, u32[]{:S(2)}) copy-start(s32[384,1,192]{0,2,1:T(8,128)} %param.12) | copy-start | bytes 884740
  24.5 5.8 %copy-start.3 = (bf16[192,384]{1,0:T(8,128)(2,1)S(1)}, bf16[192,384]{1,0:T(8,128)(2,1)}, u32[]{:S(2)}) copy-start(bf16[192,384]{1,0:T(8,128)(2,1)} %constant.43.clone.col_hbm) | copy-start | bytes 442372
  24.6 5.6 %copy-start.9 = (f32[48]{0:T(128)S(1)}, f32[48]{0:T(128)}, u32[]{:S(2)}) copy-start(f32[48]{0:T(128)} %param.16) | copy-start | bytes 580
  24.6 18.3 %collective-permute-start.9 = (bf16[2,2,112,192]{3,2,1,0:T(8,128)(2,1)S(1)}, bf16[2,2,112,192]{3,2,1,0:T(8,128)(2,1)S(1)}, u32[]{:S(2)}, u32[]{:S(2)}) collective-permute-start(bf16[2,2,112,192]{3,2,1,0:T(8,128)(2,1)S(1)} %bitcast.33), channel_id=1, source_target_pairs={{0,192},{1,193},{32,224},{33,225},{64,128},{65,129},{96,160},{97,1... | collective-permute-start | bytes 516104 | tf_op jit(solution)/shard_map/ppermute | solution.py:343
  27.2 15.7 %collective-permute-start.8 = (bf16[2,2,112,192]{3,2,1,0:T(8,128)(2,1)S(1)}, bf16[2,2,112,192]{3,2,1,0:T(8,128)(2,1)S(1)}, u32[]{:S(2)}, u32[]{:S(2)}) collective-permute-start(bf16[2,2,112,192]{3,2,1,0:T(8,128)(2,1)S(1)} %bitcast.34), channel_id=1, source_target_pairs={{0,128},{1,129},{32,160},{33,161},{64,192},{65,193},{96,224},{97,2... | collective-permute-start | bytes 516104 | tf_op jit(solution)/shard_map/ppermute | solution.py:343
  27.7 15.2 %collective-permute-start.7 = (bf16[2,2,112,192]{3,2,1,0:T(8,128)(2,1)S(1)}, bf16[2,2,112,192]{3,2,1,0:T(8,128)(2,1)S(1)}, u32[]{:S(2)}, u32[]{:S(2)}) collective-permute-start(bf16[2,2,112,192]{3,2,1,0:T(8,128)(2,1)S(1)} %bitcast.35), channel_id=1, source_target_pairs={{0,64},{1,65},{32,96},{33,97},{64,0},{65,1},{96,32},{97,33},{128,1... | collective-permute-start | bytes 516104 | tf_op jit(solution)/shard_map/ppermute | solution.py:343
  35.8 21.6 %all-to-all-start.1 = ((bf16[16,2,24,192]{3,2,1,0:T(8,128)(2,1)}), bf16[16,2,24,192]{3,2,1,0:T(8,128)(2,1)S(1)}, u32[]{:S(2)}, u32[]{:S(2)}) async-start(bf16[16,2,24,192]{3,2,1,0:T(8,128)(2,1)} %consistency.1), calls=%async_computation.1 | async-start | bytes 786432 | tf_op jit(solution)/shard_map/all_to_all | solution.py:354
  42.9 14.6 %copy-start.1 = (f32[24,1,2,2,192]{4,3,2,1,0:T(2,128)S(1)}, f32[24,1,2,2,192]{4,3,2,1,0:T(2,128)}, u32[]{:S(2)}) copy-start(f32[24,1,2,2,192]{4,3,2,1,0:T(2,128)} %image_ref.3) | copy-start | bytes 221188

commit v5 on v4

--- a/solution.py
+++ b/solution.py
@@ -62,7 +62,7 @@
     return respond.astype(ml_dtypes.bfloat16), spread.astype(ml_dtypes.bfloat16)
 
 
-def prepare_kernel(place_ref, image_ref, sent_ref, lines_ref, near_ref, far_ref, rows_ref):
+def prepare_kernel(image_ref, sent_ref, lines_ref, near_ref, far_ref, rows_ref):
     pad = jnp.zeros((ROWS, 256 - NZ), f32)
     for s in range(2):
         for p in range(2):
@@ -77,12 +77,12 @@
     lines_ref[...] = lines.astype(bf16)
     first = lines[: HALO * 4]
     last = lines[(ROWS - HALO) * 4 :]
-    even = place_ref[0] == 0
+    even = lax.rem(lax.axis_index("coil"), 2) == 0
     near_ref[...] = jnp.where(even, last, first).astype(bf16)
     far_ref[...] = jnp.where(even, first, last).astype(bf16)
 
 
-def prepare(place, image):
+def prepare(image):
     vmem = pl.BlockSpec(memory_space=pltpu.VMEM)
     return pl.pallas_call(
         prepare_kernel,
@@ -92,30 +92,30 @@
             jax.ShapeDtypeStruct((HALO * 4, NZ), bf16),
             jax.ShapeDtypeStruct((HALO * 4, NZ), bf16),
         ),
-        in_specs=[pl.BlockSpec(memory_space=pltpu.SMEM), vmem],
+        in_specs=[vmem],
         out_specs=(vmem, vmem, vmem, vmem),
         scratch_shapes=[pltpu.VMEM((2, ROWS * 4, 128), f32)],
         compiler_params=pltpu.CompilerParams(vmem_limit_bytes=8 << 20),
         name="prepare",
-    )(place, image)
+    )(image)
 
 
 def consistency_kernel(
-    place_ref, x_ref, kspace_hbm, maps_hbm, other_k_hbm, other_m_hbm, sampling_hbm, row_hbm, col_hbm, out_ref,
-    mine, other, sampling, row, col, sem
+    x_ref, kspace_hbm, maps_hbm, other_k_hbm, other_m_hbm, sampling_hbm, row_hbm, col_hbm, out_hbm,
+    measured, maps, sampling, row, col, out_ref, sem
 ):
-    core = place_ref[0]
+    core = lax.rem(lax.axis_index("coil"), 2)
     copies = [
         pltpu.make_async_copy(source, target, sem.at[i])
         for i, (source, target) in enumerate(
             (
-                (maps_hbm.at[core], mine.at[2:4]),
+                (maps_hbm.at[core], maps.at[0]),
+                (other_m_hbm, maps.at[1]),
                 (col_hbm, col),
                 (row_hbm, row),
-                (kspace_hbm.at[core], mine.at[0:2]),
+                (kspace_hbm.at[core], measured.at[0]),
+                (other_k_hbm, measured.at[1]),
                 (sampling_hbm, sampling),
-                (other_m_hbm, other.at[2:4]),
-                (other_k_hbm, other.at[0:2]),
             )
         )
     ]
@@ -127,64 +127,88 @@
 
     x_real = x_ref[:, 0].astype(f32).reshape(NY, NZ).T
     x_imag = x_ref[:, 1].astype(f32).reshape(NY, NZ).T
-    sum_real = jnp.zeros((NZ, NY), f32)
-    sum_imag = jnp.zeros((NZ, NY), f32)
-    copies[0].wait()
-    copies[1].wait()
-    for ref in (mine, other):
-        if ref is other:
-            copies[5].wait()
-            copies[6].wait()
-        map_real = ref[2].astype(f32)
-        map_imag = ref[3].astype(f32)
+    for copy in copies[:3]:
+        copy.wait()
+    columns = []
+    for c in range(2):
+        map_real = maps[c, 0].astype(f32)
+        map_imag = maps[c, 1].astype(f32)
         w_real = (map_real * x_real - map_imag * x_imag).astype(bf16)
         w_imag = (map_real * x_imag + map_imag * x_real).astype(bf16)
-        h_real = dot(col[...], jnp.concatenate([w_real, w_imag], 0)).astype(bf16)
-        h_imag = dot(col[...], jnp.concatenate([w_imag, -w_real], 0)).astype(bf16)
-        if ref is mine:
-            for copy in copies[2:5]:
-                copy.wait()
-        sampled = sampling[...].astype(f32)
-        s_real = dot(jnp.concatenate([h_real, h_imag], 1), row[...])
-        s_imag = dot(jnp.concatenate([h_imag, -h_real], 1), row[...])
-        r_real = (sampled * (s_real - ref[0].astype(f32))).astype(bf16)
-        r_imag = (sampled * (s_imag - ref[1].astype(f32))).astype(bf16)
-        b_real = dot(jnp.concatenate([r_real, -r_imag], 1), row[...]).astype(bf16)
-        b_imag = dot(jnp.concatenate([r_imag, r_real], 1), row[...]).astype(bf16)
-        o_real = dot(col[...], jnp.concatenate([b_real, -b_imag], 0))
-        o_imag = dot(col[...], jnp.concatenate([b_imag, b_real], 0))
-        sum_real = sum_real + map_real * o_real + map_imag * o_imag
-        sum_imag = sum_imag + map_real * o_imag - map_imag * o_real
-    out_ref[:, 0] = sum_real.T.reshape(COILS, ROWS, NZ).astype(bf16)
-    out_ref[:, 1] = sum_imag.T.reshape(COILS, ROWS, NZ).astype(bf16)
-
-
-def consistency(place, x, kspace, maps, other_k, other_m, sampling, row, col):
-    vmem = pl.BlockSpec(memory_space=pltpu.VMEM)
+        columns.append(jnp.concatenate([w_real, w_imag], 0))
+        columns.append(jnp.concatenate([w_imag, -w_real], 0))
+    h = dot(col[...], jnp.concatenate(columns, 1)).astype(bf16)
+    h = [h[:, i * NY : (i + 1) * NY] for i in range(4)]
+    for copy in copies[3:]:
+        copy.wait()
+    lines = []
+    for real, imag in ((h[0], h[1]), (h[2], h[3])):
+        lines.append(jnp.concatenate([real, imag], 1))
+        lines.append(jnp.concatenate([imag, -real], 1))
+    s = dot(jnp.concatenate(lines, 0), row[...])
+    sampled = sampling[...].astype(f32)
+    r = [
+        (sampled * (s[i * NZ : (i + 1) * NZ] - measured[i // 2, i % 2].astype(f32))).astype(bf16)
+        for i in range(4)
+    ]
+    lines = []
+    for real, imag in ((r[0], r[1]), (r[2], r[3])):
+        lines.append(jnp.concatenate([real, -imag], 1))
+        lines.append(jnp.concatenate([imag, real], 1))
+    b = dot(jnp.concatenate(lines, 0), row[...]).astype(bf16)
+    b = [b[i * NZ : (i + 1) * NZ] for i in range(4)]
+    columns = []
+    for real, imag in ((b[0], b[1]), (b[2], b[3])):
+        columns.append(jnp.concatenate([real, -imag], 0))
+        columns.append(jnp.concatenate([imag, real], 0))
+    o = dot(col[...], jnp.concatenate(columns, 1))
+    o = [o[:, i * NY : (i + 1) * NY] for i in range(4)]
+    outs = []
+    for part in range(2):
+        total = None
+        for c in range(2):
+            map_real = maps[c, 0].astype(f32)
+            map_imag = maps[c, 1].astype(f32)
+            if part == 0:
+                term = map_real * o[2 * c] + map_imag * o[2 * c + 1]
+            else:
+                term = map_real * o[2 * c + 1] - map_imag * o[2 * c]
+            total = term if total is None else total + term
+        out_ref[part] = total.T.reshape(COILS, ROWS, NZ).astype(bf16)
+        outs.append(
+            pltpu.make_async_copy(out_ref.at[part], out_hbm.at[:, part], sem.at[7 + part])
+        )
+        outs[-1].start()
+    for copy in outs:
+        copy.wait()
+
+
+def consistency(x, kspace, maps, other_k, other_m, sampling, row, col):
+    hbm = pl.BlockSpec(memory_space=pl.ANY)
     return pl.pallas_call(
         consistency_kernel,
         out_shape=jax.ShapeDtypeStruct((COILS, 2, ROWS, NZ), bf16),
-        in_specs=[pl.BlockSpec(memory_space=pltpu.SMEM), vmem]
-        + [pl.BlockSpec(memory_space=pl.ANY)] * 7,
-        out_specs=vmem,
+        in_specs=[pl.BlockSpec(memory_space=pltpu.VMEM)]
+        + [hbm] * 7,
+        out_specs=hbm,
         scratch_shapes=[
-            pltpu.VMEM((4, NZ, NY), bf16),
-            pltpu.VMEM((4, NZ, NY), bf16),
+            pltpu.VMEM((2, 2, NZ, NY), bf16),
+            pltpu.VMEM((2, 2, NZ, NY), bf16),
             pltpu.VMEM((NZ, NY), jnp.int32),
             pltpu.VMEM((2 * NY, NY), bf16),
             pltpu.VMEM((NZ, 2 * NZ), bf16),
-            pltpu.SemaphoreType.DMA((7,)),
+            pltpu.VMEM((2, COILS, ROWS, NZ), bf16),
+            pltpu.SemaphoreType.DMA((9,)),
         ],
         compiler_params=pltpu.CompilerParams(vmem_limit_bytes=52 << 20),
         cost_estimate=pl.CostEstimate(
             flops=4_000_000_000, bytes_accessed=3_000_000, transcendentals=0
         ),
         name="consistency",
-    )(place, x, kspace, maps, other_k, other_m, sampling, row, col)
+    )(x, kspace, maps, other_k, other_m, sampling, row, col)
 
 
 def regularizer_kernel(
-    place_ref,
     x0_ref,
     x1_ref,
     x2_ref,
@@ -198,6 +222,7 @@
     shifted_ref,
     total_ref,
 ):
+    coil = lax.axis_index("coil")
     for site in range(3):
         taps = jnp.dot(taps_ref[...], respond_ref[site], preferred_element_type=f32)
         for t in range(BAND):
@@ -228,10 +253,10 @@
         factor = magnitude / (magnitude + levels[first * SITES :, :])
         shrunk = response * factor
         if base == 0:
-            top = shrunk[:SITES] * place_ref[1].astype(f32)
+            top = shrunk[:SITES] * (coil > 0).astype(f32)
             shrunk = jnp.concatenate([top, shrunk[SITES:]], 0)
         if base == BASES[-1]:
-            bottom = shrunk[-SITES:] * place_ref[2].astype(f32)
+            bottom = shrunk[-SITES:] * (coil < COILS - 1).astype(f32)
             shrunk = jnp.concatenate([shrunk[:-SITES], bottom], 0)
         shrunk = shrunk.astype(bf16)
         for t in range(0, BAND - first, PAIR):
@@ -253,12 +278,12 @@
     out_ref[1] = jnp.concatenate([penalty[:, 128:], pad], 1)
 
 
-def regularizer(place, blocks, taps, respond, spread, thresholds):
+def regularizer(blocks, taps, respond, spread, thresholds):
     vmem = pl.BlockSpec(memory_space=pltpu.VMEM)
     return pl.pallas_call(
         regularizer_kernel,
         out_shape=jax.ShapeDtypeStruct((2, ROWS * 4, 128), f32),
-        in_specs=[pl.BlockSpec(memory_space=pltpu.SMEM)] + [vmem] * 8,
+        in_specs=[vmem] * 8,
         out_specs=vmem,
         scratch_shapes=[
             pltpu.VMEM((BAND * SITES, 256), bf16),
@@ -270,7 +295,7 @@
             flops=9_000_000_000, bytes_accessed=2_000_000, transcendentals=1_000_000
         ),
         name="regularizer",
-    )(place, *blocks, taps, respond, spread, thresholds)
+    )(*blocks, taps, respond, spread, thresholds)
 
 
 def update_kernel(weight_ref, image_ref, arrived_ref, penalty_ref, out_ref):
@@ -304,9 +329,8 @@
     coil = lax.axis_index("coil")
     core = lax.rem(coil, 2)
     read = lax.axis_index("read")
-    place = jnp.stack([core, (coil > 0).astype(jnp.int32), (coil < COILS - 1).astype(jnp.int32)])
-
-    sent, lines, near, far = prepare(place, image)
+
+    sent, lines, near, far = prepare(image)
     gathered = lax.all_to_all(sent, "coil", 0, 0, tiled=True)
 
     respond, spread = np_expansions()
@@ -349,10 +373,10 @@
         (gathered, taps, respond, spread, levels)
     )
     partial = consistency(
-        place, gathered, measured, maps, other_k, other_m, sampling[:, 0].T, row, col
+        gathered, measured, maps, other_k, other_m, sampling[:, 0].T, row, col
     )
     arrived = lax.all_to_all(partial, "coil", 0, 0, tiled=True)
-    penalty = regularizer(place, blocks, taps, respond, spread, levels)
+    penalty = regularizer(blocks, taps, respond, spread, levels)
     return update(dc_weight, image, arrived, penalty)
 
 

time: 58.5 us -> 57.1 us (0.976)
  Pallas kernels: 14.3 us -> 12 us
    pallas_call x1, Pallas kernels: 5.4 us -> 4.2 us  [consistency(): pl.pallas_call(consistency_kernel, out_shape=jax.ShapeDtypeStruct((COILS,...]
  transfers between devices with their start and end apart: 12 -> 12, of which waited for: 4 -> 4; matrix products, arithmetic and copies ran while one was open for 1% -> 1% of each run, Pallas kernels for 21% -> 18%
where the time goes in v5:
time: 57.1 us; the launch traced here: 56.7 us
  starting transfers between devices  28.4 us (50%)
  waiting for transfers between devices  13.1 us (23%)
  Pallas kernels  12 us (21%)
  local copies, waits for them, and re-layouts  2.04 us (4%)
  between operations  0.87 us (2%)
    all_to_all x1, waiting for transfers between devices, body(): arrived = lax.all_to_all(partial, 'coil', 0, 0, tiled=True)  8.35 us
    all_to_all x1, starting transfers between devices, body(): gathered = lax.all_to_all(sent, 'coil', 0, 0, tiled=True)  8.2 us
    ppermute x6, starting transfers between devices, swap(): return lax.ppermute(block, ('echo', 'read'), pairs)  7.44 us
    all_to_all x1, starting transfers between devices, body(): arrived = lax.all_to_all(partial, 'coil', 0, 0, tiled=True)  7.37 us
    pallas_call x1, Pallas kernels, regularizer(): pl.pallas_call(regularizer_kernel, out_shape=jax.ShapeDtypeStruct((2, ROW...  6.16 us
    ppermute x1, starting transfers between devices, body(): far = lax.ppermute(far, 'coil', next_chip)  4.92 us
    pallas_call x1, Pallas kernels, consistency(): pl.pallas_call(consistency_kernel, out_shape=jax.ShapeDtypeStruct((COILS,...  4.2 us
    ppermute x6, waiting for transfers between devices, swap(): return lax.ppermute(block, ('echo', 'read'), pairs)  2.62 us
  transfers between devices with their start and end apart: 12, of which 4 were waited for; matrix products, arithmetic and copies ran while one was open for 1% of the time, Pallas kernels for 18%

profile of v5, /device:TPU:1, one launch (start us, length us, event | category | flops | bytes accessed | tf_op | source)
XLA Modules:
  0.0 56.7 jit_solution(12237444107598029370)
XLA Ops:
  0.0 0.0 copy-start
  0.0 0.9 %copy-done = f32[24,1,2,2,192]{4,3,2,1,0:T(2,128)S(1)} copy-done((f32[24,1,2,2,192]{4,3,2,1,0:T(2,128)S(1)}, f32[24,1,2,2,192]{4,3,2,1,0:T(2,128)}, u32[]{:S(2)}) %copy-start) | copy-done | bytes 73752
  0.9 0.0 copy-start.5
  0.9 0.9 %prepare.1 = (bf16[16,2,24,192]{3,2,1,0:T(8,128)(2,1)}, bf16[96,192]{1,0:T(8,128)(2,1)S(1)}, bf16[8,192]{1,0:T(8,128)(2,1)S(1)}, bf16[8,192]{1,0:T(8,128)(2,1)S(1)}) custom-call(f32[24,1,2,2,192]{4,3,2,1,0:T(2,128)S(1)} %copy-done), custom_call_target="tpu_custom_call" | custom-call | tf_op jit(solution)/shard_map/prepare/pallas_call | solution.py:87
  1.8 4.9 %collective-permute-start = (bf16[8,192]{1,0:T(8,128)(2,1)S(1)}, bf16[8,192]{1,0:T(8,128)(2,1)S(1)}, u32[]{:S(2)}, u32[]{:S(2)}) collective-permute-start(bf16[8,192]{1,0:T(8,128)(2,1)S(1)} %get-tuple-element.19), channel_id=1, source_target_pairs={{2,4},{6,8},{10,12},{14,16},{18,20},{22,24},{26,28},{4,2},{8,6},{1... | collective-permute-start | bytes 9224 | tf_op jit(solution)/shard_map/ppermute | solution.py:349
  6.7 0.1 collective-permute-start.1
  6.8 0.0 copy-start.8
  6.8 8.2 %all-to-all-start = ((bf16[16,2,24,192]{3,2,1,0:T(8,128)(2,1)}), bf16[16,2,24,192]{3,2,1,0:T(8,128)(2,1)S(1)}, u32[]{:S(2)}, u32[]{:S(2)}) async-start(bf16[16,2,24,192]{3,2,1,0:T(8,128)(2,1)} %get-tuple-element.17), calls=%async_computation | async-start | bytes 786432 | tf_op jit(solution)/shard_map/all_to_all | solution.py:334
  15.0 0.0 copy-start.4
  15.0 0.0 copy-done.8
  15.1 0.0 collective-permute-done
  15.1 0.0 collective-permute-done.1
  15.1 0.0 copy-done.5
  15.2 0.0 copy-start.7
  15.2 0.2 collective-permute-start.3
  15.4 0.7 %copy-done.4 = bf16[384,1,1,2,2,192]{0,5,4,3,2,1:T(8,128)(2,1)S(1)} copy-done((bf16[384,1,1,2,2,192]{0,5,4,3,2,1:T(8,128)(2,1)S(1)}, bf16[384,1,1,2,2,192]{0,5,4,3,2,1:T(8,128)(2,1)}, u32[]{:S(2)}) %copy-start.4) | copy-done | bytes 589848
  16.1 0.0 copy-start.6
  16.1 0.2 collective-permute-start.2
  16.3 0.0 copy-done.7
  16.3 0.1 fusion
  16.5 2.8 %collective-permute-start.6 = (bf16[112,192]{1,0:T(8,128)(2,1)S(1)}, bf16[112,192]{1,0:T(8,128)(2,1)S(1)}, u32[]{:S(2)}, u32[]{:S(2)}) collective-permute-start(bf16[112,192]{1,0:T(8,128)(2,1)S(1)} %pad_maximum_fusion.1), channel_id=1, source_target_pairs={{0,33},{1,32},{32,1},{33,0},{64,97},{65,96},{96,65},{97,64},{128,1... | collective-permute-start | bytes 129032 | tf_op jit(solution)/shard_map/ppermute | solution.py:367
  19.3 0.0 collective-permute-start.5
  19.3 1.3 %collective-permute-start.4 = (bf16[112,192]{1,0:T(8,128)(2,1)S(1)}, bf16[112,192]{1,0:T(8,128)(2,1)S(1)}, u32[]{:S(2)}, u32[]{:S(2)}) collective-permute-start(bf16[112,192]{1,0:T(8,128)(2,1)S(1)} %pad_maximum_fusion.1), channel_id=1, source_target_pairs={{0,1},{1,0},{32,33},{33,32},{64,65},{65,64},{96,97},{97,96},{128,1... | collective-permute-start | bytes 129032 | tf_op jit(solution)/shard_map/ppermute | solution.py:367
  20.6 0.0 copy-done.6
  21.3 0.0 copy-start.2
  21.3 0.1 reshape.11.spread_ref
  21.4 0.0 collective-permute-done.6
  21.4 1.2 %collective-permute-done.5 = bf16[112,192]{1,0:T(8,128)(2,1)S(1)} collective-permute-done((bf16[112,192]{1,0:T(8,128)(2,1)S(1)}, bf16[112,192]{1,0:T(8,128)(2,1)S(1)}, u32[]{:S(2)}, u32[]{:S(2)}) %collective-permute-start.5) | collective-permute-done | bytes 43040 | tf_op jit(solution)/shard_map/ppermute | solution.py:367
  22.6 1.4 %collective-permute-done.4 = bf16[112,192]{1,0:T(8,128)(2,1)S(1)} collective-permute-done((bf16[112,192]{1,0:T(8,128)(2,1)S(1)}, bf16[112,192]{1,0:T(8,128)(2,1)S(1)}, u32[]{:S(2)}, u32[]{:S(2)}) %collective-permute-start.4) | collective-permute-done | bytes 43040 | tf_op jit(solution)/shard_map/ppermute | solution.py:367
  24.0 0.0 copy-start.3
  24.0 0.1 pad_maximum_fusion
  24.1 0.0 copy-start.9
  24.1 2.6 %collective-permute-start.9 = (bf16[2,2,112,192]{3,2,1,0:T(8,128)(2,1)S(1)}, bf16[2,2,112,192]{3,2,1,0:T(8,128)(2,1)S(1)}, u32[]{:S(2)}, u32[]{:S(2)}) collective-permute-start(bf16[2,2,112,192]{3,2,1,0:T(8,128)(2,1)S(1)} %bitcast.30), channel_id=1, source_target_pairs={{0,192},{1,193},{32,224},{33,225},{64,128},{65,129},{96,160},{97,1... | collective-permute-start | bytes 516104 | tf_op jit(solution)/shard_map/ppermute | solution.py:367
  26.7 0.5 collective-permute-start.8
  27.2 0.3 collective-permute-start.7
  27.4 2.1 %all-to-all-done.x_ref = bf16[16,2,24,192]{3,2,1,0:T(8,128)(2,1)S(1)} async-done(((bf16[16,2,24,192]{3,2,1,0:T(8,128)(2,1)}), bf16[16,2,24,192]{3,2,1,0:T(8,128)(2,1)S(1)}, u32[]{:S(2)}, u32[]{:S(2)}) %all-to-all-start) | async-done | bytes 294944 | tf_op jit(solution)/shard_map/all_to_all | solution.py:334
  29.6 0.0 copy-done.9
  29.6 0.1 broadcast_in_dim.2.thresholds_ref
  29.6 0.0 collective-permute-done.3.other_m_hbm
  29.7 0.0 collective-permute-done.2.other_k_hbm
  29.7 0.0 copy-done.2
  29.7 0.0 copy-done.3
  29.7 4.2 %consistency.1 = bf16[16,2,24,192]{3,2,1,0:T(8,128)(2,1)} custom-call(bf16[16,2,24,192]{3,2,1,0:T(8,128)(2,1)S(1)} %all-to-all-done.x_ref, bf16[2,2,192,384]{3,2,1,0:T(8,128)(2,1)} %bitcast.36, bf16[2,2,192,384]{3,2,1,0:T(8,128)(2,1)} %bitcast.38, bf16[2,192,384]{2,1,0:T(8,128)(2,1)S(1)} %collective-permute-done.2.other_k_hbm, ...), custom_call_target="tpu_custom_call" | custom-call | flops 4000000000 | bytes 3000000 | tf_op jit(solution)/shard_map/consistency/pallas_call | solution.py:188
  33.9 0.1 copy.16.taps_ref
  34.0 7.4 %all-to-all-start.1 = ((bf16[16,2,24,192]{3,2,1,0:T(8,128)(2,1)}), bf16[16,2,24,192]{3,2,1,0:T(8,128)(2,1)S(1)}, u32[]{:S(2)}, u32[]{:S(2)}) async-start(bf16[16,2,24,192]{3,2,1,0:T(8,128)(2,1)} %consistency.1), calls=%async_computation.1 | async-start | bytes 786432 | tf_op jit(solution)/shard_map/all_to_all | solution.py:378
  41.3 0.0 copy-start.1
  41.4 0.0 collective-permute-done.9.x3_ref
  41.4 0.0 collective-permute-done.8.x2_ref
  41.4 0.0 collective-permute-done.7.x1_ref
  41.4 6.2 %regularizer.1.penalty_ref = f32[2,96,128]{2,1,0:T(8,128)S(1)} custom-call(bf16[2,2,112,192]{3,2,1,0:T(8,128)(2,1)S(1)} %bitcast.33, bf16[2,2,112,192]{3,2,1,0:T(8,128)(2,1)S(1)} %collective-permute-done.7.x1_ref, bf16[2,2,112,192]{3,2,1,0:T(8,128)(2,1)S(1)} %collective-permute-done.8.x2_ref, bf16[2,2,112,192]{3,2,1,0:T(8,128)(2,1)S(1)} %collective-permute-done.9.x3_ref, ...), custom_call_target="tpu_custom_call" | custom-call | flops 8999999488 | bytes 2000000 | tf_op jit(solution)/shard_map/regularizer/pallas_call | solution.py:283
  47.6 8.3 %all-to-all-done.1.arrived_ref = bf16[16,2,24,192]{3,2,1,0:T(8,128)(2,1)S(1)} async-done(((bf16[16,2,24,192]{3,2,1,0:T(8,128)(2,1)}), bf16[16,2,24,192]{3,2,1,0:T(8,128)(2,1)S(1)}, u32[]{:S(2)}, u32[]{:S(2)}) %all-to-all-start.1) | async-done | bytes 294944 | tf_op jit(solution)/shard_map/all_to_all | solution.py:378
  55.9 0.0 copy-done.1
  55.9 0.8 %update.1 = f32[24,1,2,2,192]{4,3,2,1,0:T(2,128)} custom-call(f32[1]{0:T(128)S(6)} %copy.19.weight_ref, f32[24,1,2,2,192]{4,3,2,1,0:T(2,128)S(1)} %copy-done.1, bf16[16,2,24,192]{3,2,1,0:T(8,128)(2,1)S(1)} %all-to-all-done.1.arrived_ref, f32[2,96,128]{2,1,0:T(8,128)S(1)} %regularizer.1.penalty_ref), custom_call_target="tpu_custom_call" | custom-call | tf_op jit(solution)/shard_map/update/pallas_call | solution.py:316
  (7 shorter events, 0.2 us)
Async XLA Ops:
  0.0 0.9 %copy-start = (f32[24,1,2,2,192]{4,3,2,1,0:T(2,128)S(1)}, f32[24,1,2,2,192]{4,3,2,1,0:T(2,128)}, u32[]{:S(2)}) copy-start(f32[24,1,2,2,192]{4,3,2,1,0:T(2,128)} %image_ref.3) | copy-start | bytes 221188
  0.9 14.2 %copy-start.5 = (bf16[384,1,2,2,192]{0,4,3,2,1:T(8,128)(2,1)S(1)}, bf16[384,1,2,2,192]{0,4,3,2,1:T(8,128)(2,1)}, u32[]{:S(2)}) copy-start(bf16[384,1,2,2,192]{0,4,3,2,1:T(8,128)(2,1)} %param.13) | copy-start | bytes 1769476
  1.8 13.3 %collective-permute-start = (bf16[8,192]{1,0:T(8,128)(2,1)S(1)}, bf16[8,192]{1,0:T(8,128)(2,1)S(1)}, u32[]{:S(2)}, u32[]{:S(2)}) collective-permute-start(bf16[8,192]{1,0:T(8,128)(2,1)S(1)} %get-tuple-element.19), channel_id=1, source_target_pairs={{2,4},{6,8},{10,12},{14,16},{18,20},{22,24},{26,28},{4,2},{8,6},{1... | collective-permute-start | bytes 9224 | tf_op jit(solution)/shard_map/ppermute | solution.py:349
  6.7 8.4 %collective-permute-start.1 = (bf16[8,192]{1,0:T(8,128)(2,1)S(1)}, bf16[8,192]{1,0:T(8,128)(2,1)S(1)}, u32[]{:S(2)}, u32[]{:S(2)}) collective-permute-start(bf16[8,192]{1,0:T(8,128)(2,1)S(1)} %get-tuple-element.20), channel_id=1, source_target_pairs={{0,2},{2,0},{4,6},{6,4},{8,10},{10,8},{12,14},{14,12},{16,18},{18,... | collective-permute-start | bytes 9224 | tf_op jit(solution)/shard_map/ppermute | solution.py:348
  6.8 8.2 %copy-start.8 = (bf16[48,3,3,3,2]{0,4,3,2,1:T(2,128)(2,1)S(1)}, bf16[48,3,3,3,2]{0,4,3,2,1:T(2,128)(2,1)}, u32[]{:S(2)}) copy-start(bf16[48,3,3,3,2]{0,4,3,2,1:T(2,128)(2,1)} %param.15) | copy-start | bytes 15556
  6.8 22.7 %all-to-all-start = ((bf16[16,2,24,192]{3,2,1,0:T(8,128)(2,1)}), bf16[16,2,24,192]{3,2,1,0:T(8,128)(2,1)S(1)}, u32[]{:S(2)}, u32[]{:S(2)}) async-start(bf16[16,2,24,192]{3,2,1,0:T(8,128)(2,1)} %get-tuple-element.17), calls=%async_computation | async-start | bytes 786432 | tf_op jit(solution)/shard_map/all_to_all | solution.py:334
  15.0 1.1 %copy-start.4 = (bf16[384,1,1,2,2,192]{0,5,4,3,2,1:T(8,128)(2,1)S(1)}, bf16[384,1,1,2,2,192]{0,5,4,3,2,1:T(8,128)(2,1)}, u32[]{:S(2)}) copy-start(bf16[384,1,1,2,2,192]{0,5,4,3,2,1:T(8,128)(2,1)} %param.11) | copy-start | bytes 1769476
  15.2 1.1 %copy-start.7 = (bf16[2,6,54,48]{2,3,1,0:T(8,128)(2,1)S(1)}, bf16[2,6,54,48]{2,3,1,0:T(8,128)(2,1)}, u32[]{:S(2)}) copy-start(bf16[2,6,54,48]{2,3,1,0:T(8,128)(2,1)} %constant.43.clone) | copy-start | bytes 186628
  15.2 14.4 %collective-permute-start.3 = (bf16[2,192,384]{2,1,0:T(8,128)(2,1)S(1)}, bf16[2,192,384]{2,1,0:T(8,128)(2,1)S(1)}, u32[]{:S(2)}, u32[]{:S(2)}) collective-permute-start(bf16[2,192,384]{2,1,0:T(8,128)(2,1)S(1)} %dynamic-slice_bitcast_fusion), channel_id=1, source_target_pairs={{0,2},{2,0},{4,6},{6,4},{8,10},{10,8},{12,14},{14,12},{16,18},{18,... | collective-permute-start | bytes 884744 | tf_op jit(solution)/shard_map/ppermute | solution.py:361
  16.1 4.5 %copy-start.6 = (bf16[2,3,54,256]{3,2,1,0:T(8,128)(2,1)S(1)}, bf16[2,3,54,256]{3,2,1,0:T(8,128)(2,1)}, u32[]{:S(2)}) copy-start(bf16[2,3,54,256]{3,2,1,0:T(8,128)(2,1)} %constant.42.clone) | copy-start | bytes 497668
  16.1 13.5 %collective-permute-start.2 = (bf16[2,192,384]{2,1,0:T(8,128)(2,1)S(1)}, bf16[2,192,384]{2,1,0:T(8,128)(2,1)S(1)}, u32[]{:S(2)}, u32[]{:S(2)}) collective-permute-start(bf16[2,192,384]{2,1,0:T(8,128)(2,1)S(1)} %dynamic-slice_bitcast_fusion.1), channel_id=1, source_target_pairs={{0,2},{2,0},{4,6},{6,4},{8,10},{10,8},{12,14},{14,12},{16,18},{18,... | collective-permute-start | bytes 884744 | tf_op jit(solution)/shard_map/ppermute | solution.py:358
  16.5 4.9 %collective-permute-start.6 = (bf16[112,192]{1,0:T(8,128)(2,1)S(1)}, bf16[112,192]{1,0:T(8,128)(2,1)S(1)}, u32[]{:S(2)}, u32[]{:S(2)}) collective-permute-start(bf16[112,192]{1,0:T(8,128)(2,1)S(1)} %pad_maximum_fusion.1), channel_id=1, source_target_pairs={{0,33},{1,32},{32,1},{33,0},{64,97},{65,96},{96,65},{97,64},{128,1... | collective-permute-start | bytes 129032 | tf_op jit(solution)/shard_map/ppermute | solution.py:367
  19.3 3.3 %collective-permute-start.5 = (bf16[112,192]{1,0:T(8,128)(2,1)S(1)}, bf16[112,192]{1,0:T(8,128)(2,1)S(1)}, u32[]{:S(2)}, u32[]{:S(2)}) collective-permute-start(bf16[112,192]{1,0:T(8,128)(2,1)S(1)} %pad_maximum_fusion.1), channel_id=1, source_target_pairs={{0,32},{1,33},{32,0},{33,1},{64,96},{65,97},{96,64},{97,65},{128,1... | collective-permute-start | bytes 129032 | tf_op jit(solution)/shard_map/ppermute | solution.py:367
  19.3 4.7 %collective-permute-start.4 = (bf16[112,192]{1,0:T(8,128)(2,1)S(1)}, bf16[112,192]{1,0:T(8,128)(2,1)S(1)}, u32[]{:S(2)}, u32[]{:S(2)}) collective-permute-start(bf16[112,192]{1,0:T(8,128)(2,1)S(1)} %pad_maximum_fusion.1), channel_id=1, source_target_pairs={{0,1},{1,0},{32,33},{33,32},{64,65},{65,64},{96,97},{97,96},{128,1... | collective-permute-start | bytes 129032 | tf_op jit(solution)/shard_map/ppermute | solution.py:367
  21.3 8.4 %copy-start.2 = (s32[384,1,192]{0,2,1:T(8,128)S(1)}, s32[384,1,192]{0,2,1:T(8,128)}, u32[]{:S(2)}) copy-start(s32[384,1,192]{0,2,1:T(8,128)} %param.12) | copy-start | bytes 884740
  24.0 5.7 %copy-start.3 = (bf16[192,384]{1,0:T(8,128)(2,1)S(1)}, bf16[192,384]{1,0:T(8,128)(2,1)}, u32[]{:S(2)}) copy-start(bf16[192,384]{1,0:T(8,128)(2,1)} %constant.41.clone.col_hbm) | copy-start | bytes 442372
  24.1 5.5 %copy-start.9 = (f32[48]{0:T(128)S(1)}, f32[48]{0:T(128)}, u32[]{:S(2)}) copy-start(f32[48]{0:T(128)} %param.16) | copy-start | bytes 580
  24.1 17.3 %collective-permute-start.9 = (bf16[2,2,112,192]{3,2,1,0:T(8,128)(2,1)S(1)}, bf16[2,2,112,192]{3,2,1,0:T(8,128)(2,1)S(1)}, u32[]{:S(2)}, u32[]{:S(2)}) collective-permute-start(bf16[2,2,112,192]{3,2,1,0:T(8,128)(2,1)S(1)} %bitcast.30), channel_id=1, source_target_pairs={{0,192},{1,193},{32,224},{33,225},{64,128},{65,129},{96,160},{97,1... | collective-permute-start | bytes 516104 | tf_op jit(solution)/shard_map/ppermute | solution.py:367
  26.7 14.7 %collective-permute-start.8 = (bf16[2,2,112,192]{3,2,1,0:T(8,128)(2,1)S(1)}, bf16[2,2,112,192]{3,2,1,0:T(8,128)(2,1)S(1)}, u32[]{:S(2)}, u32[]{:S(2)}) collective-permute-start(bf16[2,2,112,192]{3,2,1,0:T(8,128)(2,1)S(1)} %bitcast.31), channel_id=1, source_target_pairs={{0,128},{1,129},{32,160},{33,161},{64,192},{65,193},{96,224},{97,2... | collective-permute-start | bytes 516104 | tf_op jit(solution)/shard_map/ppermute | solution.py:367
  27.2 14.2 %collective-permute-start.7 = (bf16[2,2,112,192]{3,2,1,0:T(8,128)(2,1)S(1)}, bf16[2,2,112,192]{3,2,1,0:T(8,128)(2,1)S(1)}, u32[]{:S(2)}, u32[]{:S(2)}) collective-permute-start(bf16[2,2,112,192]{3,2,1,0:T(8,128)(2,1)S(1)} %bitcast.32), channel_id=1, source_target_pairs={{0,64},{1,65},{32,96},{33,97},{64,0},{65,1},{96,32},{97,33},{128,1... | collective-permute-start | bytes 516104 | tf_op jit(solution)/shard_map/ppermute | solution.py:367
  34.0 21.9 %all-to-all-start.1 = ((bf16[16,2,24,192]{3,2,1,0:T(8,128)(2,1)}), bf16[16,2,24,192]{3,2,1,0:T(8,128)(2,1)S(1)}, u32[]{:S(2)}, u32[]{:S(2)}) async-start(bf16[16,2,24,192]{3,2,1,0:T(8,128)(2,1)} %consistency.1), calls=%async_computation.1 | async-start | bytes 786432 | tf_op jit(solution)/shard_map/all_to_all | solution.py:378
  41.3 14.6 %copy-start.1 = (f32[24,1,2,2,192]{4,3,2,1,0:T(2,128)S(1)}, f32[24,1,2,2,192]{4,3,2,1,0:T(2,128)}, u32[]{:S(2)}) copy-start(f32[24,1,2,2,192]{4,3,2,1,0:T(2,128)} %image_ref.3) | copy-start | bytes 221188

commit v6 on v5

--- a/solution.py
+++ b/solution.py
@@ -23,6 +23,7 @@
 LINES = ROWS + 2 * HALO
 BASES = (0, 8, 16, 18)
 FIRST = (0, 0, 0, 6)
+BACKWARD = list(range(COILS))[::-1]
 
 bf16 = jnp.bfloat16
 f32 = jnp.float32
@@ -72,7 +73,7 @@
             rows_ref[1, rows, :] = jnp.concatenate([plane[:, 128:], pad], 1)
             plane = plane.astype(bf16)
             for z in range(COILS // 2):
-                sent_ref[2 * z + s, p] = plane
+                sent_ref[COILS - 1 - 2 * z - s, p] = plane
     lines = jnp.concatenate([rows_ref[0], rows_ref[1, :, : NZ - 128]], 1)
     lines_ref[...] = lines.astype(bf16)
     first = lines[: HALO * 4]
@@ -125,8 +126,8 @@
     def dot(left, right):
         return jnp.dot(left, right, preferred_element_type=f32)
 
-    x_real = x_ref[:, 0].astype(f32).reshape(NY, NZ).T
-    x_imag = x_ref[:, 1].astype(f32).reshape(NY, NZ).T
+    x_real = jnp.concatenate([x_ref[c, 0].astype(f32) for c in BACKWARD], 0).T
+    x_imag = jnp.concatenate([x_ref[c, 1].astype(f32) for c in BACKWARD], 0).T
     for copy in copies[:3]:
         copy.wait()
     columns = []
@@ -174,7 +175,9 @@
             else:
                 term = map_real * o[2 * c + 1] - map_imag * o[2 * c]
             total = term if total is None else total + term
-        out_ref[part] = total.T.reshape(COILS, ROWS, NZ).astype(bf16)
+        total = total.T.astype(bf16)
+        for c in range(COILS):
+            out_ref[part, COILS - 1 - c] = total[c * ROWS : (c + 1) * ROWS]
         outs.append(
             pltpu.make_async_copy(out_ref.at[part], out_hbm.at[:, part], sem.at[7 + part])
         )
@@ -301,9 +304,9 @@
 def update_kernel(weight_ref, image_ref, arrived_ref, penalty_ref, out_ref):
     for s in range(2):
         for p in range(2):
-            total = arrived_ref[s, p].astype(f32)
+            total = arrived_ref[1 - s, p].astype(f32)
             for z in range(1, COILS // 2):
-                total = total + arrived_ref[2 * z + s, p].astype(f32)
+                total = total + arrived_ref[2 * z + 1 - s, p].astype(f32)
             rows = pl.ds(s * 2 + p, ROWS, stride=4)
             penalty = jnp.concatenate(
                 [penalty_ref[0, rows, :], penalty_ref[1, rows, :][:, : NZ - 128]], 1
@@ -331,7 +334,9 @@
     read = lax.axis_index("read")
 
     sent, lines, near, far = prepare(image)
-    gathered = lax.all_to_all(sent, "coil", 0, 0, tiled=True)
+    gathered = lax.all_to_all(
+        sent, "coil", 0, 0, tiled=True, axis_index_groups=[BACKWARD]
+    )
 
     respond, spread = np_expansions()
     taps = filters.reshape(FILTERS, 54)
@@ -375,7 +380,9 @@
     partial = consistency(
         gathered, measured, maps, other_k, other_m, sampling[:, 0].T, row, col
     )
-    arrived = lax.all_to_all(partial, "coil", 0, 0, tiled=True)
+    arrived = lax.all_to_all(
+        partial, "coil", 0, 0, tiled=True, axis_index_groups=[BACKWARD]
+    )
     penalty = regularizer(blocks, taps, respond, spread, levels)
     return update(dc_weight, image, arrived, penalty)
 

time: 57.1 us -> 54.3 us (0.951)
  waiting for transfers between devices: 13.1 us -> 6.84 us
  starting transfers between devices: 28.4 us -> 32.2 us
    all_to_all x2, waiting for transfers between devices: 10.5 us -> 4.37 us  [the longest x1 4.37 us: body(): lax.all_to_all(partial, 'coil', 0, 0, tiled=True, axis_index_groups=[BACK...]
    all_to_all x2, starting transfers between devices: 15.6 us -> 18.7 us  [the longest x1 9.75 us: body(): lax.all_to_all(sent, 'coil', 0, 0, tiled=True, axis_index_groups=[BACKWARD])]
  transfers between devices with their start and end apart: 12 -> 12, of which waited for: 4 -> 3; matrix products, arithmetic and copies ran while one was open for 1% -> 1% of each run, Pallas kernels for 18% -> 19%
where the time goes in v6:
time: 54.3 us; the launch traced here: 53.9 us
  starting transfers between devices  32.2 us (59%)
  Pallas kernels  12 us (22%)
  waiting for transfers between devices  6.84 us (13%)
  local copies, waits for them, and re-layouts  1.72 us (3%)
  between operations  0.87 us (2%)
    all_to_all x1, starting transfers between devices, body(): lax.all_to_all(sent, 'coil', 0, 0, tiled=True, axis_index_groups=[BACKWARD])  9.75 us
    all_to_all x1, starting transfers between devices, body(): lax.all_to_all(partial, 'coil', 0, 0, tiled=True, axis_index_groups=[BACK...  9 us
    ppermute x6, starting transfers between devices, swap(): return lax.ppermute(block, ('echo', 'read'), pairs)  7.44 us
    pallas_call x1, Pallas kernels, regularizer(): pl.pallas_call(regularizer_kernel, out_shape=jax.ShapeDtypeStruct((2, ROW...  6.16 us
    ppermute x1, starting transfers between devices, body(): far = lax.ppermute(far, 'coil', next_chip)  4.92 us
    all_to_all x1, waiting for transfers between devices, body(): lax.all_to_all(partial, 'coil', 0, 0, tiled=True, axis_index_groups=[BACK...  4.37 us
    pallas_call x1, Pallas kernels, consistency(): pl.pallas_call(consistency_kernel, out_shape=jax.ShapeDtypeStruct((COILS,...  4.2 us
    ppermute x6, waiting for transfers between devices, swap(): return lax.ppermute(block, ('echo', 'read'), pairs)  2.46 us
  transfers between devices with their start and end apart: 12, of which 3 were waited for; matrix products, arithmetic and copies ran while one was open for 1% of the time, Pallas kernels for 19%

profile of v6, /device:TPU:1, one launch (start us, length us, event | category | flops | bytes accessed | tf_op | source)
XLA Modules:
  0.0 53.9 jit_solution(5072674630182809567)
XLA Ops:
  0.0 0.0 copy-start
  0.0 0.9 %copy-done = f32[24,1,2,2,192]{4,3,2,1,0:T(2,128)S(1)} copy-done((f32[24,1,2,2,192]{4,3,2,1,0:T(2,128)S(1)}, f32[24,1,2,2,192]{4,3,2,1,0:T(2,128)}, u32[]{:S(2)}) %copy-start) | copy-done | bytes 73752
  0.9 0.0 copy-start.5
  0.9 0.9 %prepare.1 = (bf16[16,2,24,192]{3,2,1,0:T(8,128)(2,1)}, bf16[96,192]{1,0:T(8,128)(2,1)S(1)}, bf16[8,192]{1,0:T(8,128)(2,1)S(1)}, bf16[8,192]{1,0:T(8,128)(2,1)S(1)}) custom-call(f32[24,1,2,2,192]{4,3,2,1,0:T(2,128)S(1)} %copy-done), custom_call_target="tpu_custom_call" | custom-call | tf_op jit(solution)/shard_map/prepare/pallas_call | solution.py:88
  1.8 4.9 %collective-permute-start = (bf16[8,192]{1,0:T(8,128)(2,1)S(1)}, bf16[8,192]{1,0:T(8,128)(2,1)S(1)}, u32[]{:S(2)}, u32[]{:S(2)}) collective-permute-start(bf16[8,192]{1,0:T(8,128)(2,1)S(1)} %get-tuple-element.19), channel_id=1, source_target_pairs={{2,4},{6,8},{10,12},{14,16},{18,20},{22,24},{26,28},{4,2},{8,6},{1... | collective-permute-start | bytes 9224 | tf_op jit(solution)/shard_map/ppermute | solution.py:354
  6.7 0.1 collective-permute-start.1
  6.8 0.0 copy-start.8
  6.8 9.7 %all-to-all-start = ((bf16[16,2,24,192]{3,2,1,0:T(8,128)(2,1)}), bf16[16,2,24,192]{3,2,1,0:T(8,128)(2,1)S(1)}, u32[]{:S(2)}, u32[]{:S(2)}) async-start(bf16[16,2,24,192]{3,2,1,0:T(8,128)(2,1)} %get-tuple-element.17), calls=%async_computation | async-start | bytes 786432 | tf_op jit(solution)/shard_map/all_to_all | solution.py:337
  16.6 0.0 copy-start.4
  16.6 0.0 copy-done.8
  16.6 0.0 collective-permute-done
  16.6 0.0 collective-permute-done.1
  16.7 0.0 copy-done.5
  16.7 0.0 copy-start.7
  16.8 0.5 collective-permute-start.3
  17.3 0.4 copy-done.4
  17.6 0.0 copy-start.6
  17.7 0.5 collective-permute-start.2
  18.2 0.0 copy-done.7
  18.2 0.1 fusion
  18.3 2.8 %collective-permute-start.6 = (bf16[112,192]{1,0:T(8,128)(2,1)S(1)}, bf16[112,192]{1,0:T(8,128)(2,1)S(1)}, u32[]{:S(2)}, u32[]{:S(2)}) collective-permute-start(bf16[112,192]{1,0:T(8,128)(2,1)S(1)} %pad_maximum_fusion.1), channel_id=1, source_target_pairs={{0,33},{1,32},{32,1},{33,0},{64,97},{65,96},{96,65},{97,64},{128,1... | collective-permute-start | bytes 129032 | tf_op jit(solution)/shard_map/ppermute | solution.py:372
  21.2 0.0 collective-permute-start.5
  21.2 1.3 %collective-permute-start.4 = (bf16[112,192]{1,0:T(8,128)(2,1)S(1)}, bf16[112,192]{1,0:T(8,128)(2,1)S(1)}, u32[]{:S(2)}, u32[]{:S(2)}) collective-permute-start(bf16[112,192]{1,0:T(8,128)(2,1)S(1)} %pad_maximum_fusion.1), channel_id=1, source_target_pairs={{0,1},{1,0},{32,33},{33,32},{64,65},{65,64},{96,97},{97,96},{128,1... | collective-permute-start | bytes 129032 | tf_op jit(solution)/shard_map/ppermute | solution.py:372
  22.4 0.0 copy-done.6
  23.1 0.0 copy-start.2
  23.2 0.1 reshape.11.spread_ref
  23.3 0.0 collective-permute-done.6
  23.3 1.1 %collective-permute-done.5 = bf16[112,192]{1,0:T(8,128)(2,1)S(1)} collective-permute-done((bf16[112,192]{1,0:T(8,128)(2,1)S(1)}, bf16[112,192]{1,0:T(8,128)(2,1)S(1)}, u32[]{:S(2)}, u32[]{:S(2)}) %collective-permute-start.5) | collective-permute-done | bytes 43040 | tf_op jit(solution)/shard_map/ppermute | solution.py:372
  24.4 1.4 %collective-permute-done.4 = bf16[112,192]{1,0:T(8,128)(2,1)S(1)} collective-permute-done((bf16[112,192]{1,0:T(8,128)(2,1)S(1)}, bf16[112,192]{1,0:T(8,128)(2,1)S(1)}, u32[]{:S(2)}, u32[]{:S(2)}) %collective-permute-start.4) | collective-permute-done | bytes 43040 | tf_op jit(solution)/shard_map/ppermute | solution.py:372
  25.7 0.0 copy-start.3
  25.7 0.1 pad_maximum_fusion
  25.8 0.0 copy-start.9
  25.8 2.6 %collective-permute-start.9 = (bf16[2,2,112,192]{3,2,1,0:T(8,128)(2,1)S(1)}, bf16[2,2,112,192]{3,2,1,0:T(8,128)(2,1)S(1)}, u32[]{:S(2)}, u32[]{:S(2)}) collective-permute-start(bf16[2,2,112,192]{3,2,1,0:T(8,128)(2,1)S(1)} %bitcast.30), channel_id=1, source_target_pairs={{0,192},{1,193},{32,224},{33,225},{64,128},{65,129},{96,160},{97,1... | collective-permute-start | bytes 516104 | tf_op jit(solution)/shard_map/ppermute | solution.py:372
  28.4 0.5 collective-permute-start.8
  28.9 0.3 collective-permute-start.7
  29.1 0.0 all-to-all-done.x_ref
  29.2 0.0 copy-done.9
  29.2 0.1 broadcast_in_dim.2.thresholds_ref
  29.2 0.0 collective-permute-done.3.other_m_hbm
  29.2 0.0 collective-permute-done.2.other_k_hbm
  29.2 0.0 copy-done.2
  29.2 0.0 copy-done.3
  29.3 4.2 %consistency.1 = bf16[16,2,24,192]{3,2,1,0:T(8,128)(2,1)} custom-call(bf16[16,2,24,192]{3,2,1,0:T(8,128)(2,1)S(1)} %all-to-all-done.x_ref, bf16[2,2,192,384]{3,2,1,0:T(8,128)(2,1)} %bitcast.36, bf16[2,2,192,384]{3,2,1,0:T(8,128)(2,1)} %bitcast.38, bf16[2,192,384]{2,1,0:T(8,128)(2,1)S(1)} %collective-permute-done.2.other_k_hbm, ...), custom_call_target="tpu_custom_call" | custom-call | flops 4000000000 | bytes 3000000 | tf_op jit(solution)/shard_map/consistency/pallas_call | solution.py:191
  33.5 0.1 copy.16.taps_ref
  33.6 9.0 %all-to-all-start.1 = ((bf16[16,2,24,192]{3,2,1,0:T(8,128)(2,1)}), bf16[16,2,24,192]{3,2,1,0:T(8,128)(2,1)S(1)}, u32[]{:S(2)}, u32[]{:S(2)}) async-start(bf16[16,2,24,192]{3,2,1,0:T(8,128)(2,1)} %consistency.1), calls=%async_computation.1 | async-start | bytes 786432 | tf_op jit(solution)/shard_map/all_to_all | solution.py:383
  42.6 0.0 copy-start.1
  42.6 0.0 collective-permute-done.9.x3_ref
  42.6 0.0 collective-permute-done.8.x2_ref
  42.6 0.0 collective-permute-done.7.x1_ref
  42.6 6.2 %regularizer.1.penalty_ref = f32[2,96,128]{2,1,0:T(8,128)S(1)} custom-call(bf16[2,2,112,192]{3,2,1,0:T(8,128)(2,1)S(1)} %bitcast.33, bf16[2,2,112,192]{3,2,1,0:T(8,128)(2,1)S(1)} %collective-permute-done.7.x1_ref, bf16[2,2,112,192]{3,2,1,0:T(8,128)(2,1)S(1)} %collective-permute-done.8.x2_ref, bf16[2,2,112,192]{3,2,1,0:T(8,128)(2,1)S(1)} %collective-permute-done.9.x3_ref, ...), custom_call_target="tpu_custom_call" | custom-call | flops 8999999488 | bytes 2000000 | tf_op jit(solution)/shard_map/regularizer/pallas_call | solution.py:286
  48.8 4.4 %all-to-all-done.1.arrived_ref = bf16[16,2,24,192]{3,2,1,0:T(8,128)(2,1)S(1)} async-done(((bf16[16,2,24,192]{3,2,1,0:T(8,128)(2,1)}), bf16[16,2,24,192]{3,2,1,0:T(8,128)(2,1)S(1)}, u32[]{:S(2)}, u32[]{:S(2)}) %all-to-all-start.1) | async-done | bytes 294944 | tf_op jit(solution)/shard_map/all_to_all | solution.py:383
  53.1 0.0 copy-done.1
  53.1 0.8 %update.1 = f32[24,1,2,2,192]{4,3,2,1,0:T(2,128)} custom-call(f32[1]{0:T(128)S(6)} %copy.19.weight_ref, f32[24,1,2,2,192]{4,3,2,1,0:T(2,128)S(1)} %copy-done.1, bf16[16,2,24,192]{3,2,1,0:T(8,128)(2,1)S(1)} %all-to-all-done.1.arrived_ref, f32[2,96,128]{2,1,0:T(8,128)S(1)} %regularizer.1.penalty_ref), custom_call_target="tpu_custom_call" | custom-call | tf_op jit(solution)/shard_map/update/pallas_call | solution.py:319
  (7 shorter events, 0.2 us)
Async XLA Ops:
  0.0 0.9 %copy-start = (f32[24,1,2,2,192]{4,3,2,1,0:T(2,128)S(1)}, f32[24,1,2,2,192]{4,3,2,1,0:T(2,128)}, u32[]{:S(2)}) copy-start(f32[24,1,2,2,192]{4,3,2,1,0:T(2,128)} %image_ref.3) | copy-start | bytes 221188
  0.9 15.8 %copy-start.5 = (bf16[384,1,2,2,192]{0,4,3,2,1:T(8,128)(2,1)S(1)}, bf16[384,1,2,2,192]{0,4,3,2,1:T(8,128)(2,1)}, u32[]{:S(2)}) copy-start(bf16[384,1,2,2,192]{0,4,3,2,1:T(8,128)(2,1)} %param.13) | copy-start | bytes 1769476
  1.8 14.9 %collective-permute-start = (bf16[8,192]{1,0:T(8,128)(2,1)S(1)}, bf16[8,192]{1,0:T(8,128)(2,1)S(1)}, u32[]{:S(2)}, u32[]{:S(2)}) collective-permute-start(bf16[8,192]{1,0:T(8,128)(2,1)S(1)} %get-tuple-element.19), channel_id=1, source_target_pairs={{2,4},{6,8},{10,12},{14,16},{18,20},{22,24},{26,28},{4,2},{8,6},{1... | collective-permute-start | bytes 9224 | tf_op jit(solution)/shard_map/ppermute | solution.py:354
  6.7 9.9 %collective-permute-start.1 = (bf16[8,192]{1,0:T(8,128)(2,1)S(1)}, bf16[8,192]{1,0:T(8,128)(2,1)S(1)}, u32[]{:S(2)}, u32[]{:S(2)}) collective-permute-start(bf16[8,192]{1,0:T(8,128)(2,1)S(1)} %get-tuple-element.20), channel_id=1, source_target_pairs={{0,2},{2,0},{4,6},{6,4},{8,10},{10,8},{12,14},{14,12},{16,18},{18,... | collective-permute-start | bytes 9224 | tf_op jit(solution)/shard_map/ppermute | solution.py:353
  6.8 9.8 %copy-start.8 = (bf16[48,3,3,3,2]{0,4,3,2,1:T(2,128)(2,1)S(1)}, bf16[48,3,3,3,2]{0,4,3,2,1:T(2,128)(2,1)}, u32[]{:S(2)}) copy-start(bf16[48,3,3,3,2]{0,4,3,2,1:T(2,128)(2,1)} %param.15) | copy-start | bytes 15556
  6.8 22.3 %all-to-all-start = ((bf16[16,2,24,192]{3,2,1,0:T(8,128)(2,1)}), bf16[16,2,24,192]{3,2,1,0:T(8,128)(2,1)S(1)}, u32[]{:S(2)}, u32[]{:S(2)}) async-start(bf16[16,2,24,192]{3,2,1,0:T(8,128)(2,1)} %get-tuple-element.17), calls=%async_computation | async-start | bytes 786432 | tf_op jit(solution)/shard_map/all_to_all | solution.py:337
  16.6 1.1 %copy-start.4 = (bf16[384,1,1,2,2,192]{0,5,4,3,2,1:T(8,128)(2,1)S(1)}, bf16[384,1,1,2,2,192]{0,5,4,3,2,1:T(8,128)(2,1)}, u32[]{:S(2)}) copy-start(bf16[384,1,1,2,2,192]{0,5,4,3,2,1:T(8,128)(2,1)} %param.11) | copy-start | bytes 1769476
  16.7 1.4 %copy-start.7 = (bf16[2,6,54,48]{2,3,1,0:T(8,128)(2,1)S(1)}, bf16[2,6,54,48]{2,3,1,0:T(8,128)(2,1)}, u32[]{:S(2)}) copy-start(bf16[2,6,54,48]{2,3,1,0:T(8,128)(2,1)} %constant.43.clone) | copy-start | bytes 186628
  16.8 12.5 %collective-permute-start.3 = (bf16[2,192,384]{2,1,0:T(8,128)(2,1)S(1)}, bf16[2,192,384]{2,1,0:T(8,128)(2,1)S(1)}, u32[]{:S(2)}, u32[]{:S(2)}) collective-permute-start(bf16[2,192,384]{2,1,0:T(8,128)(2,1)S(1)} %dynamic-slice_bitcast_fusion), channel_id=1, source_target_pairs={{0,2},{2,0},{4,6},{6,4},{8,10},{10,8},{12,14},{14,12},{16,18},{18,... | collective-permute-start | bytes 884744 | tf_op jit(solution)/shard_map/ppermute | solution.py:366
  17.6 4.8 %copy-start.6 = (bf16[2,3,54,256]{3,2,1,0:T(8,128)(2,1)S(1)}, bf16[2,3,54,256]{3,2,1,0:T(8,128)(2,1)}, u32[]{:S(2)}) copy-start(bf16[2,3,54,256]{3,2,1,0:T(8,128)(2,1)} %constant.42.clone) | copy-start | bytes 497668
  17.7 11.6 %collective-permute-start.2 = (bf16[2,192,384]{2,1,0:T(8,128)(2,1)S(1)}, bf16[2,192,384]{2,1,0:T(8,128)(2,1)S(1)}, u32[]{:S(2)}, u32[]{:S(2)}) collective-permute-start(bf16[2,192,384]{2,1,0:T(8,128)(2,1)S(1)} %dynamic-slice_bitcast_fusion.1), channel_id=1, source_target_pairs={{0,2},{2,0},{4,6},{6,4},{8,10},{10,8},{12,14},{14,12},{16,18},{18,... | collective-permute-start | bytes 884744 | tf_op jit(solution)/shard_map/ppermute | solution.py:363
  18.3 4.9 %collective-permute-start.6 = (bf16[112,192]{1,0:T(8,128)(2,1)S(1)}, bf16[112,192]{1,0:T(8,128)(2,1)S(1)}, u32[]{:S(2)}, u32[]{:S(2)}) collective-permute-start(bf16[112,192]{1,0:T(8,128)(2,1)S(1)} %pad_maximum_fusion.1), channel_id=1, source_target_pairs={{0,33},{1,32},{32,1},{33,0},{64,97},{65,96},{96,65},{97,64},{128,1... | collective-permute-start | bytes 129032 | tf_op jit(solution)/shard_map/ppermute | solution.py:372
  21.2 3.2 %collective-permute-start.5 = (bf16[112,192]{1,0:T(8,128)(2,1)S(1)}, bf16[112,192]{1,0:T(8,128)(2,1)S(1)}, u32[]{:S(2)}, u32[]{:S(2)}) collective-permute-start(bf16[112,192]{1,0:T(8,128)(2,1)S(1)} %pad_maximum_fusion.1), channel_id=1, source_target_pairs={{0,32},{1,33},{32,0},{33,1},{64,96},{65,97},{96,64},{97,65},{128,1... | collective-permute-start | bytes 129032 | tf_op jit(solution)/shard_map/ppermute | solution.py:372
  21.2 4.6 %collective-permute-start.4 = (bf16[112,192]{1,0:T(8,128)(2,1)S(1)}, bf16[112,192]{1,0:T(8,128)(2,1)S(1)}, u32[]{:S(2)}, u32[]{:S(2)}) collective-permute-start(bf16[112,192]{1,0:T(8,128)(2,1)S(1)} %pad_maximum_fusion.1), channel_id=1, source_target_pairs={{0,1},{1,0},{32,33},{33,32},{64,65},{65,64},{96,97},{97,96},{128,1... | collective-permute-start | bytes 129032 | tf_op jit(solution)/shard_map/ppermute | solution.py:372
  23.1 6.1 %copy-start.2 = (s32[384,1,192]{0,2,1:T(8,128)S(1)}, s32[384,1,192]{0,2,1:T(8,128)}, u32[]{:S(2)}) copy-start(s32[384,1,192]{0,2,1:T(8,128)} %param.12) | copy-start | bytes 884740
  25.7 3.5 %copy-start.3 = (bf16[192,384]{1,0:T(8,128)(2,1)S(1)}, bf16[192,384]{1,0:T(8,128)(2,1)}, u32[]{:S(2)}) copy-start(bf16[192,384]{1,0:T(8,128)(2,1)} %constant.41.clone.col_hbm) | copy-start | bytes 442372
  25.8 3.4 %copy-start.9 = (f32[48]{0:T(128)S(1)}, f32[48]{0:T(128)}, u32[]{:S(2)}) copy-start(f32[48]{0:T(128)} %param.16) | copy-start | bytes 580
  25.8 16.8 %collective-permute-start.9 = (bf16[2,2,112,192]{3,2,1,0:T(8,128)(2,1)S(1)}, bf16[2,2,112,192]{3,2,1,0:T(8,128)(2,1)S(1)}, u32[]{:S(2)}, u32[]{:S(2)}) collective-permute-start(bf16[2,2,112,192]{3,2,1,0:T(8,128)(2,1)S(1)} %bitcast.30), channel_id=1, source_target_pairs={{0,192},{1,193},{32,224},{33,225},{64,128},{65,129},{96,160},{97,1... | collective-permute-start | bytes 516104 | tf_op jit(solution)/shard_map/ppermute | solution.py:372
  28.4 14.2 %collective-permute-start.8 = (bf16[2,2,112,192]{3,2,1,0:T(8,128)(2,1)S(1)}, bf16[2,2,112,192]{3,2,1,0:T(8,128)(2,1)S(1)}, u32[]{:S(2)}, u32[]{:S(2)}) collective-permute-start(bf16[2,2,112,192]{3,2,1,0:T(8,128)(2,1)S(1)} %bitcast.31), channel_id=1, source_target_pairs={{0,128},{1,129},{32,160},{33,161},{64,192},{65,193},{96,224},{97,2... | collective-permute-start | bytes 516104 | tf_op jit(solution)/shard_map/ppermute | solution.py:372
  28.9 13.7 %collective-permute-start.7 = (bf16[2,2,112,192]{3,2,1,0:T(8,128)(2,1)S(1)}, bf16[2,2,112,192]{3,2,1,0:T(8,128)(2,1)S(1)}, u32[]{:S(2)}, u32[]{:S(2)}) collective-permute-start(bf16[2,2,112,192]{3,2,1,0:T(8,128)(2,1)S(1)} %bitcast.32), channel_id=1, source_target_pairs={{0,64},{1,65},{32,96},{33,97},{64,0},{65,1},{96,32},{97,33},{128,1... | collective-permute-start | bytes 516104 | tf_op jit(solution)/shard_map/ppermute | solution.py:372
  33.6 19.6 %all-to-all-start.1 = ((bf16[16,2,24,192]{3,2,1,0:T(8,128)(2,1)}), bf16[16,2,24,192]{3,2,1,0:T(8,128)(2,1)S(1)}, u32[]{:S(2)}, u32[]{:S(2)}) async-start(bf16[16,2,24,192]{3,2,1,0:T(8,128)(2,1)} %consistency.1), calls=%async_computation.1 | async-start | bytes 786432 | tf_op jit(solution)/shard_map/all_to_all | solution.py:383
  42.6 10.6 %copy-start.1 = (f32[24,1,2,2,192]{4,3,2,1,0:T(2,128)S(1)}, f32[24,1,2,2,192]{4,3,2,1,0:T(2,128)}, u32[]{:S(2)}) copy-start(f32[24,1,2,2,192]{4,3,2,1,0:T(2,128)} %image_ref.3) | copy-start | bytes 221188

commit v7 on v6

--- a/solution.py
+++ b/solution.py
@@ -175,7 +175,7 @@
             else:
                 term = map_real * o[2 * c + 1] - map_imag * o[2 * c]
             total = term if total is None else total + term
-        total = total.T.astype(bf16)
+        total = total.astype(bf16).T
         for c in range(COILS):
             out_ref[part, COILS - 1 - c] = total[c * ROWS : (c + 1) * ROWS]
         outs.append(

time: 54.3 us -> 54.3 us (level)
  no operation moved by 1% of the time
where the time goes in v7:
time: 54.3 us; the launch traced here: 53.9 us
  starting transfers between devices  32.2 us (59%)
  Pallas kernels  12 us (22%)
  waiting for transfers between devices  6.84 us (13%)
  local copies, waits for them, and re-layouts  1.72 us (3%)
  between operations  0.87 us (2%)
    all_to_all x1, starting transfers between devices, body(): lax.all_to_all(sent, 'coil', 0, 0, tiled=True, axis_index_groups=[BACKWARD])  9.75 us
    all_to_all x1, starting transfers between devices, body(): lax.all_to_all(partial, 'coil', 0, 0, tiled=True, axis_index_groups=[BACK...  9 us
    ppermute x6, starting transfers between devices, swap(): return lax.ppermute(block, ('echo', 'read'), pairs)  7.44 us
    pallas_call x1, Pallas kernels, regularizer(): pl.pallas_call(regularizer_kernel, out_shape=jax.ShapeDtypeStruct((2, ROW...  6.16 us
    ppermute x1, starting transfers between devices, body(): far = lax.ppermute(far, 'coil', next_chip)  4.92 us
    all_to_all x1, waiting for transfers between devices, body(): lax.all_to_all(partial, 'coil', 0, 0, tiled=True, axis_index_groups=[BACK...  4.37 us
    pallas_call x1, Pallas kernels, consistency(): pl.pallas_call(consistency_kernel, out_shape=jax.ShapeDtypeStruct((COILS,...  4.2 us
    ppermute x6, waiting for transfers between devices, swap(): return lax.ppermute(block, ('echo', 'read'), pairs)  2.46 us
  transfers between devices with their start and end apart: 12, of which 3 were waited for; matrix products, arithmetic and copies ran while one was open for 1% of the time, Pallas kernels for 19%

profile of v7, /device:TPU:1, one launch (start us, length us, event | category | flops | bytes accessed | tf_op | source)
XLA Modules:
  0.0 53.9 jit_solution(13495327950783606070)
XLA Ops:
  0.0 0.0 copy-start
  0.0 0.9 %copy-done = f32[24,1,2,2,192]{4,3,2,1,0:T(2,128)S(1)} copy-done((f32[24,1,2,2,192]{4,3,2,1,0:T(2,128)S(1)}, f32[24,1,2,2,192]{4,3,2,1,0:T(2,128)}, u32[]{:S(2)}) %copy-start) | copy-done | bytes 73752
  0.9 0.0 copy-start.5
  0.9 0.9 %prepare.1 = (bf16[16,2,24,192]{3,2,1,0:T(8,128)(2,1)}, bf16[96,192]{1,0:T(8,128)(2,1)S(1)}, bf16[8,192]{1,0:T(8,128)(2,1)S(1)}, bf16[8,192]{1,0:T(8,128)(2,1)S(1)}) custom-call(f32[24,1,2,2,192]{4,3,2,1,0:T(2,128)S(1)} %copy-done), custom_call_target="tpu_custom_call" | custom-call | tf_op jit(solution)/shard_map/prepare/pallas_call | solution.py:88
  1.8 4.9 %collective-permute-start = (bf16[8,192]{1,0:T(8,128)(2,1)S(1)}, bf16[8,192]{1,0:T(8,128)(2,1)S(1)}, u32[]{:S(2)}, u32[]{:S(2)}) collective-permute-start(bf16[8,192]{1,0:T(8,128)(2,1)S(1)} %get-tuple-element.19), channel_id=1, source_target_pairs={{2,4},{6,8},{10,12},{14,16},{18,20},{22,24},{26,28},{4,2},{8,6},{1... | collective-permute-start | bytes 9224 | tf_op jit(solution)/shard_map/ppermute | solution.py:354
  6.7 0.1 collective-permute-start.1
  6.8 0.0 copy-start.8
  6.8 9.7 %all-to-all-start = ((bf16[16,2,24,192]{3,2,1,0:T(8,128)(2,1)}), bf16[16,2,24,192]{3,2,1,0:T(8,128)(2,1)S(1)}, u32[]{:S(2)}, u32[]{:S(2)}) async-start(bf16[16,2,24,192]{3,2,1,0:T(8,128)(2,1)} %get-tuple-element.17), calls=%async_computation | async-start | bytes 786432 | tf_op jit(solution)/shard_map/all_to_all | solution.py:337
  16.6 0.0 copy-start.4
  16.6 0.0 copy-done.8
  16.6 0.0 collective-permute-done
  16.6 0.0 collective-permute-done.1
  16.7 0.0 copy-done.5
  16.7 0.0 copy-start.7
  16.8 0.5 collective-permute-start.3
  17.3 0.4 copy-done.4
  17.6 0.0 copy-start.6
  17.7 0.5 collective-permute-start.2
  18.2 0.0 copy-done.7
  18.2 0.1 fusion
  18.3 2.8 %collective-permute-start.6 = (bf16[112,192]{1,0:T(8,128)(2,1)S(1)}, bf16[112,192]{1,0:T(8,128)(2,1)S(1)}, u32[]{:S(2)}, u32[]{:S(2)}) collective-permute-start(bf16[112,192]{1,0:T(8,128)(2,1)S(1)} %pad_maximum_fusion.1), channel_id=1, source_target_pairs={{0,33},{1,32},{32,1},{33,0},{64,97},{65,96},{96,65},{97,64},{128,1... | collective-permute-start | bytes 129032 | tf_op jit(solution)/shard_map/ppermute | solution.py:372
  21.2 0.0 collective-permute-start.5
  21.2 1.3 %collective-permute-start.4 = (bf16[112,192]{1,0:T(8,128)(2,1)S(1)}, bf16[112,192]{1,0:T(8,128)(2,1)S(1)}, u32[]{:S(2)}, u32[]{:S(2)}) collective-permute-start(bf16[112,192]{1,0:T(8,128)(2,1)S(1)} %pad_maximum_fusion.1), channel_id=1, source_target_pairs={{0,1},{1,0},{32,33},{33,32},{64,65},{65,64},{96,97},{97,96},{128,1... | collective-permute-start | bytes 129032 | tf_op jit(solution)/shard_map/ppermute | solution.py:372
  22.4 0.0 copy-done.6
  23.1 0.0 copy-start.2
  23.2 0.1 reshape.11.spread_ref
  23.3 0.0 collective-permute-done.6
  23.3 1.1 %collective-permute-done.5 = bf16[112,192]{1,0:T(8,128)(2,1)S(1)} collective-permute-done((bf16[112,192]{1,0:T(8,128)(2,1)S(1)}, bf16[112,192]{1,0:T(8,128)(2,1)S(1)}, u32[]{:S(2)}, u32[]{:S(2)}) %collective-permute-start.5) | collective-permute-done | bytes 43040 | tf_op jit(solution)/shard_map/ppermute | solution.py:372
  24.4 1.4 %collective-permute-done.4 = bf16[112,192]{1,0:T(8,128)(2,1)S(1)} collective-permute-done((bf16[112,192]{1,0:T(8,128)(2,1)S(1)}, bf16[112,192]{1,0:T(8,128)(2,1)S(1)}, u32[]{:S(2)}, u32[]{:S(2)}) %collective-permute-start.4) | collective-permute-done | bytes 43040 | tf_op jit(solution)/shard_map/ppermute | solution.py:372
  25.7 0.0 copy-start.3
  25.7 0.1 pad_maximum_fusion
  25.8 0.0 copy-start.9
  25.8 2.6 %collective-permute-start.9 = (bf16[2,2,112,192]{3,2,1,0:T(8,128)(2,1)S(1)}, bf16[2,2,112,192]{3,2,1,0:T(8,128)(2,1)S(1)}, u32[]{:S(2)}, u32[]{:S(2)}) collective-permute-start(bf16[2,2,112,192]{3,2,1,0:T(8,128)(2,1)S(1)} %bitcast.30), channel_id=1, source_target_pairs={{0,192},{1,193},{32,224},{33,225},{64,128},{65,129},{96,160},{97,1... | collective-permute-start | bytes 516104 | tf_op jit(solution)/shard_map/ppermute | solution.py:372
  28.4 0.5 collective-permute-start.8
  28.9 0.3 collective-permute-start.7
  29.1 0.0 all-to-all-done.x_ref
  29.2 0.0 copy-done.9
  29.2 0.1 broadcast_in_dim.2.thresholds_ref
  29.2 0.0 collective-permute-done.3.other_m_hbm
  29.2 0.0 collective-permute-done.2.other_k_hbm
  29.2 0.0 copy-done.2
  29.2 0.0 copy-done.3
  29.3 4.2 %consistency.1 = bf16[16,2,24,192]{3,2,1,0:T(8,128)(2,1)} custom-call(bf16[16,2,24,192]{3,2,1,0:T(8,128)(2,1)S(1)} %all-to-all-done.x_ref, bf16[2,2,192,384]{3,2,1,0:T(8,128)(2,1)} %bitcast.36, bf16[2,2,192,384]{3,2,1,0:T(8,128)(2,1)} %bitcast.38, bf16[2,192,384]{2,1,0:T(8,128)(2,1)S(1)} %collective-permute-done.2.other_k_hbm, ...), custom_call_target="tpu_custom_call" | custom-call | flops 4000000000 | bytes 3000000 | tf_op jit(solution)/shard_map/consistency/pallas_call | solution.py:191
  33.5 0.1 copy.16.taps_ref
  33.6 9.0 %all-to-all-start.1 = ((bf16[16,2,24,192]{3,2,1,0:T(8,128)(2,1)}), bf16[16,2,24,192]{3,2,1,0:T(8,128)(2,1)S(1)}, u32[]{:S(2)}, u32[]{:S(2)}) async-start(bf16[16,2,24,192]{3,2,1,0:T(8,128)(2,1)} %consistency.1), calls=%async_computation.1 | async-start | bytes 786432 | tf_op jit(solution)/shard_map/all_to_all | solution.py:383
  42.6 0.0 copy-start.1
  42.6 0.0 collective-permute-done.9.x3_ref
  42.6 0.0 collective-permute-done.8.x2_ref
  42.6 0.0 collective-permute-done.7.x1_ref
  42.6 6.2 %regularizer.1.penalty_ref = f32[2,96,128]{2,1,0:T(8,128)S(1)} custom-call(bf16[2,2,112,192]{3,2,1,0:T(8,128)(2,1)S(1)} %bitcast.33, bf16[2,2,112,192]{3,2,1,0:T(8,128)(2,1)S(1)} %collective-permute-done.7.x1_ref, bf16[2,2,112,192]{3,2,1,0:T(8,128)(2,1)S(1)} %collective-permute-done.8.x2_ref, bf16[2,2,112,192]{3,2,1,0:T(8,128)(2,1)S(1)} %collective-permute-done.9.x3_ref, ...), custom_call_target="tpu_custom_call" | custom-call | flops 8999999488 | bytes 2000000 | tf_op jit(solution)/shard_map/regularizer/pallas_call | solution.py:286
  48.8 4.4 %all-to-all-done.1.arrived_ref = bf16[16,2,24,192]{3,2,1,0:T(8,128)(2,1)S(1)} async-done(((bf16[16,2,24,192]{3,2,1,0:T(8,128)(2,1)}), bf16[16,2,24,192]{3,2,1,0:T(8,128)(2,1)S(1)}, u32[]{:S(2)}, u32[]{:S(2)}) %all-to-all-start.1) | async-done | bytes 294944 | tf_op jit(solution)/shard_map/all_to_all | solution.py:383
  53.1 0.0 copy-done.1
  53.1 0.8 %update.1 = f32[24,1,2,2,192]{4,3,2,1,0:T(2,128)} custom-call(f32[1]{0:T(128)S(6)} %copy.19.weight_ref, f32[24,1,2,2,192]{4,3,2,1,0:T(2,128)S(1)} %copy-done.1, bf16[16,2,24,192]{3,2,1,0:T(8,128)(2,1)S(1)} %all-to-all-done.1.arrived_ref, f32[2,96,128]{2,1,0:T(8,128)S(1)} %regularizer.1.penalty_ref), custom_call_target="tpu_custom_call" | custom-call | tf_op jit(solution)/shard_map/update/pallas_call | solution.py:319
  (7 shorter events, 0.2 us)
Async XLA Ops:
  0.0 0.9 %copy-start = (f32[24,1,2,2,192]{4,3,2,1,0:T(2,128)S(1)}, f32[24,1,2,2,192]{4,3,2,1,0:T(2,128)}, u32[]{:S(2)}) copy-start(f32[24,1,2,2,192]{4,3,2,1,0:T(2,128)} %image_ref.3) | copy-start | bytes 221188
  0.9 15.8 %copy-start.5 = (bf16[384,1,2,2,192]{0,4,3,2,1:T(8,128)(2,1)S(1)}, bf16[384,1,2,2,192]{0,4,3,2,1:T(8,128)(2,1)}, u32[]{:S(2)}) copy-start(bf16[384,1,2,2,192]{0,4,3,2,1:T(8,128)(2,1)} %param.13) | copy-start | bytes 1769476
  1.8 14.9 %collective-permute-start = (bf16[8,192]{1,0:T(8,128)(2,1)S(1)}, bf16[8,192]{1,0:T(8,128)(2,1)S(1)}, u32[]{:S(2)}, u32[]{:S(2)}) collective-permute-start(bf16[8,192]{1,0:T(8,128)(2,1)S(1)} %get-tuple-element.19), channel_id=1, source_target_pairs={{2,4},{6,8},{10,12},{14,16},{18,20},{22,24},{26,28},{4,2},{8,6},{1... | collective-permute-start | bytes 9224 | tf_op jit(solution)/shard_map/ppermute | solution.py:354
  6.7 9.9 %collective-permute-start.1 = (bf16[8,192]{1,0:T(8,128)(2,1)S(1)}, bf16[8,192]{1,0:T(8,128)(2,1)S(1)}, u32[]{:S(2)}, u32[]{:S(2)}) collective-permute-start(bf16[8,192]{1,0:T(8,128)(2,1)S(1)} %get-tuple-element.20), channel_id=1, source_target_pairs={{0,2},{2,0},{4,6},{6,4},{8,10},{10,8},{12,14},{14,12},{16,18},{18,... | collective-permute-start | bytes 9224 | tf_op jit(solution)/shard_map/ppermute | solution.py:353
  6.8 9.8 %copy-start.8 = (bf16[48,3,3,3,2]{0,4,3,2,1:T(2,128)(2,1)S(1)}, bf16[48,3,3,3,2]{0,4,3,2,1:T(2,128)(2,1)}, u32[]{:S(2)}) copy-start(bf16[48,3,3,3,2]{0,4,3,2,1:T(2,128)(2,1)} %param.15) | copy-start | bytes 15556
  6.8 22.3 %all-to-all-start = ((bf16[16,2,24,192]{3,2,1,0:T(8,128)(2,1)}), bf16[16,2,24,192]{3,2,1,0:T(8,128)(2,1)S(1)}, u32[]{:S(2)}, u32[]{:S(2)}) async-start(bf16[16,2,24,192]{3,2,1,0:T(8,128)(2,1)} %get-tuple-element.17), calls=%async_computation | async-start | bytes 786432 | tf_op jit(solution)/shard_map/all_to_all | solution.py:337
  16.6 1.1 %copy-start.4 = (bf16[384,1,1,2,2,192]{0,5,4,3,2,1:T(8,128)(2,1)S(1)}, bf16[384,1,1,2,2,192]{0,5,4,3,2,1:T(8,128)(2,1)}, u32[]{:S(2)}) copy-start(bf16[384,1,1,2,2,192]{0,5,4,3,2,1:T(8,128)(2,1)} %param.11) | copy-start | bytes 1769476
  16.7 1.4 %copy-start.7 = (bf16[2,6,54,48]{2,3,1,0:T(8,128)(2,1)S(1)}, bf16[2,6,54,48]{2,3,1,0:T(8,128)(2,1)}, u32[]{:S(2)}) copy-start(bf16[2,6,54,48]{2,3,1,0:T(8,128)(2,1)} %constant.43.clone) | copy-start | bytes 186628
  16.8 12.5 %collective-permute-start.3 = (bf16[2,192,384]{2,1,0:T(8,128)(2,1)S(1)}, bf16[2,192,384]{2,1,0:T(8,128)(2,1)S(1)}, u32[]{:S(2)}, u32[]{:S(2)}) collective-permute-start(bf16[2,192,384]{2,1,0:T(8,128)(2,1)S(1)} %dynamic-slice_bitcast_fusion), channel_id=1, source_target_pairs={{0,2},{2,0},{4,6},{6,4},{8,10},{10,8},{12,14},{14,12},{16,18},{18,... | collective-permute-start | bytes 884744 | tf_op jit(solution)/shard_map/ppermute | solution.py:366
  17.6 4.8 %copy-start.6 = (bf16[2,3,54,256]{3,2,1,0:T(8,128)(2,1)S(1)}, bf16[2,3,54,256]{3,2,1,0:T(8,128)(2,1)}, u32[]{:S(2)}) copy-start(bf16[2,3,54,256]{3,2,1,0:T(8,128)(2,1)} %constant.42.clone) | copy-start | bytes 497668
  17.7 11.6 %collective-permute-start.2 = (bf16[2,192,384]{2,1,0:T(8,128)(2,1)S(1)}, bf16[2,192,384]{2,1,0:T(8,128)(2,1)S(1)}, u32[]{:S(2)}, u32[]{:S(2)}) collective-permute-start(bf16[2,192,384]{2,1,0:T(8,128)(2,1)S(1)} %dynamic-slice_bitcast_fusion.1), channel_id=1, source_target_pairs={{0,2},{2,0},{4,6},{6,4},{8,10},{10,8},{12,14},{14,12},{16,18},{18,... | collective-permute-start | bytes 884744 | tf_op jit(solution)/shard_map/ppermute | solution.py:363
  18.3 4.9 %collective-permute-start.6 = (bf16[112,192]{1,0:T(8,128)(2,1)S(1)}, bf16[112,192]{1,0:T(8,128)(2,1)S(1)}, u32[]{:S(2)}, u32[]{:S(2)}) collective-permute-start(bf16[112,192]{1,0:T(8,128)(2,1)S(1)} %pad_maximum_fusion.1), channel_id=1, source_target_pairs={{0,33},{1,32},{32,1},{33,0},{64,97},{65,96},{96,65},{97,64},{128,1... | collective-permute-start | bytes 129032 | tf_op jit(solution)/shard_map/ppermute | solution.py:372
  21.2 3.2 %collective-permute-start.5 = (bf16[112,192]{1,0:T(8,128)(2,1)S(1)}, bf16[112,192]{1,0:T(8,128)(2,1)S(1)}, u32[]{:S(2)}, u32[]{:S(2)}) collective-permute-start(bf16[112,192]{1,0:T(8,128)(2,1)S(1)} %pad_maximum_fusion.1), channel_id=1, source_target_pairs={{0,32},{1,33},{32,0},{33,1},{64,96},{65,97},{96,64},{97,65},{128,1... | collective-permute-start | bytes 129032 | tf_op jit(solution)/shard_map/ppermute | solution.py:372
  21.2 4.6 %collective-permute-start.4 = (bf16[112,192]{1,0:T(8,128)(2,1)S(1)}, bf16[112,192]{1,0:T(8,128)(2,1)S(1)}, u32[]{:S(2)}, u32[]{:S(2)}) collective-permute-start(bf16[112,192]{1,0:T(8,128)(2,1)S(1)} %pad_maximum_fusion.1), channel_id=1, source_target_pairs={{0,1},{1,0},{32,33},{33,32},{64,65},{65,64},{96,97},{97,96},{128,1... | collective-permute-start | bytes 129032 | tf_op jit(solution)/shard_map/ppermute | solution.py:372
  23.1 6.1 %copy-start.2 = (s32[384,1,192]{0,2,1:T(8,128)S(1)}, s32[384,1,192]{0,2,1:T(8,128)}, u32[]{:S(2)}) copy-start(s32[384,1,192]{0,2,1:T(8,128)} %param.12) | copy-start | bytes 884740
  25.7 3.5 %copy-start.3 = (bf16[192,384]{1,0:T(8,128)(2,1)S(1)}, bf16[192,384]{1,0:T(8,128)(2,1)}, u32[]{:S(2)}) copy-start(bf16[192,384]{1,0:T(8,128)(2,1)} %constant.41.clone.col_hbm) | copy-start | bytes 442372
  25.8 3.4 %copy-start.9 = (f32[48]{0:T(128)S(1)}, f32[48]{0:T(128)}, u32[]{:S(2)}) copy-start(f32[48]{0:T(128)} %param.16) | copy-start | bytes 580
  25.8 16.8 %collective-permute-start.9 = (bf16[2,2,112,192]{3,2,1,0:T(8,128)(2,1)S(1)}, bf16[2,2,112,192]{3,2,1,0:T(8,128)(2,1)S(1)}, u32[]{:S(2)}, u32[]{:S(2)}) collective-permute-start(bf16[2,2,112,192]{3,2,1,0:T(8,128)(2,1)S(1)} %bitcast.30), channel_id=1, source_target_pairs={{0,192},{1,193},{32,224},{33,225},{64,128},{65,129},{96,160},{97,1... | collective-permute-start | bytes 516104 | tf_op jit(solution)/shard_map/ppermute | solution.py:372
  28.4 14.2 %collective-permute-start.8 = (bf16[2,2,112,192]{3,2,1,0:T(8,128)(2,1)S(1)}, bf16[2,2,112,192]{3,2,1,0:T(8,128)(2,1)S(1)}, u32[]{:S(2)}, u32[]{:S(2)}) collective-permute-start(bf16[2,2,112,192]{3,2,1,0:T(8,128)(2,1)S(1)} %bitcast.31), channel_id=1, source_target_pairs={{0,128},{1,129},{32,160},{33,161},{64,192},{65,193},{96,224},{97,2... | collective-permute-start | bytes 516104 | tf_op jit(solution)/shard_map/ppermute | solution.py:372
  28.9 13.7 %collective-permute-start.7 = (bf16[2,2,112,192]{3,2,1,0:T(8,128)(2,1)S(1)}, bf16[2,2,112,192]{3,2,1,0:T(8,128)(2,1)S(1)}, u32[]{:S(2)}, u32[]{:S(2)}) collective-permute-start(bf16[2,2,112,192]{3,2,1,0:T(8,128)(2,1)S(1)} %bitcast.32), channel_id=1, source_target_pairs={{0,64},{1,65},{32,96},{33,97},{64,0},{65,1},{96,32},{97,33},{128,1... | collective-permute-start | bytes 516104 | tf_op jit(solution)/shard_map/ppermute | solution.py:372
  33.6 19.6 %all-to-all-start.1 = ((bf16[16,2,24,192]{3,2,1,0:T(8,128)(2,1)}), bf16[16,2,24,192]{3,2,1,0:T(8,128)(2,1)S(1)}, u32[]{:S(2)}, u32[]{:S(2)}) async-start(bf16[16,2,24,192]{3,2,1,0:T(8,128)(2,1)} %consistency.1), calls=%async_computation.1 | async-start | bytes 786432 | tf_op jit(solution)/shard_map/all_to_all | solution.py:383
  42.6 10.6 %copy-start.1 = (f32[24,1,2,2,192]{4,3,2,1,0:T(2,128)S(1)}, f32[24,1,2,2,192]{4,3,2,1,0:T(2,128)}, u32[]{:S(2)}) copy-start(f32[24,1,2,2,192]{4,3,2,1,0:T(2,128)} %image_ref.3) | copy-start | bytes 221188
